TPU v7x, 32 devices: a whole 2x2x4 slice. The times are simulated.
32 devices in a mesh: wide: 16 (over z, y, core), narrow: 2 (over x).
Axes of the slice: x: 2, y: 2, z: 4, core: 2. Of those that a mesh axis runs over, the one named last changes fastest.
Arguments:
- patches: bfloat16 [32768, 768], P(('wide', 'narrow')), may hold values from -6 to 6
- conditions: bfloat16 [128, 768], P(('wide', 'narrow')), as said below
- modulation_weight: bfloat16 [768, 4608], P('narrow', 'wide'), may hold values from -0.21875 to 0.21875
- attention_weight: bfloat16 [768, 2304], P('narrow', 'wide'), may hold values from -0.21875 to 0.21875
- projection_weight: bfloat16 [768, 768], P('narrow', 'wide'), may hold values from -3.5 to 3.5
- expand_weight: bfloat16 [768, 3072], P('narrow', 'wide'), may hold values from -0.21875 to 0.21875
- contract_weight: bfloat16 [3072, 768], P('narrow', 'wide'), may hold values from -0.109375 to 0.109375
- expert_expand: bfloat16 [16, 768, 3072], P('wide', 'narrow'), may hold values from -0.21875 to 0.21875
- expert_contract: bfloat16 [16, 3072, 768], P('wide', 'narrow'), may hold values from -0.21875 to 0.21875
- image_start: int32 [32768], P('wide'), may hold values from 0 to 127, as said below
- routes: int32 [32768, 2], P(('wide', 'narrow')), may hold values from 0 to 15, all different within a row; in each aligned block of 1024 rows (0 to 1023, 1024 to 2047, ...) at most 256 rows name the same one
- route_gates: float32 [32768, 2], P(('wide', 'narrow')), may hold values from 0.1 to 0.9
- cotangent: bfloat16 [32768, 768], P(('wide', 'narrow')), may hold values from -6 to 6
Outputs:
- block_out: bfloat16 [32768, 768], P(('wide', 'narrow'))
- patch_grad: bfloat16 [32768, 768], P(('wide', 'narrow'))
- modulation_grad: float32 [768, 4608], P('narrow', 'wide')
- attention_grad: float32 [768, 2304], P('narrow', 'wide')
- projection_grad: float32 [768, 768], P('narrow', 'wide')
- expand_grad: float32 [768, 3072], P('narrow', 'wide')
- contract_grad: float32 [3072, 768], P('narrow', 'wide')
- expert_expand_grad: float32 [16, 768, 3072], P('wide', 'narrow')
- expert_contract_grad: float32 [16, 3072, 768], P('wide', 'narrow')
Inputs may be any that keep to these rules, and one draw needn't show every extreme that they name: `image_start`: each aligned group of 2048 patches begins with one image that starts at the group's first patch and ends within the group's last 1024 patches, a whole number of blocks of 256; the group's remaining patches are images of 256 patches; every patch of an image holds the index of the image's first block of 256 patches. `conditions`: all blocks of one image have equal rows. `routes`: each row names two different experts; among the rows of one device at most 256 choices name one expert, and exactly 256 do for some expert in every draw; every expert is named.
All inputs are finite; a program needn't handle non-finite values.
Results may differ from a plain program's by a relative error of at most 0.015.
Values may be sent and summed in bfloat16 or wider, within the bound.
No kernel may reach another device: no remote copies, remote signals or barrier semaphores. Data moves between devices by JAX's collectives and lax.ppermute only.
A program may use at most 384 MiB of HBM per device.

v0:
```python
import jax
import jax.numpy as jnp
from jax import lax
from jax.sharding import PartitionSpec as P

HEADS = 12
IMG_SHORT = 256


EPSILON = 1e-06


def normalize(values):
    centered = values - jnp.mean(values, axis=-1, keepdims=True)
    variance = jnp.mean(centered * centered, axis=-1, keepdims=True)
    return centered * lax.rsqrt(variance + EPSILON)


def norm_back(values, grad_normed):
    centered = values - jnp.mean(values, axis=-1, keepdims=True)
    variance = jnp.mean(centered * centered, axis=-1, keepdims=True)
    inverse = lax.rsqrt(variance + EPSILON)
    normed = centered * inverse
    return inverse * (
        grad_normed
        - jnp.mean(grad_normed, axis=-1, keepdims=True)
        - normed * jnp.mean(grad_normed * normed, axis=-1, keepdims=True)
    )


def gelu_back(hidden, grad):
    return jax.vjp(jax.nn.gelu, hidden)[1](grad)[0]


def product(left, right, form):
    return jnp.einsum(form, left, right, preferred_element_type=jnp.float32)


def on_device(
    patches,
    conditions,
    modulation_weight,
    attention_weight,
    projection_weight,
    expand_weight,
    contract_weight,
    expert_expand,
    expert_contract,
    image_start,
    routes,
    route_gates,
    cotangent,
):
    local_rows = patches.shape[0]
    model_width = patches.shape[1]
    slot_count = conditions.shape[0]
    head_dim = model_width // HEADS
    score_scale = head_dim ** (-0.5)
    expert_count = lax.axis_size("wide")
    narrow_count = lax.axis_size("narrow")
    capacity = 4 * local_rows // expert_count
    narrow_index = lax.axis_index("narrow")
    (
        modulation_part,
        attention_part,
        projection_part,
        expand_part,
        contract_part,
        up_whole,
        down_whole,
    ) = (
        lax.all_gather(modulation_weight, "narrow", axis=0, tiled=True),
        lax.all_gather(attention_weight, "narrow", axis=0, tiled=True),
        lax.all_gather(projection_weight, "narrow", axis=0, tiled=True),
        lax.all_gather(expand_weight, "narrow", axis=0, tiled=True),
        lax.all_gather(contract_weight, "narrow", axis=0, tiled=True),
        lax.all_gather(expert_expand, "narrow", axis=1, tiled=True),
        lax.all_gather(expert_contract, "narrow", axis=1, tiled=True),
    )
    modulation_full, attention_full, projection_full, expand_full, contract_full = (
        lax.all_gather(modulation_part, "wide", axis=1, tiled=True),
        lax.all_gather(attention_part, "wide", axis=1, tiled=True),
        lax.all_gather(projection_part, "wide", axis=1, tiled=True),
        lax.all_gather(expand_part, "wide", axis=1, tiled=True),
        lax.all_gather(contract_part, "wide", axis=1, tiled=True),
    )
    up_matrix = up_whole[0]
    down_matrix = down_whole[0]
    lifted = jax.nn.silu(conditions.astype(jnp.float32)).astype(jnp.bfloat16)
    modulation = jnp.dot(lifted, modulation_full, preferred_element_type=jnp.float32).reshape(
        slot_count, 6, 1, model_width
    )
    shift_a = modulation[:, 0]
    scale_a = modulation[:, 1]
    gate_a = modulation[:, 2]
    shift_b = modulation[:, 3]
    scale_b = modulation[:, 4]
    gate_b = modulation[:, 5]
    inputs = patches.astype(jnp.float32).reshape(slot_count, IMG_SHORT, model_width)
    normed_a = normalize(inputs)
    first_entry = (
        (normed_a * (1.0 + scale_a) + shift_a).astype(jnp.bfloat16).reshape(local_rows, model_width)
    )
    triple = jnp.dot(first_entry, attention_full, preferred_element_type=jnp.float32).astype(
        jnp.bfloat16
    )
    queries = triple[:, :model_width].reshape(local_rows, HEADS, head_dim)
    keys_own = triple[:, model_width : 2 * model_width]
    values_own = triple[:, 2 * model_width :]
    query_start = lax.dynamic_slice_in_dim(image_start, narrow_index * local_rows, local_rows)
    keys_group, values_group = (
        lax.all_gather(keys_own, "narrow", axis=0, tiled=True),
        lax.all_gather(values_own, "narrow", axis=0, tiled=True),
    )
    group_rows = keys_group.shape[0]
    block_rows = min(512, group_rows)
    block_count = group_rows // block_rows
    key_blocks = keys_group.reshape(block_count, block_rows, HEADS, head_dim)
    value_blocks = values_group.reshape(block_count, block_rows, HEADS, head_dim)
    start_blocks = image_start.reshape(block_count, block_rows)

    def block_scores(key_block, start_block):
        scores = product(queries, key_block, "qhd,khd->hqk") * score_scale
        same_image = (query_start[:, None] == start_block[None, :])[None]
        return (jnp.where(same_image, scores, -1e30), same_image)

    def max_step(running, items):
        scores, same_image = block_scores(items[0], items[1])
        running_max = jnp.maximum(running[0], jnp.max(scores, axis=-1))
        running_sum = running[1] * jnp.exp(running[0] - running_max) + jnp.sum(
            jnp.where(same_image, jnp.exp(scores - running_max[..., None]), 0.0), axis=-1
        )
        return ((running_max, running_sum), None)

    start_state = (
        jnp.full((HEADS, local_rows), -1e30, jnp.float32),
        jnp.zeros((HEADS, local_rows), jnp.float32),
    )
    (running_max, running_sum), _ = lax.scan(max_step, start_state, (key_blocks, start_blocks))
    log_total = running_max + jnp.log(running_sum)

    def mix_step(running, items):
        scores, same_image = block_scores(items[0], items[2])
        weights = jnp.where(same_image, jnp.exp(scores - log_total[..., None]), 0.0).astype(
            jnp.bfloat16
        )
        return (running + product(weights, items[1], "hqk,khd->qhd"), None)

    attended_heads, _ = lax.scan(
        mix_step,
        jnp.zeros((local_rows, HEADS, head_dim), jnp.float32),
        (key_blocks, value_blocks, start_blocks),
    )
    mixed_heads = attended_heads.reshape(local_rows, model_width).astype(jnp.bfloat16)
    attended = jnp.dot(mixed_heads, projection_full, preferred_element_type=jnp.float32).reshape(
        slot_count, IMG_SHORT, model_width
    )
    middle = inputs + gate_a * attended
    normed_b = normalize(middle)
    second = (
        (normed_b * (1.0 + scale_b) + shift_b).astype(jnp.bfloat16).reshape(local_rows, model_width)
    )
    hidden = jnp.dot(second, expand_full, preferred_element_type=jnp.float32)
    activated = jax.nn.gelu(hidden).astype(jnp.bfloat16)
    shared = jnp.dot(activated, contract_full, preferred_element_type=jnp.float32)
    flat_routes = routes.reshape(-1)
    one_hot = (flat_routes[:, None] == jnp.arange(expert_count, dtype=jnp.int32)[None, :]).astype(
        jnp.int32
    )
    ranking = jnp.sum((jnp.cumsum(one_hot, axis=0) - one_hot) * one_hot, axis=1)
    placing = flat_routes * capacity + ranking
    owner_rows = jnp.arange(2 * local_rows, dtype=jnp.int32) // 2
    outgoing = (
        jnp.zeros((expert_count * capacity, model_width), jnp.bfloat16)
        .at[placing]
        .set(second[owner_rows])
    )
    arrived = lax.all_to_all(
        outgoing.reshape(expert_count, capacity, model_width),
        "wide",
        split_axis=0,
        concat_axis=0,
        tiled=True,
    ).reshape(expert_count * capacity, model_width)
    expert_hidden = jnp.dot(arrived, up_matrix, preferred_element_type=jnp.float32)
    expert_active = jax.nn.gelu(expert_hidden).astype(jnp.bfloat16)
    produced = jnp.dot(expert_active, down_matrix, preferred_element_type=jnp.float32).astype(
        jnp.bfloat16
    )
    returned = lax.all_to_all(
        produced.reshape(expert_count, capacity, model_width),
        "wide",
        split_axis=0,
        concat_axis=0,
        tiled=True,
    ).reshape(expert_count * capacity, model_width)
    routed = returned[placing].astype(jnp.float32).reshape(local_rows, 2, model_width)
    mixture = shared + jnp.sum(route_gates[:, :, None] * routed, axis=1)
    mixture_blocks = mixture.reshape(slot_count, IMG_SHORT, model_width)
    block_out = (
        (middle + gate_b * mixture_blocks).reshape(local_rows, model_width).astype(jnp.bfloat16)
    )
    grad_top = cotangent.astype(jnp.float32).reshape(slot_count, IMG_SHORT, model_width)
    grad_gate_b = jnp.sum(grad_top * mixture_blocks, axis=1)
    grad_mixture = (gate_b * grad_top).reshape(local_rows, model_width)
    grad_shared = grad_mixture.astype(jnp.bfloat16)
    grad_routed = (
        (route_gates[:, :, None] * grad_mixture[:, None, :])
        .astype(jnp.bfloat16)
        .reshape(2 * local_rows, model_width)
    )
    grad_outgoing = (
        jnp.zeros((expert_count * capacity, model_width), jnp.bfloat16).at[placing].set(grad_routed)
    )
    grad_arrived = lax.all_to_all(
        grad_outgoing.reshape(expert_count, capacity, model_width),
        "wide",
        split_axis=0,
        concat_axis=0,
        tiled=True,
    ).reshape(expert_count * capacity, model_width)
    down_grad_full = product(expert_active, grad_arrived, "rf,rd->fd")
    grad_expert_hidden = gelu_back(
        expert_hidden, product(grad_arrived, down_matrix, "rd,fd->rf")
    ).astype(jnp.bfloat16)
    up_grad_full = product(arrived, grad_expert_hidden, "rd,rf->df")
    grad_sent = product(grad_expert_hidden, up_matrix, "rf,df->rd").astype(jnp.bfloat16)
    grad_returned = lax.all_to_all(
        grad_sent.reshape(expert_count, capacity, model_width),
        "wide",
        split_axis=0,
        concat_axis=0,
        tiled=True,
    ).reshape(expert_count * capacity, model_width)
    grad_second = jnp.sum(
        grad_returned[placing].astype(jnp.float32).reshape(local_rows, 2, model_width), axis=1
    )
    contract_grad_full = product(activated, grad_shared, "tf,td->fd")
    grad_hidden = gelu_back(hidden, product(grad_shared, contract_full, "td,fd->tf")).astype(
        jnp.bfloat16
    )
    expand_grad_full = product(second, grad_hidden, "td,tf->df")
    grad_second = grad_second + product(grad_hidden, expand_full, "tf,df->td")
    grad_second_blocks = grad_second.reshape(slot_count, IMG_SHORT, model_width)
    grad_shift_b = jnp.sum(grad_second_blocks, axis=1)
    grad_scale_b = jnp.sum(grad_second_blocks * normed_b, axis=1)
    grad_middle = grad_top + norm_back(middle, grad_second_blocks * (1.0 + scale_b))
    grad_gate_a = jnp.sum(grad_middle * attended, axis=1)
    grad_attended = (gate_a * grad_middle).reshape(local_rows, model_width).astype(jnp.bfloat16)
    projection_grad_full = product(mixed_heads, grad_attended, "td,te->de")
    grad_mixed = (
        product(grad_attended, projection_full, "te,de->td")
        .astype(jnp.bfloat16)
        .reshape(local_rows, HEADS, head_dim)
    )
    row_dots = jnp.transpose(jnp.sum(grad_mixed.astype(jnp.float32) * attended_heads, axis=-1))

    def back_step(grad_queries, items):
        key_block, value_block, start_block = items
        scores, same_image = block_scores(key_block, start_block)
        softmax = jnp.where(same_image, jnp.exp(scores - log_total[..., None]), 0.0)
        grad_values = product(softmax.astype(jnp.bfloat16), grad_mixed, "hqk,qhd->khd")
        grad_softmax = product(grad_mixed, value_block, "qhd,khd->hqk")
        grad_scores = (softmax * (grad_softmax - row_dots[..., None])).astype(jnp.bfloat16)
        grad_keys = product(grad_scores, queries, "hqk,qhd->khd") * score_scale
        grad_queries = grad_queries + product(grad_scores, key_block, "hqk,khd->qhd") * score_scale
        return (grad_queries, (grad_keys, grad_values))

    grad_queries, (grad_key_blocks, grad_value_blocks) = lax.scan(
        back_step,
        jnp.zeros((local_rows, HEADS, head_dim), jnp.float32),
        (key_blocks, value_blocks, start_blocks),
    )
    grad_keys_all = grad_key_blocks.reshape(group_rows, model_width)
    grad_values_all = grad_value_blocks.reshape(group_rows, model_width)
    grad_keys_own, grad_values_own = (
        lax.psum_scatter(
            grad_keys_all.astype(jnp.bfloat16), "narrow", scatter_dimension=0, tiled=True
        ).astype(jnp.float32),
        lax.psum_scatter(
            grad_values_all.astype(jnp.bfloat16), "narrow", scatter_dimension=0, tiled=True
        ).astype(jnp.float32),
    )
    grad_triple = jnp.concatenate(
        [grad_queries.reshape(local_rows, model_width), grad_keys_own, grad_values_own], axis=1
    ).astype(jnp.bfloat16)
    attention_grad_full = product(first_entry, grad_triple, "td,te->de")
    grad_entry = product(grad_triple, attention_full, "te,de->td").reshape(
        slot_count, IMG_SHORT, model_width
    )
    grad_shift_a = jnp.sum(grad_entry, axis=1)
    grad_scale_a = jnp.sum(grad_entry * normed_a, axis=1)
    grad_inputs = grad_middle + norm_back(inputs, grad_entry * (1.0 + scale_a))
    grad_modulation = (
        jnp.stack(
            [grad_shift_a, grad_scale_a, grad_gate_a, grad_shift_b, grad_scale_b, grad_gate_b],
            axis=1,
        )
        .reshape(slot_count, 6 * model_width)
        .astype(jnp.bfloat16)
    )
    row_share = model_width // narrow_count
    column_share = 6 * model_width // expert_count
    modulation_grad_full = product(lifted, grad_modulation, "sd,se->de")
    arranged = (
        modulation_grad_full.reshape(narrow_count, row_share, expert_count, column_share)
        .transpose(2, 0, 1, 3)
        .reshape(expert_count * narrow_count * row_share, column_share)
    )
    modulation_grad = lax.psum_scatter(
        arranged, ("wide", "narrow"), scatter_dimension=0, tiled=True
    )
    wide_attention, wide_projection, wide_expand, wide_contract = (
        lax.psum_scatter(
            attention_grad_full.astype(jnp.bfloat16), "wide", scatter_dimension=1, tiled=True
        ).astype(jnp.float32),
        lax.psum_scatter(
            projection_grad_full.astype(jnp.bfloat16), "wide", scatter_dimension=1, tiled=True
        ).astype(jnp.float32),
        lax.psum_scatter(
            expand_grad_full.astype(jnp.bfloat16), "wide", scatter_dimension=1, tiled=True
        ).astype(jnp.float32),
        lax.psum_scatter(
            contract_grad_full.astype(jnp.bfloat16), "wide", scatter_dimension=1, tiled=True
        ).astype(jnp.float32),
    )
    (
        attention_grad,
        projection_grad,
        expand_grad,
        contract_grad,
        expert_up_grad,
        expert_down_grad,
    ) = (
        lax.psum_scatter(
            wide_attention.astype(jnp.bfloat16), "narrow", scatter_dimension=0, tiled=True
        ).astype(jnp.float32),
        lax.psum_scatter(
            wide_projection.astype(jnp.bfloat16), "narrow", scatter_dimension=0, tiled=True
        ).astype(jnp.float32),
        lax.psum_scatter(
            wide_expand.astype(jnp.bfloat16), "narrow", scatter_dimension=0, tiled=True
        ).astype(jnp.float32),
        lax.psum_scatter(
            wide_contract.astype(jnp.bfloat16), "narrow", scatter_dimension=0, tiled=True
        ).astype(jnp.float32),
        lax.psum_scatter(
            up_grad_full[None].astype(jnp.bfloat16), "narrow", scatter_dimension=1, tiled=True
        ).astype(jnp.float32),
        lax.psum_scatter(
            down_grad_full[None].astype(jnp.bfloat16), "narrow", scatter_dimension=1, tiled=True
        ).astype(jnp.float32),
    )
    patch_grad = grad_inputs.reshape(local_rows, model_width).astype(jnp.bfloat16)
    return (
        block_out,
        patch_grad,
        modulation_grad,
        attention_grad,
        projection_grad,
        expand_grad,
        contract_grad,
        expert_up_grad,
        expert_down_grad,
    )


def solution(mesh):
    return jax.shard_map(
        on_device,
        mesh=mesh,
        in_specs=(
            P(("wide", "narrow"), None),
            P(("wide", "narrow"), None),
            P("narrow", "wide"),
            P("narrow", "wide"),
            P("narrow", "wide"),
            P("narrow", "wide"),
            P("narrow", "wide"),
            P("wide", "narrow", None),
            P("wide", "narrow", None),
            P("wide"),
            P(("wide", "narrow"), None),
            P(("wide", "narrow"), None),
            P(("wide", "narrow"), None),
        ),
        out_specs=(
            P(("wide", "narrow"), None),
            P(("wide", "narrow"), None),
            P("narrow", "wide"),
            P("narrow", "wide"),
            P("narrow", "wide"),
            P("narrow", "wide"),
            P("narrow", "wide"),
            P("wide", "narrow", None),
            P("wide", "narrow", None),
        ),
        check_vma=False,
    )
```

profile of v0, /device:TPU:0, one launch (start us, length us, event | category | flops | bytes accessed | tf_op | source)
XLA Modules:
  0.0 2203.8 jit_solution(2078229991312258647)
XLA Ops:
  26.6 58.9 %all-gather.10.cloned.1.call-done = bf16[768,4608]{0,1:T(8,128)(2,1)} async-done(((bf16[768,288]{0,1:T(8,128)(2,1)}), bf16[768,4608]{0,1:T(8,128)(2,1)}) %all-gather.10.cloned.1.call-update) | async-done | bytes 7077904 | tf_op jit(solution)/shard_map/all_gather | solution.py:81
  92.5 41.0 %all-gather.12.cloned.1.call-done = bf16[768,2304]{0,1:T(8,128)(2,1)} async-done(((bf16[768,144]{0,1:T(8,128)(2,1)}), bf16[768,2304]{0,1:T(8,128)(2,1)}) %all-gather.12.cloned.1.call-update) | async-done | bytes 3538960 | tf_op jit(solution)/shard_map/all_gather | solution.py:82
  201.5 31.4 %all-gather.16.cloned.1.call-done = bf16[2048,768]{1,0:T(8,128)(2,1)} async-done(((bf16[1024,768]{1,0:T(8,128)(2,1)}), bf16[2048,768]{1,0:T(8,128)(2,1)}) %all-gather.16.cloned.1.call-update) | async-done | bytes 3145744 | tf_op jit(solution)/shard_map/all_gather | solution.py:112
  248.1 94.1 %while.39 = (s32[]{:T(128)}, f32[12,1024]{1,0:T(8,128)S(1)}, f32[12,1024]{1,0:T(8,128)S(1)}, s32[1024]{0:T(1024)S(1)}, s32[4,512]{1,0:T(4,128)S(1)}, /*index=5*/...) while((s32[]{:T(128)}, f32[12,1024]{1,0:T(8,128)S(1)}, ...), condition=%wide.region_5.6_spmd.clone, body=%wide.region_2.5_spmd.clone.sunk | while | flops 856223744 | bytes 54913140 | solution.py:139
  342.3 48.1 %while.40 = (s32[]{:T(128)}, f32[1024,12,64]{0,2,1:T(8,128)}, bf16[4,512,12,64]{1,3,2,0:T(8,128)(2,1)}, s32[1024]{0:T(1024)S(1)}, s32[4,512]{1,0:T(4,128)S(1)}, ...) while((s32[]{:T(128)}, f32[1024,12,64]{0,2,1:T(8,128)}, ...), condition=%wide.region_7.8_spmd.clone, body=%wide.region_6.7_spmd.clone.sunk | while | flops 1644167168 | bytes 10546810 | solution.py:149
  472.4 81.9 %all-to-all-done = bf16[16,256,768]{2,1,0:T(8,128)(2,1)} async-done(((bf16[16,256,768]{2,1,0:T(8,128)(2,1)}), bf16[16,256,768]{2,1,0:T(8,128)(2,1)}, u32[]{:S(2)}, u32[]{:S(2)}) %all-to-all-start) | async-done | bytes 6291488 | tf_op jit(solution)/shard_map/all_to_all | solution.py:178
  554.3 28.2 %all-to-all-start.2 = ((bf16[16,256,768]{2,1,0:T(8,128)(2,1)}), bf16[16,256,768]{2,1,0:T(8,128)(2,1)}, u32[]{:S(2)}, u32[]{:S(2)}) async-start(bf16[16,256,768]{2,1,0:T(8,128)(2,1)} %bitcast.333), calls=%async_computation.2 | async-start | bytes 12582912 | tf_op jit(solution)/shard_map/all_to_all | solution.py:215
  590.5 43.2 %multiply_convert_fusion = (bf16[4096,3072]{1,0:T(8,128)(2,1)}, f32[4096,3072]{1,0:T(8,128)}) fusion(bf16[4096,768]{1,0:T(8,128)(2,1)} %bitcast.11, bf16[1,768,3072]{2,1,0:T(8,128)(2,1)} %all-gather.24.cloned.1.call-done), kind=kOutput, calls=%fused_computation.72 | convolution fusion | flops 19440599040 | bytes 86507520 | tf_op jit(solution)/shard_map/dot_general | solution.py:185
  647.9 58.3 %all-to-all-done.2 = bf16[16,256,768]{2,1,0:T(8,128)(2,1)} async-done(((bf16[16,256,768]{2,1,0:T(8,128)(2,1)}), bf16[16,256,768]{2,1,0:T(8,128)(2,1)}, u32[]{:S(2)}, u32[]{:S(2)}) %all-to-all-start.2) | async-done | bytes 6291488 | tf_op jit(solution)/shard_map/all_to_all | solution.py:215
  706.2 53.0 %fusion.57 = bf16[4096,3072]{1,0:T(8,128)(2,1)} fusion(f32[4096,3072]{1,0:T(8,128)} %get-tuple-element.440, bf16[4096,768]{1,0:T(8,128)(2,1)} %bitcast.21, bf16[1,3072,768]{2,1,0:T(8,128)(2,1)} %all-gather.26.cloned.1.call-done), kind=kOutput, calls=%fused_computation.71 | convolution fusion | flops 19579011072 | bytes 86507520 | tf_op jit(solution)/shard_map/rd,fd->rf/dot_general | solution.py:36
  784.9 47.2 %all-to-all-start.3 = ((bf16[16,256,768]{2,1,0:T(8,128)(2,1)}), bf16[16,256,768]{2,1,0:T(8,128)(2,1)}, u32[]{:S(2)}, u32[]{:S(2)}) async-start(bf16[16,256,768]{2,1,0:T(8,128)(2,1)} %bitcast.339), calls=%async_computation.3 | async-start | bytes 12582912 | tf_op jit(solution)/shard_map/all_to_all | solution.py:228
  864.6 110.2 %all-to-all-done.3 = bf16[16,256,768]{2,1,0:T(8,128)(2,1)} async-done(((bf16[16,256,768]{2,1,0:T(8,128)(2,1)}), bf16[16,256,768]{2,1,0:T(8,128)(2,1)}, u32[]{:S(2)}, u32[]{:S(2)}) %all-to-all-start.3) | async-done | bytes 6291488 | tf_op jit(solution)/shard_map/all_to_all | solution.py:228
  974.7 28.2 %all-to-all-start.1 = ((bf16[16,256,768]{2,1,0:T(8,128)(2,1)}), bf16[16,256,768]{2,1,0:T(8,128)(2,1)}, u32[]{:S(2)}, u32[]{:S(2)}) async-start(bf16[16,256,768]{2,1,0:T(8,128)(2,1)} %bitcast.338), calls=%async_computation.1 | async-start | bytes 12582912 | tf_op jit(solution)/shard_map/all_to_all | solution.py:190
  1073.5 43.7 %all-to-all-done.1 = bf16[16,256,768]{2,1,0:T(8,128)(2,1)} async-done(((bf16[16,256,768]{2,1,0:T(8,128)(2,1)}), bf16[16,256,768]{2,1,0:T(8,128)(2,1)}, u32[]{:S(2)}, u32[]{:S(2)}) %all-to-all-start.1) | async-done | bytes 6291488 | tf_op jit(solution)/shard_map/all_to_all | solution.py:190
  1139.1 31.3 %multiply_reduce_fusion = f32[1024,768]{1,0:T(8,128)S(1)} fusion(f32[1024,2,768]{2,1,0:T(2,128)} %reshape.441, f32[1024,2]{1,0:T(8,128)} %copy-done.15), kind=kLoop, calls=%fused_computation.86 | loop fusion | flops 2359296 | bytes 9445376 | tf_op jit(solution)/shard_map/reduce_sum | solution.py:198
  1194.7 240.3 %while.41 = (s32[]{:T(128)}, f32[1024,12,64]{0,2,1:T(8,128)}, bf16[4,512,12,64]{1,3,2,0:T(8,128)(2,1)}, bf16[4,512,12,64]{1,3,2,0:T(8,128)(2,1)}, bf16[4,512,12,...) while((s32[]{:T(128)}, f32[1024,12,64]{0,2,1:T(8,128)}, ...), condition=%wide.region_21.22_spmd.clone, body=%wide.region_20.21_spmd.clone.sunk | while | flops 4105306112 | bytes 133064872 | solution.py:269
  1480.5 27.5 %reduce-scatter.22.cloned.1.call-done = bf16[1024,768]{0,1:T(8,128)(2,1)} async-done(((bf16[2048,768]{0,1:T(8,128)(2,1)}), bf16[1024,768]{0,1:T(8,128)(2,1)}) %reduce-scatter.22.cloned.1.call-update) | async-done | bytes 1572880 | tf_op jit(solution)/shard_map/reduce_scatter | solution.py:280
  1508.0 45.7 %reduce-scatter.20.cloned.1.call-done = bf16[1024,768]{0,1:T(8,128)(2,1)} async-done(((bf16[2048,768]{0,1:T(8,128)(2,1)}), bf16[1024,768]{0,1:T(8,128)(2,1)}) %reduce-scatter.20.cloned.1.call-update) | async-done | bytes 1572880 | tf_op jit(solution)/shard_map/reduce_scatter | solution.py:277
  1562.2 71.4 %reduce-scatter.30.cloned.1.call-done = bf16[768,192]{0,1:T(8,128)(2,1)} async-done(((bf16[768,3072]{0,1:T(8,128)(2,1)}), bf16[768,192]{0,1:T(8,128)(2,1)}) %reduce-scatter.30.cloned.1.call-update) | async-done | bytes 294928 | tf_op jit(solution)/shard_map/reduce_scatter | solution.py:320
  1635.6 77.5 %reduce-scatter.32.cloned.1.call-done = bf16[3072,48]{0,1:T(8,128)(2,1)} async-done(((bf16[3072,768]{0,1:T(8,128)(2,1)}), bf16[3072,48]{0,1:T(8,128)(2,1)}) %reduce-scatter.32.cloned.1.call-update) | async-done | bytes 294928 | tf_op jit(solution)/shard_map/reduce_scatter | solution.py:323
  1790.2 54.3 %reduce-scatter.26.cloned.1.call-done = bf16[768,144]{0,1:T(8,128)(2,1)} async-done(((bf16[768,2304]{0,1:T(8,128)(2,1)}), bf16[768,144]{0,1:T(8,128)(2,1)}) %reduce-scatter.26.cloned.1.call-update) | async-done | bytes 221200 | tf_op jit(solution)/shard_map/reduce_scatter | solution.py:314
  1886.1 49.6 %reduce-scatter.36.cloned.1.call-done = bf16[1,384,3072]{2,1,0:T(8,128)(2,1)} async-done(((bf16[1,768,3072]{2,1,0:T(8,128)(2,1)}), bf16[1,384,3072]{2,1,0:T(8,128)(2,1)}) %reduce-scatter.36.cloned.1.call-update) | async-done | bytes 2359312 | tf_op jit(solution)/shard_map/reduce_scatter | solution.py:347
  1940.1 57.9 %reduce-scatter.38.cloned.1.call-done = bf16[1,1536,768]{2,1,0:T(8,128)(2,1)} async-done(((bf16[1,3072,768]{2,1,0:T(8,128)(2,1)}), bf16[1,1536,768]{2,1,0:T(8,128)(2,1)}) %reduce-scatter.38.cloned.1.call-update) | async-done | bytes 2359312 | tf_op jit(solution)/shard_map/reduce_scatter | solution.py:350
  2029.0 167.8 %reduce-scatter.24.cloned.1.call-done = f32[384,288]{0,1:T(8,128)} async-done(((f32[12288,288]{0,1:T(8,128)}), f32[384,288]{0,1:T(8,128)}) %reduce-scatter.24.cloned.1.call-update) | async-done | bytes 442384 | tf_op jit(solution)/shard_map/reduce_scatter | solution.py:310
  (374 shorter events, 979.4 us)
Async XLA Ops:
  18.4 115.1 %all-gather.12.cloned.1.call-start = ((), (), s32[]{:S(2)}) async-start(), calls=%async_computation.18 | async-start | bytes 3760128 | tf_op jit(solution)/shard_map/all_gather | solution.py:82
  24.2 161.8 %all-gather.14.cloned.1.call-start = ((), (), s32[]{:S(2)}) async-start(), calls=%async_computation.19 | async-start | bytes 4718592 | tf_op jit(solution)/shard_map/all_gather | solution.py:113
  141.9 91.0 %all-gather.16.cloned.1.call-start = ((), (), s32[]{:S(2)}) async-start(), calls=%async_computation.20 | async-start | bytes 4718592 | tf_op jit(solution)/shard_map/all_gather | solution.py:112
  142.5 257.6 %all-gather.18.cloned.1.call-start = ((), (), s32[]{:S(2)}) async-start(), calls=%async_computation.21 | async-start | bytes 1253376 | tf_op jit(solution)/shard_map/all_gather | solution.py:83
  434.4 119.9 %all-to-all-start = ((bf16[16,256,768]{2,1,0:T(8,128)(2,1)}), bf16[16,256,768]{2,1,0:T(8,128)(2,1)}, u32[]{:S(2)}, u32[]{:S(2)}) async-start(bf16[16,256,768]{2,1,0:T(8,128)(2,1)} %bitcast.332), calls=%async_computation | async-start | bytes 12582912 | tf_op jit(solution)/shard_map/all_to_all | solution.py:178
  440.1 150.4 %all-gather.24.cloned.1.call-start = ((), (), s32[]{:S(2)}) async-start(), calls=%async_computation.24 | async-start | bytes 7077888 | tf_op jit(solution)/shard_map/all_gather | solution.py:77
  554.3 151.9 %all-to-all-start.2 = ((bf16[16,256,768]{2,1,0:T(8,128)(2,1)}), bf16[16,256,768]{2,1,0:T(8,128)(2,1)}, u32[]{:S(2)}, u32[]{:S(2)}) async-start(bf16[16,256,768]{2,1,0:T(8,128)(2,1)} %bitcast.333), calls=%async_computation.2 | async-start | bytes 12582912 | tf_op jit(solution)/shard_map/all_to_all | solution.py:215
  583.3 419.8 %all-gather.20.cloned.1.call-start = ((), (), s32[]{:S(2)}) async-start(), calls=%async_computation.22 | async-start | bytes 5013504 | tf_op jit(solution)/shard_map/all_gather | solution.py:84
  784.9 189.9 %all-to-all-start.3 = ((bf16[16,256,768]{2,1,0:T(8,128)(2,1)}), bf16[16,256,768]{2,1,0:T(8,128)(2,1)}, u32[]{:S(2)}, u32[]{:S(2)}) async-start(bf16[16,256,768]{2,1,0:T(8,128)(2,1)} %bitcast.339), calls=%async_computation.3 | async-start | bytes 12582912 | tf_op jit(solution)/shard_map/all_to_all | solution.py:228
  832.1 181.3 %all-gather.22.cloned.1.call-start = ((), (), s32[]{:S(2)}) async-start(), calls=%async_computation.23 | async-start | bytes 5013504 | tf_op jit(solution)/shard_map/all_gather | solution.py:85
  974.7 142.5 %all-to-all-start.1 = ((bf16[16,256,768]{2,1,0:T(8,128)(2,1)}), bf16[16,256,768]{2,1,0:T(8,128)(2,1)}, u32[]{:S(2)}, u32[]{:S(2)}) async-start(bf16[16,256,768]{2,1,0:T(8,128)(2,1)} %bitcast.338), calls=%async_computation.1 | async-start | bytes 12582912 | tf_op jit(solution)/shard_map/all_to_all | solution.py:190
  1003.0 505.0 %reduce-scatter.22.cloned.1.call-start = ((), (), s32[]{:S(2)}) async-start(), calls=%async_computation.27 | async-start | bytes 4718592 | tf_op jit(solution)/shard_map/reduce_scatter | solution.py:280
  1442.1 111.7 %reduce-scatter.20.cloned.1.call-start = ((), (), s32[]{:S(2)}) async-start(), calls=%async_computation.26 | async-start | bytes 4718592 | tf_op jit(solution)/shard_map/reduce_scatter | solution.py:277
  1449.0 184.6 %reduce-scatter.30.cloned.1.call-start = ((), (), s32[]{:S(2)}) async-start(), calls=%async_computation.31 | async-start | bytes 5013504 | tf_op jit(solution)/shard_map/reduce_scatter | solution.py:320
  1462.2 250.9 %reduce-scatter.32.cloned.1.call-start = ((), (), s32[]{:S(2)}) async-start(), calls=%async_computation.32 | async-start | bytes 5013504 | tf_op jit(solution)/shard_map/reduce_scatter | solution.py:323
  1474.5 299.2 %reduce-scatter.28.cloned.1.call-start = ((), (), s32[]{:S(2)}) async-start(), calls=%async_computation.30 | async-start | bytes 1253376 | tf_op jit(solution)/shard_map/reduce_scatter | solution.py:317
  1479.1 365.4 %reduce-scatter.26.cloned.1.call-start = ((), (), s32[]{:S(2)}) async-start(), calls=%async_computation.29 | async-start | bytes 3760128 | tf_op jit(solution)/shard_map/reduce_scatter | solution.py:314
  1562.2 320.5 %reduce-scatter.44.cloned.1.call-start = ((), (), s32[]{:S(2)}) async-start(), calls=%async_computation.38 | async-start | bytes 589824
  1635.5 248.9 %reduce-scatter.34.cloned.1.call-start = ((), (), s32[]{:S(2)}) async-start(), calls=%async_computation.33 | async-start | bytes 442368 | tf_op jit(solution)/shard_map/reduce_scatter | solution.py:344
  1713.2 222.5 %reduce-scatter.36.cloned.1.call-start = ((), (), s32[]{:S(2)}) async-start(), calls=%async_computation.34 | async-start | bytes 7077888 | tf_op jit(solution)/shard_map/reduce_scatter | solution.py:347
  1739.6 258.4 %reduce-scatter.38.cloned.1.call-start = ((), (), s32[]{:S(2)}) async-start(), calls=%async_computation.35 | async-start | bytes 7077888 | tf_op jit(solution)/shard_map/reduce_scatter | solution.py:350
  1766.2 245.5 %reduce-scatter.42.cloned.1.call-start = ((), (), s32[]{:S(2)}) async-start(), calls=%async_computation.37 | async-start | bytes 294912
  1775.4 251.8 %reduce-scatter.40.cloned.1.call-start = ((), (), s32[]{:S(2)}) async-start(), calls=%async_computation.36 | async-start | bytes 589824
  1846.4 350.4 %reduce-scatter.24.cloned.1.call-start = ((), (), s32[]{:S(2)}) async-start(), calls=%async_computation.28 | async-start | bytes 14598144 | tf_op jit(solution)/shard_map/reduce_scatter | solution.py:310
  (64 other events, 799.9 us)
Sparse Core Ops, SparseCore 0:
  18.5 66.9 all-gather.9
  87.8 45.6 all-gather.11
  142.0 43.9 all-gather.13
  188.0 44.9 all-gather.15
  235.1 38.3 all-gather.17
  442.2 62.9 all-gather.23
  584.9 62.9 all-gather.25
  650.2 88.0 all-gather.19
  839.2 120.4 all-gather.21
  1442.2 65.7 reduce-scatter.21
  1510.3 43.3 reduce-scatter.19
  1558.0 75.5 reduce-scatter.29
  1638.5 74.5 reduce-scatter.31
  1716.6 57.0 reduce-scatter.27
  1777.4 67.0 reduce-scatter.25
  1846.6 11.8 reduce-scatter.43
  1860.7 12.0 reduce-scatter.33
  1875.6 59.9 reduce-scatter.35
  1938.0 59.9 reduce-scatter.37
  2000.7 10.9 reduce-scatter.41
  2014.1 13.1 reduce-scatter.39
  2033.8 162.9 reduce-scatter.23
where the time goes:
time: 2210 us; the launch traced here: 2200 us
  waiting for transfers between devices  1050 us (48%)
  matrix products  643 us (29%)
  local copies, waits for them, and re-layouts  193 us (9%)
  other arithmetic  154 us (7%)
  starting transfers between devices  110 us (5%)
  blocking collectives  35.6 us (2%)
    dot_general x41, matrix products, product(): return jnp.einsum(form, left, right, preferred_element_type=jnp.float32)  533 us
    reduce_scatter x1, waiting for transfers between devices, on_device(): lax.psum_scatter(arranged, ('wide', 'narrow'), scatter_dimension=0, tiled...  168 us
    all_to_all x1, waiting for transfers between devices, on_device(): lax.all_to_all(grad_sent.reshape(expert_count, capacity, model_width), 'w...  110 us
    all_to_all x1, waiting for transfers between devices, on_device(): lax.all_to_all(outgoing.reshape(expert_count, capacity, model_width), 'wi...  81.9 us
    reduce_scatter x1, waiting for transfers between devices, on_device(): lax.psum_scatter(contract_grad_full.astype(jnp.bfloat16), 'wide', scatter...  77.5 us
    reduce_scatter x1, waiting for transfers between devices, on_device(): lax.psum_scatter(expand_grad_full.astype(jnp.bfloat16), 'wide', scatter_d...  71.4 us
    all_gather x1, waiting for transfers between devices, on_device(): lax.all_gather(modulation_part, 'wide', axis=1, tiled=True)  58.9 us
    all_to_all x1, waiting for transfers between devices, on_device(): lax.all_to_all(grad_outgoing.reshape(expert_count, capacity, model_width)...  58.3 us
  transfers between devices with their start and end apart: 26, of which 20 were waited for; matrix products, arithmetic and copies ran while one was open for 28% of the time, Pallas kernels for 0%

commit v1 on v0

v1 whole, which is shorter than its diff:
```python
import functools

import jax
import jax.numpy as jnp
from jax import lax
from jax.experimental import pallas as pl
from jax.experimental.pallas import tpu as pltpu
from jax.sharding import PartitionSpec as P

HEADS = 12
IMG_SHORT = 256
EPSILON = 1e-06
QUAD = 4
F32 = jnp.float32
BF16 = jnp.bfloat16
NN = (((1,), (0,)), ((), ()))
NT = (((1,), (1,)), ((), ()))
VMEM_BYTES = 48 << 20


def dot(left, right, dims=NN):
    return lax.dot_general(left, right, dims, preferred_element_type=F32)


def product(left, right, form):
    return jnp.einsum(form, left, right, preferred_element_type=F32)


def normalize(values):
    centered = values - jnp.mean(values, axis=-1, keepdims=True)
    variance = jnp.mean(centered * centered, axis=-1, keepdims=True)
    return centered * lax.rsqrt(variance + EPSILON)


def norm_back(values, grad_normed):
    centered = values - jnp.mean(values, axis=-1, keepdims=True)
    variance = jnp.mean(centered * centered, axis=-1, keepdims=True)
    inverse = lax.rsqrt(variance + EPSILON)
    normed = centered * inverse
    return inverse * (
        grad_normed
        - jnp.mean(grad_normed, axis=-1, keepdims=True)
        - normed * jnp.mean(grad_normed * normed, axis=-1, keepdims=True)
    )


def of_head(values, which, axis, head_dim):
    place = lax.broadcasted_iota(jnp.int32, values.shape, axis) // head_dim
    return jnp.where(place == which, values, jnp.zeros_like(values))


def over_blocks(low, high, all_blocks, step, state):
    def unrolled():
        inner = state
        for block in range(all_blocks):
            inner = step(block, inner)
        return inner

    def several(count):
        def body(index, inner):
            for extra in range(count):
                inner = step(low + index * count + extra, inner)
            return inner

        return body

    def looped():
        groups = (high - low) // 4
        inner = lax.fori_loop(0, groups, several(4), state)
        return lax.fori_loop(low + groups * 4, high, step, inner)

    return lax.cond(high - low == all_blocks, unrolled, looped)


def at_block(block, size):
    return block * size if isinstance(block, int) else pl.multiple_of(block * size, size)


def forward_kernel(
    head_dim, size, low_ref, high_ref, q_ref, k_ref, v_ref, out_ref, exact_ref, total_ref, vt, kept
):
    row_block = pl.program_id(1)

    @pl.when(row_block == 0)
    def _():
        vt[...] = v_ref[...].T

    queries = (q_ref[...].astype(F32) * head_dim**-0.5).astype(BF16).T
    rows = q_ref.shape[0]
    by_head = [of_head(queries, h, 0, head_dim) for h in range(QUAD)]
    low, high = low_ref[row_block], high_ref[row_block]
    blocks = k_ref.shape[0] // size

    def score_step(block, tops):
        at = at_block(block, size)
        keys = k_ref[pl.ds(at, size), :]
        fresh = []
        for h in range(QUAD):
            scores = dot(keys, by_head[h])
            kept[h, pl.ds(at, size), :] = scores
            fresh.append(
                jnp.maximum(tops[h], jnp.max(scores.reshape(size // 8, 8, rows), axis=0))
            )
        return tuple(fresh)

    tops = over_blocks(
        low, high, blocks, score_step, tuple(jnp.full((8, rows), -1e30, F32) for _ in range(QUAD))
    )
    tops = [jnp.max(t, axis=0, keepdims=True) for t in tops]

    def mix_step(block, state):
        at = at_block(block, size)
        fresh = []
        for h in range(QUAD):
            total, mixed = state[h]
            weights = jnp.exp(kept[h, pl.ds(at, size), :] - tops[h])
            total = total + jnp.sum(weights.reshape(size // 8, 8, rows), axis=0)
            values = vt[h * head_dim : (h + 1) * head_dim, pl.ds(at, size)]
            fresh.append((total, mixed + dot(values, weights.astype(BF16))))
        return tuple(fresh)

    state = over_blocks(
        low,
        high,
        blocks,
        mix_step,
        tuple((jnp.zeros((8, rows), F32), jnp.zeros((head_dim, rows), F32)) for _ in range(QUAD)),
    )
    mixed = []
    for h in range(QUAD):
        total = jnp.sum(state[h][0], axis=0, keepdims=True)
        mixed.append(state[h][1] / total)
        total_ref[0, h : h + 1, :] = tops[h] + jnp.log(total)
    mixed = jnp.concatenate(mixed, axis=0).T
    exact_ref[...] = mixed
    out_ref[...] = mixed.astype(BF16)


def attention_forward(queries, keys, values, low, high):
    rows, width = queries.shape
    key_rows = keys.shape[0]
    head_dim = width // HEADS
    lanes, quads = QUAD * head_dim, HEADS // QUAD
    size = IMG_SHORT
    row_spec = pl.BlockSpec((size, lanes), lambda j, i, *_: (i, j))
    key_spec = pl.BlockSpec((key_rows, lanes), lambda j, i, *_: (0, j))
    return pl.pallas_call(
        functools.partial(forward_kernel, head_dim, size),
        grid_spec=pltpu.PrefetchScalarGridSpec(
            num_scalar_prefetch=2,
            grid=(quads, rows // size),
            in_specs=[row_spec, key_spec, key_spec],
            out_specs=[
                row_spec,
                row_spec,
                pl.BlockSpec((1, QUAD, size), lambda j, i, *_: (j, 0, i)),
            ],
            scratch_shapes=[
                pltpu.VMEM((lanes, key_rows), BF16),
                pltpu.VMEM((QUAD, key_rows, size), F32),
            ],
        ),
        out_shape=[
            jax.ShapeDtypeStruct((rows, width), BF16),
            jax.ShapeDtypeStruct((rows, width), F32),
            jax.ShapeDtypeStruct((quads, QUAD, rows), F32),
        ],
        compiler_params=pltpu.CompilerParams(vmem_limit_bytes=VMEM_BYTES),
        cost_estimate=pl.CostEstimate(
            flops=16 * rows * key_rows * width,
            transcendentals=rows * key_rows * HEADS,
            bytes_accessed=4 * key_rows * width + 8 * rows * width,
        ),
        name="attention_forward",
    )(low, high, queries, keys, values)


def backward_kernel(
    head_dim,
    size,
    low_ref,
    high_ref,
    q_ref,
    k_ref,
    v_ref,
    grad_ref,
    exact_ref,
    total_ref,
    dq_ref,
    dk_ref,
    dv_ref,
    kt,
    dk_sum,
    dv_sum,
):
    row_block = pl.program_id(1)

    @pl.when(row_block == 0)
    def _():
        kt[...] = k_ref[...].T
        dk_sum[...] = jnp.zeros_like(dk_sum)
        dv_sum[...] = jnp.zeros_like(dv_sum)

    scale = head_dim**-0.5
    queries = (q_ref[...].astype(F32) * scale).astype(BF16)
    grads = grad_ref[...]
    rows = queries.shape[0]
    heads = range(QUAD)
    dots = (grads.astype(F32) * exact_ref[...]).T
    dots = [
        jnp.sum(dots[h * head_dim : (h + 1) * head_dim], axis=0, keepdims=True) for h in heads
    ]
    q_columns, g_columns = queries.T, grads.T
    q_columns = [of_head(q_columns, h, 0, head_dim) for h in heads]
    g_columns = [of_head(g_columns, h, 0, head_dim) for h in heads]
    q_rows = jnp.concatenate([of_head(queries, h, 1, head_dim) for h in heads], axis=0)
    g_rows = jnp.concatenate([of_head(grads, h, 1, head_dim) for h in heads], axis=0)
    totals = [total_ref[0, h : h + 1, :] for h in heads]
    low, high = low_ref[row_block], high_ref[row_block]
    blocks = k_ref.shape[0] // size

    def step(block, dq):
        at = at_block(block, size)
        keys = k_ref[pl.ds(at, size), :]
        values = v_ref[pl.ds(at, size), :]
        weights, score_grads, fresh = [], [], []
        for h in heads:
            softmax = jnp.exp(dot(keys, q_columns[h]) - totals[h])
            grad = (softmax * (dot(values, g_columns[h]) - dots[h])).astype(BF16)
            weights.append(softmax.astype(BF16))
            score_grads.append(grad)
            columns = kt[h * head_dim : (h + 1) * head_dim, pl.ds(at, size)]
            fresh.append(dq[h] + dot(columns, grad))
        dv_sum[pl.ds(at, size), :] += dot(jnp.concatenate(weights, axis=1), g_rows)
        dk_sum[pl.ds(at, size), :] += dot(jnp.concatenate(score_grads, axis=1), q_rows)
        return tuple(fresh)

    dq = over_blocks(
        low, high, blocks, step, tuple(jnp.zeros((head_dim, rows), F32) for _ in heads)
    )
    dq_ref[...] = (jnp.concatenate(dq, axis=0) * scale).T.astype(BF16)

    @pl.when(row_block == pl.num_programs(1) - 1)
    def _():
        dk_ref[...] = dk_sum[...].astype(BF16)
        dv_ref[...] = dv_sum[...].astype(BF16)


def attention_backward(queries, keys, values, grads, exact, totals, low, high):
    rows, width = queries.shape
    key_rows = keys.shape[0]
    head_dim = width // HEADS
    lanes, quads = QUAD * head_dim, HEADS // QUAD
    size = IMG_SHORT
    row_spec = pl.BlockSpec((size, lanes), lambda j, i, *_: (i, j))
    key_spec = pl.BlockSpec((key_rows, lanes), lambda j, i, *_: (0, j))
    return pl.pallas_call(
        functools.partial(backward_kernel, head_dim, size),
        grid_spec=pltpu.PrefetchScalarGridSpec(
            num_scalar_prefetch=2,
            grid=(quads, rows // size),
            in_specs=[
                row_spec,
                key_spec,
                key_spec,
                row_spec,
                row_spec,
                pl.BlockSpec((1, QUAD, size), lambda j, i, *_: (j, 0, i)),
            ],
            out_specs=[row_spec, key_spec, key_spec],
            scratch_shapes=[
                pltpu.VMEM((lanes, key_rows), BF16),
                pltpu.VMEM((key_rows, lanes), F32),
                pltpu.VMEM((key_rows, lanes), F32),
            ],
        ),
        out_shape=[
            jax.ShapeDtypeStruct((rows, width), BF16),
            jax.ShapeDtypeStruct((key_rows, width), BF16),
            jax.ShapeDtypeStruct((key_rows, width), BF16),
        ],
        compiler_params=pltpu.CompilerParams(vmem_limit_bytes=VMEM_BYTES),
        cost_estimate=pl.CostEstimate(
            flops=40 * rows * key_rows * width,
            transcendentals=rows * key_rows * HEADS,
            bytes_accessed=8 * key_rows * width + 10 * rows * width,
        ),
        name="attention_backward",
    )(low, high, queries, keys, values, grads, exact, totals)


def pack_kernel(place_ref, scale_ref, values_ref, out_ref):
    expert = pl.program_id(0)
    capacity = out_ref.shape[0]
    places = place_ref[pl.ds(expert, 1), :]
    slots = lax.broadcasted_iota(jnp.int32, (capacity, places.shape[1]), 0)
    chosen = slots == places
    rows = dot(chosen.astype(BF16), values_ref[...])
    if scale_ref is not None:
        scales = jnp.where(chosen, scale_ref[pl.ds(expert, 1), :], 0.0)
        rows = rows * jnp.sum(scales, axis=1, keepdims=True)
    out_ref[...] = rows.astype(BF16)


def pack(places, scales, values, capacity):
    experts, rows = places.shape
    width = values.shape[1]
    whole = lambda shape: pl.BlockSpec(shape, lambda e: (0, 0))
    operands = [places, values] if scales is None else [places, scales, values]
    kernel = pack_kernel
    if scales is None:
        kernel = lambda place_ref, values_ref, out_ref: pack_kernel(
            place_ref, None, values_ref, out_ref
        )
    return pl.pallas_call(
        kernel,
        grid=(experts,),
        in_specs=[whole(o.shape) for o in operands],
        out_specs=pl.BlockSpec((capacity, width), lambda e: (e, 0)),
        out_shape=jax.ShapeDtypeStruct((experts * capacity, width), BF16),
        compiler_params=pltpu.CompilerParams(vmem_limit_bytes=VMEM_BYTES),
        cost_estimate=pl.CostEstimate(
            flops=2 * experts * capacity * rows * width,
            transcendentals=0,
            bytes_accessed=2 * width * (rows + experts * capacity),
        ),
        name="pack",
    )(*operands)


def combine_kernel(experts, capacity, place_ref, scale_ref, rows_ref, out_ref):
    total = None
    tokens = out_ref.shape[0]
    slots = lax.broadcasted_iota(jnp.int32, (tokens, capacity), 1)
    for expert in range(experts):
        scale = 1.0 if scale_ref is None else scale_ref[:, expert : expert + 1]
        chosen = jnp.where(slots == place_ref[:, expert : expert + 1], scale, 0.0)
        part = dot(chosen.astype(BF16), rows_ref[expert * capacity : (expert + 1) * capacity, :])
        total = part if total is None else total + part
    out_ref[...] = total


def combine(places, scales, rows, capacity):
    tokens, experts = places.shape
    width = rows.shape[1]
    block = min(256, tokens)
    part = pl.BlockSpec((block, experts), lambda i: (i, 0))
    kernel = functools.partial(combine_kernel, experts, capacity)
    operands = [places, rows] if scales is None else [places, scales, rows]
    if scales is None:
        kernel = lambda place_ref, rows_ref, out_ref: combine_kernel(
            experts, capacity, place_ref, None, rows_ref, out_ref
        )
    return pl.pallas_call(
        kernel,
        grid=(tokens // block,),
        in_specs=[part] * (len(operands) - 1)
        + [pl.BlockSpec(rows.shape, lambda i: (0, 0), pipeline_mode=pl.Buffered(1))],
        out_specs=pl.BlockSpec((block, width), lambda i: (i, 0)),
        out_shape=jax.ShapeDtypeStruct((tokens, width), F32),
        compiler_params=pltpu.CompilerParams(vmem_limit_bytes=VMEM_BYTES),
        cost_estimate=pl.CostEstimate(
            flops=2 * experts * capacity * tokens * width,
            transcendentals=0,
            bytes_accessed=2 * width * (2 * tokens + experts * capacity),
        ),
        name="combine",
    )(*operands)


def gelu_both(hidden):
    inner = 0.7978845608028654
    square = hidden * hidden
    bend = jnp.tanh(hidden * (inner + (inner * 0.044715) * square))
    half = 0.5 + 0.5 * bend
    slope = half + (0.5 * hidden) * (1.0 - bend * bend) * (inner + (3 * inner * 0.044715) * square)
    return hidden * half, slope


def feed_kernel(
    transposed, tile, with_out, in_ref, grad_ref, up_ref, down_ref, act_ref, hid_ref, back_ref, *out
):
    rows, grads = in_ref[...], grad_ref[...]
    hidden_size = act_ref.shape[1]
    for start in range(0, hidden_size, tile):
        part = slice(start, start + tile)
        if transposed:
            hidden = dot(rows, up_ref[part, :], NT)
            grad = dot(grads, down_ref[:, part])
        else:
            hidden = dot(rows, up_ref[:, part])
            grad = dot(grads, down_ref[part, :], NT)
        active, slope = gelu_both(hidden)
        act_ref[:, part] = active.astype(BF16)
        hid_ref[:, part] = (grad * slope).astype(BF16)
    back = dot(hid_ref[...], up_ref[...], NN if transposed else NT)
    back_ref[...] = back.astype(back_ref.dtype)
    if with_out:
        out[0][...] = dot(act_ref[...], down_ref[...], NT if transposed else NN).astype(
            out[0].dtype
        )


def feed(rows, grads, up, down, transposed, out_dtype, with_out):
    count, width = rows.shape
    hidden_size = up.shape[0] if transposed else up.shape[1]
    block = min(256, count)
    row = pl.BlockSpec((block, width), lambda i: (i, 0))
    hid = pl.BlockSpec((block, hidden_size), lambda i: (i, 0))
    fixed = lambda a: pl.BlockSpec(a.shape, lambda i: (0, 0), pipeline_mode=pl.Buffered(1))
    extra = 1 if with_out else 0
    return pl.pallas_call(
        functools.partial(feed_kernel, transposed, min(512, hidden_size), with_out),
        grid=(count // block,),
        in_specs=[row, row, fixed(up), fixed(down)],
        out_specs=[hid, hid, row] + [row] * extra,
        out_shape=[
            jax.ShapeDtypeStruct((count, hidden_size), BF16),
            jax.ShapeDtypeStruct((count, hidden_size), BF16),
            jax.ShapeDtypeStruct((count, width), out_dtype),
        ]
        + [jax.ShapeDtypeStruct((count, width), out_dtype)] * extra,
        compiler_params=pltpu.CompilerParams(vmem_limit_bytes=VMEM_BYTES),
        cost_estimate=pl.CostEstimate(
            flops=(6 + 2 * extra) * count * width * hidden_size,
            transcendentals=count * hidden_size,
            bytes_accessed=4 * count * hidden_size + 8 * count * width + 4 * width * hidden_size,
        ),
        name="feed",
    )(rows, grads, up, down)


def swap(values):
    return lax.ppermute(values, "narrow", [(0, 1), (1, 0)])


def gather_narrow(values, axis):
    if lax.axis_size("narrow") != 2:
        return lax.all_gather(values, "narrow", axis=axis, tiled=True)
    other = swap(values)
    return jnp.where(
        lax.axis_index("narrow") == 0,
        jnp.concatenate([values, other], axis=axis),
        jnp.concatenate([other, values], axis=axis),
    )


def part_of(values, index, size, axis):
    return lax.dynamic_slice_in_dim(values, index * size, size, axis)


def reduce_narrow(values, axis):
    count = lax.axis_size("narrow")
    if count != 2:
        return lax.psum_scatter(
            values.astype(BF16), "narrow", scatter_dimension=axis, tiled=True
        ).astype(F32)
    size = values.shape[axis] // 2
    index = lax.axis_index("narrow")
    other = swap(part_of(values, 1 - index, size, axis).astype(BF16))
    return part_of(values, index, size, axis).astype(F32) + other.astype(F32)


def exchange(rows):
    wide = lax.axis_size("wide")
    blocks = rows.reshape(wide, rows.shape[0] // wide, rows.shape[1])
    return lax.all_to_all(blocks, "wide", split_axis=0, concat_axis=0, tiled=True).reshape(
        rows.shape
    )


def gather_wide(values):
    return lax.all_gather(values, "wide", axis=0, tiled=True)


def reduce_wide(values):
    return lax.psum_scatter(values, "wide", scatter_dimension=0, tiled=True)


def on_device(
    patches,
    conditions,
    modulation_weight,
    attention_weight,
    projection_weight,
    expand_weight,
    contract_weight,
    expert_expand,
    expert_contract,
    image_start,
    routes,
    route_gates,
    cotangent,
):
    local_rows, width = patches.shape
    slots = conditions.shape[0]
    experts = lax.axis_size("wide")
    narrow = lax.axis_size("narrow")
    capacity = 4 * local_rows // experts
    mine = lax.axis_index("narrow")
    group_slots = narrow * slots
    group_rows = narrow * local_rows

    attention_t = gather_wide(gather_narrow(attention_weight.T, 1))
    modulation_columns = gather_narrow(modulation_weight, 0)
    group_patches = gather_narrow(patches, 0)
    projection_t = gather_wide(gather_narrow(projection_weight.T, 1))
    expand_t = gather_wide(gather_narrow(expand_weight.T, 1))
    contract_t = gather_wide(gather_narrow(contract_weight.T, 1))
    up = gather_narrow(expert_expand[0], 0)
    down = gather_narrow(expert_contract[0], 0)

    all_conditions = lax.all_gather(conditions, ("wide", "narrow"), axis=0, tiled=True)
    lifted = jax.nn.silu(all_conditions.astype(F32)).astype(BF16)
    columns = jnp.dot(lifted, modulation_columns, preferred_element_type=F32)
    share = columns.shape[1]
    modulation = lax.all_to_all(
        columns.reshape(experts, group_slots, share), "wide", split_axis=0, concat_axis=0, tiled=True
    )
    modulation = modulation.transpose(1, 0, 2).reshape(group_slots, 6, 1, width)
    own = part_of(modulation, mine, slots, 0)
    shift_a, scale_a, gate_a, shift_b, scale_b, gate_b = [own[:, i] for i in range(6)]

    expert_ids = jnp.arange(experts, dtype=jnp.int32)[None, :]
    named = routes[:, :, None] == expert_ids[None]
    chosen = jnp.any(named, axis=1)
    order = jnp.arange(local_rows, dtype=jnp.int32)
    earlier = (order[:, None] > order[None, :]).astype(BF16)
    rank = jnp.dot(earlier, chosen.astype(BF16), preferred_element_type=F32).astype(jnp.int32)
    places = jnp.where(chosen, rank, -1)
    gates = jnp.sum(jnp.where(named, route_gates[:, :, None], 0.0), axis=1)
    places_t, gates_t = places.T, gates.T

    grad_top = cotangent.astype(F32).reshape(slots, IMG_SHORT, width)
    grad_shared = (gate_b * grad_top).astype(BF16).reshape(local_rows, width)
    grad_arrived = exchange(pack(places_t, gates_t, grad_shared, capacity))

    block_start = image_start.reshape(group_slots, IMG_SHORT)[:, 0]
    own_start = part_of(block_start, mine, slots, 0)
    low = own_start - block_start[0]
    high = low + jnp.sum(own_start[:, None] == block_start[None, :], axis=1, dtype=jnp.int32)
    group_inputs = group_patches.astype(F32).reshape(group_slots, IMG_SHORT, width)
    group_entry = (
        (normalize(group_inputs) * (1.0 + modulation[:, 1]) + modulation[:, 0])
        .astype(BF16)
        .reshape(group_rows, width)
    )
    first_entry = part_of(group_entry, mine, local_rows, 0)
    query_t, key_value_t = attention_t[:width], attention_t[width:]
    queries = product(first_entry, query_t, "td,ed->te").astype(BF16)
    keys = product(group_entry, attention_t[width : 2 * width], "td,ed->te").astype(BF16)
    values = product(group_entry, attention_t[2 * width :], "td,ed->te").astype(BF16)
    mixed_heads, exact_heads, totals = attention_forward(queries, keys, values, low, high)
    attended = product(mixed_heads, projection_t, "td,ed->te").reshape(slots, IMG_SHORT, width)
    inputs = patches.astype(F32).reshape(slots, IMG_SHORT, width)
    middle = inputs + gate_a * attended
    normed_b = normalize(middle)
    second = (normed_b * (1.0 + scale_b) + shift_b).astype(BF16).reshape(local_rows, width)

    arrived = exchange(pack(places_t, None, second, capacity))
    expert_active, grad_expert_hidden, grad_sent = feed(
        arrived, grad_arrived, up, down, False, BF16, False
    )
    grad_returned = exchange(grad_sent)
    produced = product(expert_active, down, "rf,fd->rd").astype(BF16)
    returned = exchange(produced)

    activated, grad_hidden, grad_second, shared = feed(
        second, grad_shared, expand_t, contract_t, True, F32, True
    )
    contract_grad_t = product(grad_shared, activated, "td,tf->df").astype(BF16)
    expand_grad_t = product(grad_hidden, second, "tf,td->fd").astype(BF16)
    down_grad = product(expert_active, grad_arrived, "rf,rd->fd")
    up_grad = product(arrived, grad_expert_hidden, "rd,rf->df")
    expert_up_grad = reduce_narrow(up_grad, 0)[None]
    expert_down_grad = reduce_narrow(down_grad, 0)[None]

    grad_second = grad_second + combine(places, None, grad_returned, capacity)
    grad_second = grad_second.reshape(slots, IMG_SHORT, width)
    grad_shift_b = jnp.sum(grad_second, axis=1)
    grad_scale_b = jnp.sum(grad_second * normed_b, axis=1)
    grad_middle = grad_top + norm_back(middle, grad_second * (1.0 + scale_b))
    grad_gate_a = jnp.sum(grad_middle * attended, axis=1)
    grad_attended = (gate_a * grad_middle).reshape(local_rows, width).astype(BF16)
    projection_grad_t = product(grad_attended, mixed_heads, "te,td->ed").astype(BF16)
    grad_mixed = product(grad_attended, projection_t, "te,ed->td").astype(BF16)
    grad_queries, grad_keys, grad_values = attention_backward(
        queries, keys, values, grad_mixed, exact_heads, totals, low, high
    )

    mixture = shared + combine(places, gates, returned, capacity)
    mixture = mixture.reshape(slots, IMG_SHORT, width)
    block_out = (middle + gate_b * mixture).reshape(local_rows, width).astype(BF16)
    grad_gate_b = jnp.sum(grad_top * mixture, axis=1)

    attention_grad_t = jnp.concatenate(
        [
            product(grad_queries, first_entry, "te,td->ed").astype(BF16),
            product(grad_keys, group_entry, "te,td->ed").astype(BF16),
            product(grad_values, group_entry, "te,td->ed").astype(BF16),
        ],
        axis=0,
    )
    grad_group = product(grad_keys, attention_t[width : 2 * width], "te,ed->td") + product(
        grad_values, attention_t[2 * width :], "te,ed->td"
    )
    grad_entry = reduce_narrow(grad_group, 0) + product(grad_queries, query_t, "te,ed->td")
    grad_entry = grad_entry.reshape(slots, IMG_SHORT, width)
    grad_shift_a = jnp.sum(grad_entry, axis=1)
    grad_scale_a = jnp.sum(grad_entry * normalize(inputs), axis=1)
    grad_inputs = grad_middle + norm_back(inputs, grad_entry * (1.0 + scale_a))
    patch_grad = grad_inputs.reshape(local_rows, width).astype(BF16)

    grad_modulation = jnp.stack(
        [grad_shift_a, grad_scale_a, grad_gate_a, grad_shift_b, grad_scale_b, grad_gate_b], axis=1
    )
    grad_modulation = grad_modulation.reshape(slots, experts, share).astype(BF16)
    grad_modulation = lax.all_to_all(
        grad_modulation.transpose(1, 0, 2), "wide", split_axis=0, concat_axis=0, tiled=True
    )
    grad_modulation = lax.all_gather(grad_modulation, "narrow", axis=1, tiled=True)
    row_share = width // narrow
    modulation_grad = product(
        part_of(lifted, mine, row_share, 1),
        grad_modulation.reshape(experts * group_slots, share),
        "sd,se->de",
    )
    expand_grad = reduce_narrow(reduce_wide(expand_grad_t), 1).T
    contract_grad = reduce_narrow(reduce_wide(contract_grad_t), 1).T
    projection_grad = reduce_narrow(reduce_wide(projection_grad_t), 1).T
    attention_grad = reduce_narrow(reduce_wide(attention_grad_t), 1).T
    return (
        block_out,
        patch_grad,
        modulation_grad,
        attention_grad,
        projection_grad,
        expand_grad,
        contract_grad,
        expert_up_grad,
        expert_down_grad,
    )


def solution(mesh):
    rows = P(("wide", "narrow"), None)
    dense = P("narrow", "wide")
    expert = P("wide", "narrow", None)
    return jax.shard_map(
        on_device,
        mesh=mesh,
        in_specs=(rows, rows, dense, dense, dense, dense, dense, expert, expert, P("wide"), rows, rows, rows),
        out_specs=(rows, rows, dense, dense, dense, dense, dense, expert, expert),
        check_vma=False,
    )
```

time: 2210 us -> 963 us (0.44)
  waiting for transfers between devices: 1050 us -> 174 us
  matrix products: 643 us -> 142 us
  Pallas kernels: 0 us -> 321 us
  local copies, waits for them, and re-layouts: 193 us -> 25.4 us
  other arithmetic: 154 us -> 75.2 us
  blocking collectives: 35.6 us -> 70.8 us
  starting transfers between devices: 110 us -> 136 us
    reduce_scatter x10 -> x4, waiting for transfers between devices: 559 us -> 12.4 us  [reduce_wide(): return lax.psum_scatter(values, 'wide', scatter_dimension=0, tiled=True)]
    dot_general x48 -> x20, matrix products: 643 us -> 142 us  [the longest x18 140 us: product(): return jnp.einsum(form, left, right, preferred_element_type=F32)]
    pallas_call x0 -> x8, Pallas kernels: none -> 321 us  [the longest x1 120 us: attention_backward(): pl.pallas_call(functools.partial(backward_kernel, head_dim, size), grid_s...]
    all_to_all x4 -> x6, waiting for transfers between devices: 294 us -> 24.5 us  [the longest x4 15.7 us: exchange(): lax.all_to_all(blocks, 'wide', split_axis=0, concat_axis=0, tiled=True)]
    all_gather x9 -> x4, waiting for transfers between devices: 173 us -> 0.04 us  [gather_wide(): return lax.all_gather(values, 'wide', axis=0, tiled=True)]
    ppermute x0 -> x15, waiting for transfers between devices: none -> 137 us  [swap(): return lax.ppermute(values, 'narrow', [(0, 1), (1, 0)])]
    reduce_sum x11 -> x5, other arithmetic: 105 us -> 8.38 us  [the longest x1 4.67 us: on_device(): grad_scale_b = jnp.sum(grad_second * normed_b, axis=1)]
    all_gather x5 -> x2, blocking collectives: 35.6 us -> 70.8 us  [the longest x1 66 us: on_device(): lax.all_gather(conditions, ('wide', 'narrow'), axis=0, tiled=True)]
  transfers between devices with their start and end apart: 26 -> 29, of which waited for: 20 -> 15; matrix products, arithmetic and copies ran while one was open for 28% -> 24% of each run, Pallas kernels for 0% -> 33%
where the time goes in v1:
time: 963 us; the launch traced here: 959 us
  Pallas kernels  321 us (33%)
  waiting for transfers between devices  174 us (18%)
  matrix products  142 us (15%)
  starting transfers between devices  136 us (14%)
  other arithmetic  75.2 us (8%)
  blocking collectives  70.8 us (7%)
  local copies, waits for them, and re-layouts  25.4 us (3%)
  between operations  15.6 us (2%)
    dot_general x18, matrix products, product(): return jnp.einsum(form, left, right, preferred_element_type=F32)  140 us
    ppermute x15, waiting for transfers between devices, swap(): return lax.ppermute(values, 'narrow', [(0, 1), (1, 0)])  137 us
    pallas_call x1, Pallas kernels, attention_backward(): pl.pallas_call(functools.partial(backward_kernel, head_dim, size), grid_s...  120 us
    pallas_call x2, Pallas kernels, feed(): pl.pallas_call(functools.partial(feed_kernel, transposed, min(512, hidden...  105 us
    all_to_all x4, starting transfers between devices, exchange(): lax.all_to_all(blocks, 'wide', split_axis=0, concat_axis=0, tiled=True)  102 us
    all_gather x1, blocking collectives, on_device(): lax.all_gather(conditions, ('wide', 'narrow'), axis=0, tiled=True)  66 us
    pallas_call x1, Pallas kernels, attention_forward(): pl.pallas_call(functools.partial(forward_kernel, head_dim, size), grid_sp...  50.2 us
    pallas_call x2, Pallas kernels, pack(): pl.pallas_call(kernel, grid=(experts,), in_specs=[whole(o.shape) for o in...  24 us
  transfers between devices with their start and end apart: 29, of which 15 were waited for; matrix products, arithmetic and copies ran while one was open for 24% of the time, Pallas kernels for 33%

profile of v1, /device:TPU:0, one launch (start us, length us, event | category | flops | bytes accessed | tf_op | source)
XLA Modules:
  0.0 958.7 jit_solution(5774649610295934247)
XLA Ops:
  30.1 66.0 %all-gather = bf16[32,4,768]{2,1,0:T(4,128)(2,1)S(1)} all-gather(bf16[1,4,768]{2,1,0:T(4,128)(2,1)} %bitcast.198), channel_id=1, replica_groups=mesh['wide'=16,'narrow'=2] {'wide','narrow'}, dimensions={0}, use_global_device_ids=true | all-gather | bytes 202752 | tf_op jit(solution)/shard_map/all_gather | solution.py:513
  102.8 8.1 all-to-all-done
  112.4 12.5 %pack.3 = bf16[4096,768]{1,0:T(8,128)(2,1)} custom-call(s32[16,1024]{1,0:T(8,128)S(1)} %copy.63.place_ref, f32[16,1024]{1,0:T(8,128)S(1)} %bitcast.165, bf16[1024,768]{1,0:T(8,128)(2,1)S(1)} %fusion.9.grad_ref.values_ref), custom_call_target="tpu_custom_call" | custom-call | flops 6442450944 | bytes 7864320 | tf_op jit(solution)/shard_map/pack/pallas_call | solution.py:315
  142.8 31.1 %collective-permute-done.1 = bf16[1024,768]{1,0:T(8,128)(2,1)} collective-permute-done((bf16[1024,768]{1,0:T(8,128)(2,1)S(1)}, bf16[1024,768]{1,0:T(8,128)(2,1)}, u32[]{:S(2)}, u32[]{:S(2)}) %collective-permute-start.1) | collective-permute-done | bytes 1572896 | tf_op jit(solution)/shard_map/ppermute | solution.py:434
  199.5 50.2 %attention_forward.1 = (bf16[1024,768]{1,0:T(8,128)(2,1)S(1)}, f32[1024,768]{1,0:T(8,128)}, f32[3,4,1024]{2,1,0:T(4,128)S(1)}) custom-call(s32[4]{0:T(128)S(1)} %get-tuple-element.54.low_ref, s32[4]{0:T(128)S(1)} %get-tuple-element.53.high_ref, bf16[1024,768]{1,0:T(8,128)(2,1)S(1)} %convolution_convert_fusion.6.q_ref, ...), custom_call_target="tpu_custom_call" | custom-call | flops 25769803776 | bytes 12582912 | tf_op jit(solution)/shard_map/attention_forward/pallas_call | solution.py:147
  257.7 11.5 %pack.2 = bf16[4096,768]{1,0:T(8,128)(2,1)} custom-call(s32[16,1024]{1,0:T(8,128)S(1)} %copy.63.place_ref, bf16[1024,768]{1,0:T(8,128)(2,1)S(1)} %fusion.13.in_ref.values_ref), custom_call_target="tpu_custom_call" | custom-call | flops 6442450944 | bytes 7864320 | tf_op jit(solution)/shard_map/pack/pallas_call | solution.py:315
  272.2 47.1 %all-to-all-start.1 = ((bf16[16,256,768]{2,1,0:T(8,128)(2,1)}), bf16[16,256,768]{2,1,0:T(8,128)(2,1)}, u32[]{:S(2)}, u32[]{:S(2)}) async-start(bf16[16,256,768]{2,1,0:T(8,128)(2,1)} %bitcast.166), calls=%async_computation.1 | async-start | bytes 12582912 | tf_op jit(solution)/shard_map/all_to_all | solution.py:467
  319.4 28.4 %feed.2 = (bf16[1024,3072]{1,0:T(8,128)(2,1)}, bf16[1024,3072]{1,0:T(8,128)(2,1)}, f32[1024,768]{1,0:T(8,128)}, f32[1024,768]{1,0:T(8,128)}) custom-call(bf16[1024,768]{1,0:T(8,128)(2,1)S(1)} %fusion.13.in_ref.values_ref, bf16[1024,768]{1,0:T(8,128)(2,1)S(1)} %fusion.9.grad_ref.values_ref, bf16[3072,768]{1,0:T(8,128)(2,1)} %all-gather.10.cloned.1.call-done.up_ref, ...), custom_call_target="tpu_custom_call" | custom-call | flops 19327352832 | bytes 28311552 | tf_op jit(solution)/shard_map/feed/pallas_call | solution.py:412
  347.9 9.8 %convolution_convert_fusion.2 = bf16[3072,768]{1,0:T(8,128)(2,1)} fusion(bf16[1024,3072]{1,0:T(8,128)(2,1)} %get-tuple-element.32, bf16[1024,768]{1,0:T(8,128)(2,1)S(1)} %fusion.13.in_ref.values_ref), kind=kOutput, calls=%fused_computation.10 | convolution fusion | flops 4834197504 | bytes 12582912 | tf_op jit(solution)/shard_map/tf,td->fd/dot_general | solution.py:26
  359.8 9.8 %convolution_convert_fusion.1 = bf16[768,3072]{1,0:T(8,128)(2,1)} fusion(bf16[1024,768]{1,0:T(8,128)(2,1)S(1)} %fusion.9.grad_ref.values_ref, bf16[1024,3072]{1,0:T(8,128)(2,1)} %get-tuple-element.33), kind=kOutput, calls=%fused_computation.9 | convolution fusion | flops 4834197504 | bytes 12582912 | tf_op jit(solution)/shard_map/td,tf->df/dot_general | solution.py:26
  371.0 41.1 %collective-permute-done.7 = bf16[1536,768]{1,0:T(8,128)(2,1)} collective-permute-done((bf16[1536,768]{1,0:T(8,128)(2,1)}, bf16[1536,768]{1,0:T(8,128)(2,1)}, u32[]{:S(2)}, u32[]{:S(2)}) %collective-permute-start.7) | collective-permute-done | bytes 2359328 | tf_op jit(solution)/shard_map/ppermute | solution.py:434
  418.3 43.9 %collective-permute-done.6 = bf16[384,3072]{1,0:T(8,128)(2,1)} collective-permute-done((bf16[384,3072]{1,0:T(8,128)(2,1)}, bf16[384,3072]{1,0:T(8,128)(2,1)}, u32[]{:S(2)}, u32[]{:S(2)}) %collective-permute-start.6) | collective-permute-done | bytes 2359328 | tf_op jit(solution)/shard_map/ppermute | solution.py:434
  471.2 76.3 %feed.3 = (bf16[4096,3072]{1,0:T(8,128)(2,1)}, bf16[4096,3072]{1,0:T(8,128)(2,1)}, bf16[4096,768]{1,0:T(8,128)(2,1)}) custom-call(bf16[4096,768]{1,0:T(8,128)(2,1)} %bitcast.16.in_ref, bf16[4096,768]{1,0:T(8,128)(2,1)} %bitcast.19.grad_ref, bf16[768,3072]{1,0:T(8,128)(2,1)S(1)} %copy-done, bf16[3072,768]{1,0:T(8,128)(2,1)} %maximum_select_fusion.1.down_ref), custom_call_target="tpu_custom_call" | custom-call | flops 57982058496 | bytes 84934656 | tf_op jit(solution)/shard_map/feed/pallas_call | solution.py:412
  547.5 21.5 %all-to-all-start.4 = ((bf16[16,256,768]{2,1,0:T(8,128)(2,1)}), bf16[16,256,768]{2,1,0:T(8,128)(2,1)}, u32[]{:S(2)}, u32[]{:S(2)}) async-start(bf16[16,256,768]{2,1,0:T(8,128)(2,1)} %bitcast.169), calls=%async_computation.4 | async-start | bytes 12582912 | tf_op jit(solution)/shard_map/all_to_all | solution.py:467
  582.9 25.8 %fusion.53 = f32[3072,768]{1,0:T(8,128)S(1)} fusion(bf16[4096,3072]{1,0:T(8,128)(2,1)} %get-tuple-element.24, bf16[4096,768]{1,0:T(8,128)(2,1)} %bitcast.19.grad_ref), kind=kOutput, calls=%fused_computation.147 | convolution fusion | flops 19327352832 | bytes 40894464 | tf_op jit(solution)/shard_map/rf,rd->fd/dot_general | solution.py:26
  611.9 28.0 %fusion.52 = f32[768,3072]{1,0:T(8,128)S(1)} fusion(bf16[4096,768]{1,0:T(8,128)(2,1)} %bitcast.16.in_ref, bf16[4096,3072]{1,0:T(8,128)(2,1)} %get-tuple-element.34), kind=kOutput, calls=%fused_computation.146 | convolution fusion | flops 19327352832 | bytes 40894464 | tf_op jit(solution)/shard_map/rd,rf->df/dot_general | solution.py:26
  645.9 24.6 %convolution_convert_fusion = bf16[4096,768]{1,0:T(8,128)(2,1)} fusion(bf16[4096,3072]{1,0:T(8,128)(2,1)} %get-tuple-element.24, bf16[3072,768]{1,0:T(8,128)(2,1)S(1)} %bitcast.171), kind=kOutput, calls=%fused_computation.4 | convolution fusion | flops 19330498560 | bytes 36175872 | tf_op jit(solution)/shard_map/rf,fd->rd/dot_general | solution.py:26
  670.5 12.7 %all-to-all-done.4 = bf16[16,256,768]{2,1,0:T(8,128)(2,1)} async-done(((bf16[16,256,768]{2,1,0:T(8,128)(2,1)}), bf16[16,256,768]{2,1,0:T(8,128)(2,1)}, u32[]{:S(2)}, u32[]{:S(2)}) %all-to-all-start.4) | async-done | bytes 6291488 | tf_op jit(solution)/shard_map/all_to_all | solution.py:467
  683.2 28.2 %all-to-all-start.3 = ((bf16[16,256,768]{2,1,0:T(8,128)(2,1)}), bf16[16,256,768]{2,1,0:T(8,128)(2,1)}, u32[]{:S(2)}, u32[]{:S(2)}) async-start(bf16[16,256,768]{2,1,0:T(8,128)(2,1)} %bitcast.168), calls=%async_computation.3 | async-start | bytes 12582912 | tf_op jit(solution)/shard_map/all_to_all | solution.py:467
  711.5 10.5 %combine.3 = f32[1024,768]{1,0:T(8,128)S(1)} custom-call(s32[1024,16]{1,0:T(8,128)S(1)} %copy-done.4, bf16[4096,768]{1,0:T(8,128)(2,1)} %bitcast.25.rows_ref), custom_call_target="tpu_custom_call" | custom-call | flops 6442450944 | bytes 9437184 | tf_op jit(solution)/shard_map/combine/pallas_call | solution.py:354
  733.6 119.9 %attention_backward.1 = (bf16[1024,768]{1,0:T(8,128)(2,1)S(1)}, bf16[2048,768]{1,0:T(8,128)(2,1)}, bf16[2048,768]{1,0:T(8,128)(2,1)}) custom-call(s32[4]{0:T(128)S(1)} %get-tuple-element.54.low_ref, s32[4]{0:T(128)S(1)} %get-tuple-element.53.high_ref, bf16[1024,768]{1,0:T(8,128)(2,1)S(1)} %copy-done.6, bf16[2048,768]{1,0:T(8,128)(2,1)} %convolution_convert_fusion.4.k_ref, ...), custom_call_target="tpu_custom_call" | custom-call | flops 64424509440 | bytes 20447232 | tf_op jit(solution)/shard_map/attention_backward/pallas_call | solution.py:257
  883.9 11.4 %combine.2 = f32[1024,768]{1,0:T(8,128)S(1)} custom-call(s32[1024,16]{1,0:T(8,128)S(1)} %copy-done.4, f32[1024,16]{1,0:T(8,128)S(1)} %copy.65.scale_ref, bf16[4096,768]{1,0:T(8,128)(2,1)} %bitcast.23.rows_ref), custom_call_target="tpu_custom_call" | custom-call | flops 6442450944 | bytes 9437184 | tf_op jit(solution)/shard_map/combine/pallas_call | solution.py:354
  908.0 9.2 all-to-all-start.5
  931.7 12.4 %reduce-scatter.5.cloned.1.call-done = bf16[144,768]{1,0:T(8,128)(2,1)} async-done(((bf16[2304,768]{1,0:T(8,128)(2,1)}), bf16[144,768]{1,0:T(8,128)(2,1)}) %reduce-scatter.5.cloned.1.call-update) | async-done | bytes 221200 | tf_op jit(solution)/shard_map/reduce_scatter | solution.py:477
  (272 shorter events, 203.3 us)
Async XLA Ops:
  7.2 180.4 %all-gather.6.cloned.1.call-start = ((), (), s32[]{:S(2)}) async-start(), calls=%async_computation.10 | async-start | bytes 3760128 | tf_op jit(solution)/shard_map/all_gather | solution.py:473
  15.2 234.4 %all-gather.8.cloned.1.call-start = ((), (), s32[]{:S(2)}) async-start(), calls=%async_computation.11 | async-start | bytes 1253376 | tf_op jit(solution)/shard_map/all_gather | solution.py:473
  21.0 298.4 %all-gather.10.cloned.1.call-start = ((), (), s32[]{:S(2)}) async-start(), calls=%async_computation.12 | async-start | bytes 5013504 | tf_op jit(solution)/shard_map/all_gather | solution.py:473
  28.3 69.0 %collective-permute-start = (bf16[384,288]{0,1:T(8,128)(2,1)}, bf16[384,288]{0,1:T(8,128)(2,1)S(1)}, u32[]{:S(2)}, u32[]{:S(2)}) collective-permute-start(bf16[384,288]{0,1:T(8,128)(2,1)} %param.15), channel_id=1, source_target_pairs={{0,1},{1,0},{2,3},{3,2},{4,5},{5,4},{6,7},{7,6},{8,9},{9,8},{10,11... | collective-permute-start | bytes 663560 | tf_op jit(solution)/shard_map/ppermute | solution.py:434
  98.4 12.5 %all-to-all-start = ((f32[16,8,288]{2,1,0:T(8,128)}), f32[16,8,288]{2,1,0:T(8,128)S(1)}, u32[]{:S(2)}, u32[]{:S(2)}) async-start(f32[16,8,288]{2,1,0:T(8,128)} %convolution_bitcast_fusion), calls=%async_computation | async-start | bytes 393216 | tf_op jit(solution)/shard_map/all_to_all | solution.py:517
  124.9 147.4 %all-to-all-start.2 = ((bf16[16,256,768]{2,1,0:T(8,128)(2,1)}), bf16[16,256,768]{2,1,0:T(8,128)(2,1)}, u32[]{:S(2)}, u32[]{:S(2)}) async-start(bf16[16,256,768]{2,1,0:T(8,128)(2,1)} %bitcast.167), calls=%async_computation.2 | async-start | bytes 12582912 | tf_op jit(solution)/shard_map/all_to_all | solution.py:467
  129.7 189.7 %all-gather.12.cloned.1.call-start = ((), (), s32[]{:S(2)}) async-start(), calls=%async_computation.13 | async-start | bytes 5013504 | tf_op jit(solution)/shard_map/all_gather | solution.py:473
  138.0 36.0 %collective-permute-start.1 = (bf16[1024,768]{1,0:T(8,128)(2,1)S(1)}, bf16[1024,768]{1,0:T(8,128)(2,1)}, u32[]{:S(2)}, u32[]{:S(2)}) collective-permute-start(bf16[1024,768]{1,0:T(8,128)(2,1)S(1)} %copy-done.10), channel_id=1, source_target_pairs={{0,1},{1,0},{2,3},{3,2},{4,5},{5,4},{6,7},{7,6},{8,9},{9,8},{10,11... | collective-permute-start | bytes 4718600 | tf_op jit(solution)/shard_map/ppermute | solution.py:434
  272.2 196.6 %all-to-all-start.1 = ((bf16[16,256,768]{2,1,0:T(8,128)(2,1)}), bf16[16,256,768]{2,1,0:T(8,128)(2,1)}, u32[]{:S(2)}, u32[]{:S(2)}) async-start(bf16[16,256,768]{2,1,0:T(8,128)(2,1)} %bitcast.166), calls=%async_computation.1 | async-start | bytes 12582912 | tf_op jit(solution)/shard_map/all_to_all | solution.py:467
  319.3 251.5 %reduce-scatter.9.cloned.1.call-start = ((), (), s32[]{:S(2)}) async-start(), calls=%async_computation.16 | async-start | bytes 5013504 | tf_op jit(solution)/shard_map/reduce_scatter | solution.py:477
  357.6 215.8 %reduce-scatter.11.cloned.1.call-start = ((), (), s32[]{:S(2)}) async-start(), calls=%async_computation.17 | async-start | bytes 5013504 | tf_op jit(solution)/shard_map/reduce_scatter | solution.py:477
  357.7 54.5 %collective-permute-start.7 = (bf16[1536,768]{1,0:T(8,128)(2,1)}, bf16[1536,768]{1,0:T(8,128)(2,1)}, u32[]{:S(2)}, u32[]{:S(2)}) collective-permute-start(bf16[1536,768]{1,0:T(8,128)(2,1)} %bitcast.172), channel_id=1, source_target_pairs={{0,1},{1,0},{2,3},{3,2},{4,5},{5,4},{6,7},{7,6},{8,9},{9,8},{10,11... | collective-permute-start | bytes 7077896 | tf_op jit(solution)/shard_map/ppermute | solution.py:434
  359.4 102.7 %collective-permute-start.6 = (bf16[384,3072]{1,0:T(8,128)(2,1)}, bf16[384,3072]{1,0:T(8,128)(2,1)}, u32[]{:S(2)}, u32[]{:S(2)}) collective-permute-start(bf16[384,3072]{1,0:T(8,128)(2,1)} %bitcast.174), channel_id=1, source_target_pairs={{0,1},{1,0},{2,3},{3,2},{4,5},{5,4},{6,7},{7,6},{8,9},{9,8},{10,11... | collective-permute-start | bytes 7077896 | tf_op jit(solution)/shard_map/ppermute | solution.py:434
  547.5 135.7 %all-to-all-start.4 = ((bf16[16,256,768]{2,1,0:T(8,128)(2,1)}), bf16[16,256,768]{2,1,0:T(8,128)(2,1)}, u32[]{:S(2)}, u32[]{:S(2)}) async-start(bf16[16,256,768]{2,1,0:T(8,128)(2,1)} %bitcast.169), calls=%async_computation.4 | async-start | bytes 12582912 | tf_op jit(solution)/shard_map/all_to_all | solution.py:467
  571.7 6.7 collective-permute-start.11
  574.3 6.9 collective-permute-start.12
  610.3 261.4 %collective-permute-start.14 = (bf16[1536,768]{1,0:T(8,128)(2,1)}, bf16[1536,768]{1,0:T(8,128)(2,1)}, u32[]{:S(2)}, u32[]{:S(2)}) collective-permute-start(bf16[1536,768]{1,0:T(8,128)(2,1)} %dynamic-slice_convert_fusion), channel_id=1, source_target_pairs={{0,1},{1,0},{2,3},{3,2},{4,5},{5,4},{6,7},{7,6},{8,9},{9,8},{10,11... | collective-permute-start | bytes 7077896 | tf_op jit(solution)/shard_map/ppermute | solution.py:434
  644.3 233.3 %collective-permute-start.13 = (bf16[384,3072]{1,0:T(8,128)(2,1)}, bf16[384,3072]{1,0:T(8,128)(2,1)}, u32[]{:S(2)}, u32[]{:S(2)}) collective-permute-start(bf16[384,3072]{1,0:T(8,128)(2,1)} %dynamic-slice_convert_fusion.1), channel_id=1, source_target_pairs={{0,1},{1,0},{2,3},{3,2},{4,5},{5,4},{6,7},{7,6},{8,9},{9,8},{10,11... | collective-permute-start | bytes 7077896 | tf_op jit(solution)/shard_map/ppermute | solution.py:434
  683.2 200.7 %all-to-all-start.3 = ((bf16[16,256,768]{2,1,0:T(8,128)(2,1)}), bf16[16,256,768]{2,1,0:T(8,128)(2,1)}, u32[]{:S(2)}, u32[]{:S(2)}) async-start(bf16[16,256,768]{2,1,0:T(8,128)(2,1)} %bitcast.168), calls=%async_computation.3 | async-start | bytes 12582912 | tf_op jit(solution)/shard_map/all_to_all | solution.py:467
  711.4 219.4 %reduce-scatter.7.cloned.1.call-start = ((), (), s32[]{:S(2)}) async-start(), calls=%async_computation.15 | async-start | bytes 1253376 | tf_op jit(solution)/shard_map/reduce_scatter | solution.py:477
  730.7 213.4 %reduce-scatter.5.cloned.1.call-start = ((), (), s32[]{:S(2)}) async-start(), calls=%async_computation.14 | async-start | bytes 3760128 | tf_op jit(solution)/shard_map/reduce_scatter | solution.py:477
  864.8 30.6 %collective-permute-start.8 = (bf16[1024,768]{1,0:T(8,128)(2,1)}, bf16[1024,768]{1,0:T(8,128)(2,1)}, u32[]{:S(2)}, u32[]{:S(2)}) collective-permute-start(bf16[1024,768]{1,0:T(8,128)(2,1)} %dynamic-slice_convert_fusion.2), channel_id=1, source_target_pairs={{0,1},{1,0},{2,3},{3,2},{4,5},{5,4},{6,7},{7,6},{8,9},{9,8},{10,11... | collective-permute-start | bytes 4718600 | tf_op jit(solution)/shard_map/ppermute | solution.py:434
  908.0 17.0 %all-to-all-start.5 = ((bf16[16,4,288]{2,1,0:T(4,128)(2,1)}), bf16[16,4,288]{2,1,0:T(4,128)(2,1)S(1)}, u32[]{:S(2)}, u32[]{:S(2)}) async-start(bf16[16,4,288]{2,1,0:T(4,128)(2,1)} %copy.67), calls=%async_computation.5 | async-start | bytes 98304 | tf_op jit(solution)/shard_map/all_to_all | solution.py:618
  931.6 15.0 %collective-permute-start.10 = (bf16[48,384]{1,0:T(8,128)(2,1)S(1)}, bf16[48,384]{1,0:T(8,128)(2,1)S(1)}, u32[]{:S(2)}, u32[]{:S(2)}) collective-permute-start(bf16[48,384]{1,0:T(8,128)(2,1)S(1)} %constant_dynamic-slice_fusion.5), channel_id=1, source_target_pairs={{0,1},{1,0},{2,3},{3,2},{4,5},{5,4},{6,7},{7,6},{8,9},{9,8},{10,11... | collective-permute-start | bytes 110600 | tf_op jit(solution)/shard_map/ppermute | solution.py:434
  (64 other events, 1110.6 us)
Sparse Core Ops, SparseCore 0:
  15.4 48.9 all-gather.5
  67.2 37.3 all-gather.7
  107.5 91.0 all-gather.9
  201.3 103.9 all-gather.11
  357.8 118.3 reduce-scatter.8
  480.3 84.4 reduce-scatter.10
  730.8 102.5 reduce-scatter.6
  871.9 72.1 reduce-scatter.4

commit v2 on v1

--- a/solution.py
+++ b/solution.py
@@ -11,6 +11,13 @@
 IMG_SHORT = 256
 EPSILON = 1e-06
 QUAD = 4
+HALVES = 2
+FORWARD_CHUNK = 512
+BACKWARD_CHUNK = 1024
+FEED_ROWS = 512
+FEED_TILE = 768
+PACK_EXPERTS = 2
+COMBINE_ROWS = 256
 F32 = jnp.float32
 BF16 = jnp.bfloat16
 NN = (((1,), (0,)), ((), ()))
@@ -49,35 +56,34 @@
     return jnp.where(place == which, values, jnp.zeros_like(values))
 
 
-def over_blocks(low, high, all_blocks, step, state):
+def over_keys(low, high, key_rows, chunk, step, state):
     def unrolled():
         inner = state
-        for block in range(all_blocks):
-            inner = step(block, inner)
+        for start in range(0, key_rows, chunk):
+            inner = step(start, chunk, inner)
         return inner
 
-    def several(count):
-        def body(index, inner):
-            for extra in range(count):
-                inner = step(low + index * count + extra, inner)
-            return inner
-
-        return body
-
     def looped():
-        groups = (high - low) // 4
-        inner = lax.fori_loop(0, groups, several(4), state)
-        return lax.fori_loop(low + groups * 4, high, step, inner)
-
-    return lax.cond(high - low == all_blocks, unrolled, looped)
-
-
-def at_block(block, size):
-    return block * size if isinstance(block, int) else pl.multiple_of(block * size, size)
+        first, inner = low, state
+        for count in (4, 2, 1):
+            size = count * IMG_SHORT
+            if size > key_rows:
+                continue
+            turns = (high - first) // count
+
+            def body(index, inner, first=first, count=count, size=size):
+                start = (first + index * count) * IMG_SHORT
+                return step(pl.multiple_of(start, IMG_SHORT), size, inner)
+
+            inner = lax.fori_loop(0, turns, body, inner)
+            first = first + turns * count
+        return inner
+
+    return lax.cond((high - low) * IMG_SHORT == key_rows, unrolled, looped)
 
 
 def forward_kernel(
-    head_dim, size, low_ref, high_ref, q_ref, k_ref, v_ref, out_ref, exact_ref, total_ref, vt, kept
+    head_dim, low_ref, high_ref, q_ref, k_ref, v_ref, out_ref, exact_ref, total_ref, vt, kept
 ):
     row_block = pl.program_id(1)
 
@@ -89,10 +95,9 @@
     rows = q_ref.shape[0]
     by_head = [of_head(queries, h, 0, head_dim) for h in range(QUAD)]
     low, high = low_ref[row_block], high_ref[row_block]
-    blocks = k_ref.shape[0] // size
-
-    def score_step(block, tops):
-        at = at_block(block, size)
+    key_rows = k_ref.shape[0]
+
+    def score_step(at, size, tops):
         keys = k_ref[pl.ds(at, size), :]
         fresh = []
         for h in range(QUAD):
@@ -103,13 +108,13 @@
             )
         return tuple(fresh)
 
-    tops = over_blocks(
-        low, high, blocks, score_step, tuple(jnp.full((8, rows), -1e30, F32) for _ in range(QUAD))
+    chunk = min(FORWARD_CHUNK, key_rows)
+    tops = over_keys(
+        low, high, key_rows, chunk, score_step, tuple(jnp.full((8, rows), -1e30, F32) for _ in range(QUAD))
     )
     tops = [jnp.max(t, axis=0, keepdims=True) for t in tops]
 
-    def mix_step(block, state):
-        at = at_block(block, size)
+    def mix_step(at, size, state):
         fresh = []
         for h in range(QUAD):
             total, mixed = state[h]
@@ -119,10 +124,11 @@
             fresh.append((total, mixed + dot(values, weights.astype(BF16))))
         return tuple(fresh)
 
-    state = over_blocks(
+    state = over_keys(
         low,
         high,
-        blocks,
+        key_rows,
+        chunk,
         mix_step,
         tuple((jnp.zeros((8, rows), F32), jnp.zeros((head_dim, rows), F32)) for _ in range(QUAD)),
     )
@@ -145,7 +151,7 @@
     row_spec = pl.BlockSpec((size, lanes), lambda j, i, *_: (i, j))
     key_spec = pl.BlockSpec((key_rows, lanes), lambda j, i, *_: (0, j))
     return pl.pallas_call(
-        functools.partial(forward_kernel, head_dim, size),
+        functools.partial(forward_kernel, head_dim),
         grid_spec=pltpu.PrefetchScalarGridSpec(
             num_scalar_prefetch=2,
             grid=(quads, rows // size),
@@ -177,7 +183,6 @@
 
 def backward_kernel(
     head_dim,
-    size,
     low_ref,
     high_ref,
     q_ref,
@@ -217,10 +222,9 @@
     g_rows = jnp.concatenate([of_head(grads, h, 1, head_dim) for h in heads], axis=0)
     totals = [total_ref[0, h : h + 1, :] for h in heads]
     low, high = low_ref[row_block], high_ref[row_block]
-    blocks = k_ref.shape[0] // size
-
-    def step(block, dq):
-        at = at_block(block, size)
+    key_rows = k_ref.shape[0]
+
+    def step(at, size, dq):
         keys = k_ref[pl.ds(at, size), :]
         values = v_ref[pl.ds(at, size), :]
         weights, score_grads, fresh = [], [], []
@@ -235,8 +239,9 @@
         dk_sum[pl.ds(at, size), :] += dot(jnp.concatenate(score_grads, axis=1), q_rows)
         return tuple(fresh)
 
-    dq = over_blocks(
-        low, high, blocks, step, tuple(jnp.zeros((head_dim, rows), F32) for _ in heads)
+    chunk = min(BACKWARD_CHUNK, key_rows)
+    dq = over_keys(
+        low, high, key_rows, chunk, step, tuple(jnp.zeros((head_dim, rows), F32) for _ in heads)
     )
     dq_ref[...] = (jnp.concatenate(dq, axis=0) * scale).T.astype(BF16)
 
@@ -255,7 +260,7 @@
     row_spec = pl.BlockSpec((size, lanes), lambda j, i, *_: (i, j))
     key_spec = pl.BlockSpec((key_rows, lanes), lambda j, i, *_: (0, j))
     return pl.pallas_call(
-        functools.partial(backward_kernel, head_dim, size),
+        functools.partial(backward_kernel, head_dim),
         grid_spec=pltpu.PrefetchScalarGridSpec(
             num_scalar_prefetch=2,
             grid=(quads, rows // size),
@@ -289,35 +294,47 @@
     )(low, high, queries, keys, values, grads, exact, totals)
 
 
-def pack_kernel(place_ref, scale_ref, values_ref, out_ref):
-    expert = pl.program_id(0)
-    capacity = out_ref.shape[0]
-    places = place_ref[pl.ds(expert, 1), :]
-    slots = lax.broadcasted_iota(jnp.int32, (capacity, places.shape[1]), 0)
-    chosen = slots == places
-    rows = dot(chosen.astype(BF16), values_ref[...])
+def pack_kernel(count, place_ref, scale_ref, values_ref, *outs):
+    half = outs[0].shape[0] // count
+    capacity = half * len(outs)
+    picks, scales = [], []
+    for index in range(count):
+        expert = pl.program_id(0) * count + index
+        places = place_ref[pl.ds(expert, 1), :]
+        slots = lax.broadcasted_iota(jnp.int32, (capacity, places.shape[1]), 0)
+        chosen = slots == places
+        picks.append(chosen.astype(BF16))
+        if scale_ref is not None:
+            scale = jnp.where(chosen, scale_ref[pl.ds(expert, 1), :], 0.0)
+            scales.append(jnp.sum(scale, axis=1, keepdims=True))
+    rows = dot(jnp.concatenate(picks, axis=0), values_ref[...])
     if scale_ref is not None:
-        scales = jnp.where(chosen, scale_ref[pl.ds(expert, 1), :], 0.0)
-        rows = rows * jnp.sum(scales, axis=1, keepdims=True)
-    out_ref[...] = rows.astype(BF16)
+        rows = rows * jnp.concatenate(scales, axis=0)
+    for index in range(count):
+        for which, out_ref in enumerate(outs):
+            start = index * capacity + which * half
+            part = rows[start : start + half]
+            out_ref[index * half : (index + 1) * half, :] = part.astype(BF16)
 
 
 def pack(places, scales, values, capacity):
     experts, rows = places.shape
     width = values.shape[1]
+    half = capacity // HALVES
     whole = lambda shape: pl.BlockSpec(shape, lambda e: (0, 0))
     operands = [places, values] if scales is None else [places, scales, values]
-    kernel = pack_kernel
+    count = min(PACK_EXPERTS, experts)
+    kernel = functools.partial(pack_kernel, count)
     if scales is None:
-        kernel = lambda place_ref, values_ref, out_ref: pack_kernel(
-            place_ref, None, values_ref, out_ref
+        kernel = lambda place_ref, values_ref, *outs: pack_kernel(
+            count, place_ref, None, values_ref, *outs
         )
     return pl.pallas_call(
         kernel,
-        grid=(experts,),
+        grid=(experts // count,),
         in_specs=[whole(o.shape) for o in operands],
-        out_specs=pl.BlockSpec((capacity, width), lambda e: (e, 0)),
-        out_shape=jax.ShapeDtypeStruct((experts * capacity, width), BF16),
+        out_specs=[pl.BlockSpec((count * half, width), lambda e: (e, 0))] * HALVES,
+        out_shape=[jax.ShapeDtypeStruct((experts * half, width), BF16)] * HALVES,
         compiler_params=pltpu.CompilerParams(vmem_limit_bytes=VMEM_BYTES),
         cost_estimate=pl.CostEstimate(
             flops=2 * experts * capacity * rows * width,
@@ -328,34 +345,37 @@
     )(*operands)
 
 
-def combine_kernel(experts, capacity, place_ref, scale_ref, rows_ref, out_ref):
+def combine_kernel(experts, capacity, place_ref, scale_ref, first_ref, second_ref, out_ref):
+    half = capacity // HALVES
     total = None
     tokens = out_ref.shape[0]
     slots = lax.broadcasted_iota(jnp.int32, (tokens, capacity), 1)
     for expert in range(experts):
         scale = 1.0 if scale_ref is None else scale_ref[:, expert : expert + 1]
         chosen = jnp.where(slots == place_ref[:, expert : expert + 1], scale, 0.0)
-        part = dot(chosen.astype(BF16), rows_ref[expert * capacity : (expert + 1) * capacity, :])
+        span = slice(expert * half, (expert + 1) * half)
+        rows = jnp.concatenate([first_ref[span, :], second_ref[span, :]], axis=0)
+        part = dot(chosen.astype(BF16), rows)
         total = part if total is None else total + part
     out_ref[...] = total
 
 
 def combine(places, scales, rows, capacity):
     tokens, experts = places.shape
-    width = rows.shape[1]
-    block = min(256, tokens)
+    width = rows[0].shape[1]
+    block = min(COMBINE_ROWS, tokens)
     part = pl.BlockSpec((block, experts), lambda i: (i, 0))
     kernel = functools.partial(combine_kernel, experts, capacity)
-    operands = [places, rows] if scales is None else [places, scales, rows]
+    operands = [places] if scales is None else [places, scales]
     if scales is None:
-        kernel = lambda place_ref, rows_ref, out_ref: combine_kernel(
-            experts, capacity, place_ref, None, rows_ref, out_ref
+        kernel = lambda place_ref, *refs: combine_kernel(
+            experts, capacity, place_ref, None, *refs
         )
     return pl.pallas_call(
         kernel,
         grid=(tokens // block,),
-        in_specs=[part] * (len(operands) - 1)
-        + [pl.BlockSpec(rows.shape, lambda i: (0, 0), pipeline_mode=pl.Buffered(1))],
+        in_specs=[part] * len(operands)
+        + [pl.BlockSpec(r.shape, lambda i: (0, 0), pipeline_mode=pl.Buffered(1)) for r in rows],
         out_specs=pl.BlockSpec((block, width), lambda i: (i, 0)),
         out_shape=jax.ShapeDtypeStruct((tokens, width), F32),
         compiler_params=pltpu.CompilerParams(vmem_limit_bytes=VMEM_BYTES),
@@ -365,7 +385,7 @@
             bytes_accessed=2 * width * (2 * tokens + experts * capacity),
         ),
         name="combine",
-    )(*operands)
+    )(*operands, *rows)
 
 
 def gelu_both(hidden):
@@ -386,7 +406,7 @@
         part = slice(start, start + tile)
         if transposed:
             hidden = dot(rows, up_ref[part, :], NT)
-            grad = dot(grads, down_ref[:, part])
+            grad = dot(grads, down_ref[start // tile])
         else:
             hidden = dot(rows, up_ref[:, part])
             grad = dot(grads, down_ref[part, :], NT)
@@ -395,22 +415,27 @@
         hid_ref[:, part] = (grad * slope).astype(BF16)
     back = dot(hid_ref[...], up_ref[...], NN if transposed else NT)
     back_ref[...] = back.astype(back_ref.dtype)
-    if with_out:
-        out[0][...] = dot(act_ref[...], down_ref[...], NT if transposed else NN).astype(
-            out[0].dtype
-        )
+    if with_out and not transposed:
+        out[0][...] = dot(act_ref[...], down_ref[...]).astype(out[0].dtype)
+    if with_out and transposed:
+        made = [
+            dot(act_ref[:, p * tile : (p + 1) * tile], down_ref[p], NT)
+            for p in range(hidden_size // tile)
+        ]
+        out[0][...] = sum(made).astype(out[0].dtype)
 
 
 def feed(rows, grads, up, down, transposed, out_dtype, with_out):
     count, width = rows.shape
     hidden_size = up.shape[0] if transposed else up.shape[1]
-    block = min(256, count)
+    block = min(FEED_ROWS, count)
     row = pl.BlockSpec((block, width), lambda i: (i, 0))
     hid = pl.BlockSpec((block, hidden_size), lambda i: (i, 0))
-    fixed = lambda a: pl.BlockSpec(a.shape, lambda i: (0, 0), pipeline_mode=pl.Buffered(1))
+    fixed = lambda a: pl.BlockSpec(a.shape, lambda i: (0,) * a.ndim, pipeline_mode=pl.Buffered(1))
+    tile = width if transposed else min(FEED_TILE, hidden_size)
     extra = 1 if with_out else 0
     return pl.pallas_call(
-        functools.partial(feed_kernel, transposed, min(512, hidden_size), with_out),
+        functools.partial(feed_kernel, transposed, tile, with_out),
         grid=(count // block,),
         in_specs=[row, row, fixed(up), fixed(down)],
         out_specs=[hid, hid, row] + [row] * extra,
@@ -434,15 +459,24 @@
     return lax.ppermute(values, "narrow", [(0, 1), (1, 0)])
 
 
-def gather_narrow(values, axis):
+def other_narrow(values):
     if lax.axis_size("narrow") != 2:
-        return lax.all_gather(values, "narrow", axis=axis, tiled=True)
-    other = swap(values)
+        return lax.all_gather(values, "narrow", axis=0, tiled=False)
+    return swap(values)
+
+
+def merge_narrow(values, other, axis):
+    if lax.axis_size("narrow") != 2:
+        return jnp.concatenate([other[i] for i in range(other.shape[0])], axis=axis)
     return jnp.where(
         lax.axis_index("narrow") == 0,
         jnp.concatenate([values, other], axis=axis),
         jnp.concatenate([other, values], axis=axis),
     )
+
+
+def gather_narrow(values, axis):
+    return merge_narrow(values, other_narrow(values), axis)
 
 
 def part_of(values, index, size, axis):
@@ -461,12 +495,37 @@
     return part_of(values, index, size, axis).astype(F32) + other.astype(F32)
 
 
+def together(*values):
+    return lax.optimization_barrier(values)
+
+
+def to_all(blocks):
+    return lax.all_to_all(blocks, "wide", split_axis=0, concat_axis=0, tiled=True)
+
+
 def exchange(rows):
     wide = lax.axis_size("wide")
     blocks = rows.reshape(wide, rows.shape[0] // wide, rows.shape[1])
-    return lax.all_to_all(blocks, "wide", split_axis=0, concat_axis=0, tiled=True).reshape(
-        rows.shape
-    )
+    return to_all(blocks).reshape(rows.shape)
+
+
+def add_narrow(values, other):
+    if lax.axis_size("narrow") != 2:
+        return reduce_narrow(values, 0)
+    own = part_of(values, lax.axis_index("narrow"), other.shape[0], 0)
+    return own.astype(F32) + other.astype(F32)
+
+
+def join_halves(first, second, experts):
+    width = first.shape[1]
+    parts = [h.reshape(experts, -1, width) for h in (first, second)]
+    return jnp.concatenate(parts, axis=1).reshape(-1, width)
+
+
+def split_halves(rows, experts):
+    width = rows.shape[1]
+    parts = jnp.split(rows.reshape(experts, -1, width), 2, axis=1)
+    return [p.reshape(-1, width) for p in parts]
 
 
 def gather_wide(values):
@@ -501,22 +560,42 @@
     group_slots = narrow * slots
     group_rows = narrow * local_rows
 
-    attention_t = gather_wide(gather_narrow(attention_weight.T, 1))
     modulation_columns = gather_narrow(modulation_weight, 0)
-    group_patches = gather_narrow(patches, 0)
-    projection_t = gather_wide(gather_narrow(projection_weight.T, 1))
-    expand_t = gather_wide(gather_narrow(expand_weight.T, 1))
-    contract_t = gather_wide(gather_narrow(contract_weight.T, 1))
-    up = gather_narrow(expert_expand[0], 0)
-    down = gather_narrow(expert_contract[0], 0)
-
-    all_conditions = lax.all_gather(conditions, ("wide", "narrow"), axis=0, tiled=True)
+    spread = jnp.broadcast_to(conditions[None], (experts, slots, width))
+    all_conditions = gather_narrow(to_all(spread)[:, None], 1).reshape(-1, width)
+    rows_shard = gather_narrow(
+        jnp.concatenate([attention_weight.T, projection_weight.T, expand_weight.T], axis=0), 1
+    )
+    contract_shard = gather_narrow(contract_weight.T, 1)
+    column_share, hidden_size = contract_shard.shape
+    half = width // narrow
+    pieces = hidden_size // width
+    contract_shard = contract_shard.reshape(column_share, pieces, width).transpose(1, 0, 2)
+    contract_shard = contract_shard.reshape(pieces * column_share, width)
+    dense_shard = jnp.concatenate([rows_shard, contract_shard], axis=0)
+    dense = gather_wide(dense_shard)
+    dense = dense.reshape(experts, -1, width)
+    expand_end = rows_shard.shape[0]
+    attention_end = attention_weight.shape[1]
+    projection_end = attention_end + column_share
+    attention_t = dense[:, :attention_end].reshape(3 * width, width)
+    projection_t = dense[:, attention_end:projection_end].reshape(width, width)
+    expand_t = dense[:, projection_end:expand_end].reshape(hidden_size, width)
+    contract_t = dense[:, expand_end:].reshape(experts, pieces, column_share, width)
+    contract_t = contract_t.transpose(1, 0, 2, 3).reshape(pieces, width, width)
+    ready_patches, all_conditions, modulation_columns = together(
+        patches, all_conditions, modulation_columns
+    )
+    group_patches = gather_narrow(ready_patches, 0)
+    ready_up, ready_down, group_patches = together(
+        expert_expand[0], expert_contract[0], group_patches
+    )
+    other_up, other_down = other_narrow(ready_up), other_narrow(ready_down)
+
     lifted = jax.nn.silu(all_conditions.astype(F32)).astype(BF16)
     columns = jnp.dot(lifted, modulation_columns, preferred_element_type=F32)
     share = columns.shape[1]
-    modulation = lax.all_to_all(
-        columns.reshape(experts, group_slots, share), "wide", split_axis=0, concat_axis=0, tiled=True
-    )
+    modulation = to_all(columns.reshape(experts, group_slots, share))
     modulation = modulation.transpose(1, 0, 2).reshape(group_slots, 6, 1, width)
     own = part_of(modulation, mine, slots, 0)
     shift_a, scale_a, gate_a, shift_b, scale_b, gate_b = [own[:, i] for i in range(6)]
@@ -533,7 +612,9 @@
 
     grad_top = cotangent.astype(F32).reshape(slots, IMG_SHORT, width)
     grad_shared = (gate_b * grad_top).astype(BF16).reshape(local_rows, width)
-    grad_arrived = exchange(pack(places_t, gates_t, grad_shared, capacity))
+    grad_packed = pack(places_t, gates_t, grad_shared, capacity)
+    grad_first, attention_t = together(grad_packed[0], attention_t)
+    grad_arrived = [exchange(grad_first)]
 
     block_start = image_start.reshape(group_slots, IMG_SHORT)[:, 0]
     own_start = part_of(block_start, mine, slots, 0)
@@ -551,29 +632,71 @@
     keys = product(group_entry, attention_t[width : 2 * width], "td,ed->te").astype(BF16)
     values = product(group_entry, attention_t[2 * width :], "td,ed->te").astype(BF16)
     mixed_heads, exact_heads, totals = attention_forward(queries, keys, values, low, high)
+    grad_last, mixed_heads, grad_arrived[0], other_down = together(
+        grad_packed[1], mixed_heads, grad_arrived[0], other_down
+    )
+    grad_arrived.append(exchange(grad_last))
     attended = product(mixed_heads, projection_t, "td,ed->te").reshape(slots, IMG_SHORT, width)
     inputs = patches.astype(F32).reshape(slots, IMG_SHORT, width)
     middle = inputs + gate_a * attended
     normed_b = normalize(middle)
     second = (normed_b * (1.0 + scale_b) + shift_b).astype(BF16).reshape(local_rows, width)
 
-    arrived = exchange(pack(places_t, None, second, capacity))
-    expert_active, grad_expert_hidden, grad_sent = feed(
-        arrived, grad_arrived, up, down, False, BF16, False
-    )
-    grad_returned = exchange(grad_sent)
-    produced = product(expert_active, down, "rf,fd->rd").astype(BF16)
-    returned = exchange(produced)
-
+    packed = list(pack(places_t, None, second, capacity))
+    packed[0], grad_arrived[1], other_up = together(packed[0], grad_arrived[1], other_up)
+    arrived = [exchange(packed[0])]
     activated, grad_hidden, grad_second, shared = feed(
         second, grad_shared, expand_t, contract_t, True, F32, True
     )
-    contract_grad_t = product(grad_shared, activated, "td,tf->df").astype(BF16)
-    expand_grad_t = product(grad_hidden, second, "tf,td->fd").astype(BF16)
-    down_grad = product(expert_active, grad_arrived, "rf,rd->fd")
-    up_grad = product(arrived, grad_expert_hidden, "rd,rf->df")
-    expert_up_grad = reduce_narrow(up_grad, 0)[None]
-    expert_down_grad = reduce_narrow(down_grad, 0)[None]
+    up = merge_narrow(expert_expand[0], other_up, 0)
+    down = merge_narrow(expert_contract[0], other_down, 0)
+    last_packed, grad_second, up, down, arrived[0] = together(
+        packed[1], grad_second, up, down, arrived[0]
+    )
+    arrived.append(exchange(last_packed))
+    fed = feed(arrived[0], grad_arrived[0], up, down, False, BF16, True)
+    grad_ready, arrived[1] = together(fed[2], arrived[1])
+    grad_returned = [exchange(grad_ready)]
+    fed_last = feed(arrived[1], grad_arrived[1], up, down, False, BF16, True)
+    grad_ready, grad_returned[0] = together(fed_last[2], grad_returned[0])
+    grad_returned.append(exchange(grad_ready))
+    expert_active, grad_expert_hidden = (fed[0], fed_last[0]), (fed[1], fed_last[1])
+    spans = [slice(i * half, (i + 1) * half) for i in range(hidden_size // half)]
+    contract_grads = [
+        product(grad_shared, activated[:, span], "td,tf->df")
+        .astype(BF16)
+        .reshape(experts, column_share, half)
+        for span in spans
+    ]
+    expand_grads = [
+        product(grad_hidden, second[:, span], "tf,td->fd").astype(BF16).reshape(experts, -1, half)
+        for span in spans[:narrow]
+    ]
+    folds = len(spans) // narrow
+    shared_grads = jnp.stack(
+        [
+            jnp.concatenate(
+                [expand_grads[i], *contract_grads[i * folds : (i + 1) * folds]], axis=1
+            )
+            for i in range(narrow)
+        ]
+    )
+    shared_grads = shared_grads.reshape(narrow, -1, half)
+    other_shared = swap(part_of(shared_grads, 1 - mine, 1, 0)) if narrow == 2 else shared_grads
+    produced = join_halves(fed[3], fed_last[3], experts)
+    down_grad = sum(product(a, g, "rf,rd->fd") for a, g in zip(expert_active, grad_arrived))
+    up_grad = sum(product(a, g, "rd,rf->df") for a, g in zip(arrived, grad_expert_hidden))
+    send_up = part_of(up_grad, 1 - mine, half, 0) if narrow == 2 else up_grad
+    send_down = part_of(down_grad, 1 - mine, hidden_size // 2, 0) if narrow == 2 else down_grad
+    *grad_returned, send_up, send_down, produced, other_shared = together(
+        *grad_returned, send_up.astype(BF16), send_down.astype(BF16), produced, other_shared
+    )
+    returned = produced
+    returned = exchange(returned)
+
+    shared_sum = reduce_wide(add_narrow(shared_grads, other_shared)[0].astype(BF16))
+    other_up_grad = swap(send_up) if narrow == 2 else send_up
+    other_down_grad = swap(send_down) if narrow == 2 else send_down
 
     grad_second = grad_second + combine(places, None, grad_returned, capacity)
     grad_second = grad_second.reshape(slots, IMG_SHORT, width)
@@ -588,11 +711,25 @@
         queries, keys, values, grad_mixed, exact_heads, totals, low, high
     )
 
+    returned = together(returned, grad_queries)[0]
+    other_up_grad, other_down_grad, grad_queries, grad_keys, grad_values = together(
+        other_up_grad, other_down_grad, grad_queries, grad_keys, grad_values
+    )
+    expert_up_grad = add_narrow(up_grad, other_up_grad)[None]
+    expert_down_grad = add_narrow(down_grad, other_down_grad)[None]
+    returned = split_halves(returned, experts)
     mixture = shared + combine(places, gates, returned, capacity)
     mixture = mixture.reshape(slots, IMG_SHORT, width)
-    block_out = (middle + gate_b * mixture).reshape(local_rows, width).astype(BF16)
-    grad_gate_b = jnp.sum(grad_top * mixture, axis=1)
-
+    grad_group = product(grad_keys, attention_t[width : 2 * width], "te,ed->td") + product(
+        grad_values, attention_t[2 * width :], "te,ed->td"
+    )
+    grad_own = product(grad_queries, query_t, "te,ed->td")
+    if narrow == 2:
+        other_entry = swap(part_of(grad_group, 1 - mine, local_rows, 0).astype(BF16))
+        other_entry, mixture = together(other_entry, mixture)
+        grad_entry = add_narrow(grad_group, other_entry) + grad_own
+    else:
+        grad_entry = reduce_narrow(grad_group, 0) + grad_own
     attention_grad_t = jnp.concatenate(
         [
             product(grad_queries, first_entry, "te,td->ed").astype(BF16),
@@ -601,10 +738,8 @@
         ],
         axis=0,
     )
-    grad_group = product(grad_keys, attention_t[width : 2 * width], "te,ed->td") + product(
-        grad_values, attention_t[2 * width :], "te,ed->td"
-    )
-    grad_entry = reduce_narrow(grad_group, 0) + product(grad_queries, query_t, "te,ed->td")
+    block_out = (middle + gate_b * mixture).reshape(local_rows, width).astype(BF16)
+    grad_gate_b = jnp.sum(grad_top * mixture, axis=1)
     grad_entry = grad_entry.reshape(slots, IMG_SHORT, width)
     grad_shift_a = jnp.sum(grad_entry, axis=1)
     grad_scale_a = jnp.sum(grad_entry * normalize(inputs), axis=1)
@@ -615,20 +750,31 @@
         [grad_shift_a, grad_scale_a, grad_gate_a, grad_shift_b, grad_scale_b, grad_gate_b], axis=1
     )
     grad_modulation = grad_modulation.reshape(slots, experts, share).astype(BF16)
-    grad_modulation = lax.all_to_all(
-        grad_modulation.transpose(1, 0, 2), "wide", split_axis=0, concat_axis=0, tiled=True
-    )
-    grad_modulation = lax.all_gather(grad_modulation, "narrow", axis=1, tiled=True)
+    grad_modulation = gather_narrow(to_all(grad_modulation.transpose(1, 0, 2))[:, None], 1)
     row_share = width // narrow
     modulation_grad = product(
         part_of(lifted, mine, row_share, 1),
         grad_modulation.reshape(experts * group_slots, share),
         "sd,se->de",
     )
-    expand_grad = reduce_narrow(reduce_wide(expand_grad_t), 1).T
-    contract_grad = reduce_narrow(reduce_wide(contract_grad_t), 1).T
-    projection_grad = reduce_narrow(reduce_wide(projection_grad_t), 1).T
-    attention_grad = reduce_narrow(reduce_wide(attention_grad_t), 1).T
+    expand_share = expand_weight.shape[1]
+    expand_share = expand_weight.shape[1]
+    expand_grad = shared_sum[:expand_share].astype(F32).T
+    contract_grad = shared_sum[expand_share:].astype(F32).reshape(folds, column_share, half)
+    contract_grad = contract_grad.transpose(0, 2, 1).reshape(folds * half, column_share)
+    late_grads = jnp.concatenate(
+        [
+            attention_grad_t.reshape(experts, attention_end, width),
+            projection_grad_t.reshape(experts, column_share, width),
+        ],
+        axis=1,
+    )
+    late_sum = reduce_wide(late_grads.reshape(-1, width))
+    late_sum, block_out, patch_grad, modulation_grad, expand_grad, contract_grad = together(
+        late_sum, block_out, patch_grad, modulation_grad, expand_grad, contract_grad
+    )
+    late_sum = reduce_narrow(late_sum, 1).T
+    attention_grad, projection_grad = late_sum[:, :attention_end], late_sum[:, attention_end:]
     return (
         block_out,
         patch_grad,

time: 963 us -> 859 us (0.89)
  blocking collectives: 70.8 us -> 0 us
  Pallas kernels: 321 us -> 283 us
  local copies, waits for them, and re-layouts: 25.4 us -> 57.2 us
  waiting for transfers between devices: 174 us -> 154 us
  starting transfers between devices: 136 us -> 122 us
  other arithmetic: 75.2 us -> 86.3 us
    ppermute x15 -> x13, waiting for transfers between devices: 137 us -> 53.6 us  [swap(): return lax.ppermute(values, 'narrow', [(0, 1), (1, 0)])]
    all_gather x2 -> x0, blocking collectives: 70.8 us -> none  [the longest x1 66 us: on_device(): lax.all_gather(conditions, ('wide', 'narrow'), axis=0, tiled=True)]
    all_gather x4 -> x1, waiting for transfers between devices: 0.04 us -> 66.7 us  [gather_wide(): return lax.all_gather(values, 'wide', axis=0, tiled=True)]
    pallas_call x8 -> x9, Pallas kernels: 321 us -> 283 us  [the longest x3 131 us: feed(): pl.pallas_call(functools.partial(feed_kernel, transposed, tile, with_out)...]
    slice x0 -> x5, local copies, waits for them, and re-layouts: none -> 13.5 us  [the longest x1 6.79 us: on_device(): dense[:, expand_end:].reshape(experts, pieces, column_share, width)]
    reduce_scatter x4 -> x2, waiting for transfers between devices: 12.4 us -> 0.01 us  [reduce_wide(): return lax.psum_scatter(values, 'wide', scatter_dimension=0, tiled=True)]
    reduce_sum x0 -> x4, other arithmetic: none -> 12 us  [the longest x1 6.68 us: on_device(): grad_scale_a = jnp.sum(grad_entry * normalize(inputs), axis=1)]
    all_to_all x6 -> x10, starting transfers between devices: 114 us -> 104 us  [to_all(): lax.all_to_all(blocks, 'wide', split_axis=0, concat_axis=0, tiled=True)]
  transfers between devices with their start and end apart: 29 -> 26, of which waited for: 15 -> 13; matrix products, arithmetic and copies ran while one was open for 24% -> 30% of each run, Pallas kernels for 33% -> 33%
where the time goes in v2:
time: 859 us; the launch traced here: 853 us
  Pallas kernels  283 us (33%)
  waiting for transfers between devices  154 us (18%)
  matrix products  135 us (16%)
  starting transfers between devices  122 us (14%)
  other arithmetic  86.3 us (10%)
  local copies, waits for them, and re-layouts  57.2 us (7%)
  between operations  15.2 us (2%)
    dot_general x27, matrix products, product(): return jnp.einsum(form, left, right, preferred_element_type=F32)  133 us
    pallas_call x3, Pallas kernels, feed(): pl.pallas_call(functools.partial(feed_kernel, transposed, tile, with_out)...  131 us
    all_to_all x10, starting transfers between devices, to_all(): lax.all_to_all(blocks, 'wide', split_axis=0, concat_axis=0, tiled=True)  104 us
    pallas_call x1, Pallas kernels, attention_backward(): pl.pallas_call(functools.partial(backward_kernel, head_dim), grid_spec=pl...  72.1 us
    all_gather x1, waiting for transfers between devices, gather_wide(): return lax.all_gather(values, 'wide', axis=0, tiled=True)  66.7 us
    ppermute x13, waiting for transfers between devices, swap(): return lax.ppermute(values, 'narrow', [(0, 1), (1, 0)])  53.6 us
    pallas_call x1, Pallas kernels, attention_forward(): pl.pallas_call(functools.partial(forward_kernel, head_dim), grid_spec=plt...  39.1 us
    all_to_all x10, waiting for transfers between devices, to_all(): lax.all_to_all(blocks, 'wide', split_axis=0, concat_axis=0, tiled=True)  34 us
  transfers between devices with their start and end apart: 26, of which 13 were waited for; matrix products, arithmetic and copies ran while one was open for 30% of the time, Pallas kernels for 33%

profile of v2, /device:TPU:0, one launch (start us, length us, event | category | flops | bytes accessed | tf_op | source)
XLA Modules:
  0.0 852.7 jit_solution(5142885623281330190)
XLA Ops:
  12.4 9.1 %collective-permute-done.4 = bf16[48,1536]{1,0:T(8,128)(2,1)S(1)} collective-permute-done((bf16[48,1536]{1,0:T(8,128)(2,1)}, bf16[48,1536]{1,0:T(8,128)(2,1)S(1)}, u32[]{:S(2)}, u32[]{:S(2)}) %collective-permute-start.4) | collective-permute-done | bytes 147488 | tf_op jit(solution)/shard_map/ppermute | solution.py:459
  50.9 9.8 %all-to-all-done.1 = f32[16,8,288]{2,1,0:T(8,128)S(1)} async-done(((f32[16,8,288]{2,1,0:T(8,128)}), f32[16,8,288]{2,1,0:T(8,128)S(1)}, u32[]{:S(2)}, u32[]{:S(2)}) %all-to-all-start.1) | async-done | bytes 147488 | tf_op jit(solution)/shard_map/all_to_all | solution.py:503
  63.9 10.6 %pack.2 = (bf16[2048,768]{1,0:T(8,128)(2,1)}, bf16[2048,768]{1,0:T(8,128)(2,1)}) custom-call(s32[16,1024]{1,0:T(8,128)S(1)} %copy.75.place_ref, f32[16,1024]{1,0:T(8,128)S(1)} %bitcast.193, bf16[1024,768]{1,0:T(8,128)(2,1)S(1)} %fusion.12.values_ref.grad_ref), custom_call_target="tpu_custom_call" | custom-call | flops 6442450944 | bytes 7864320 | tf_op jit(solution)/shard_map/pack/pallas_call | solution.py:332
  74.5 66.7 %all-gather.2.cloned.1.call-done = bf16[9216,768]{1,0:T(8,128)(2,1)} async-done(((bf16[576,768]{1,0:T(8,128)(2,1)}), bf16[9216,768]{1,0:T(8,128)(2,1)}) %all-gather.2.cloned.1.call-update) | async-done | bytes 14155792 | tf_op jit(solution)/shard_map/all_gather | solution.py:532
  168.3 39.1 %attention_forward.1 = (bf16[1024,768]{1,0:T(8,128)(2,1)S(1)}, f32[1024,768]{1,0:T(8,128)}, f32[3,4,1024]{2,1,0:T(4,128)S(1)}) custom-call(s32[4]{0:T(128)S(1)} %get-tuple-element.156.low_ref, s32[4]{0:T(128)S(1)} %get-tuple-element.155.high_ref, bf16[1024,768]{1,0:T(8,128)(2,1)S(1)} %convolution_convert_fusion.5.q_ref, ...), custom_call_target="tpu_custom_call" | custom-call | flops 25769803776 | bytes 12582912 | tf_op jit(solution)/shard_map/attention_forward/pallas_call | solution.py:153
  209.6 15.8 %all-to-all-start.3 = ((bf16[16,128,768]{2,1,0:T(8,128)(2,1)}), bf16[16,128,768]{2,1,0:T(8,128)(2,1)}, u32[]{:S(2)}, u32[]{:S(2)}) async-start(bf16[16,128,768]{2,1,0:T(8,128)(2,1)} %bitcast.215), calls=%async_computation.3 | async-start | bytes 6291456 | tf_op jit(solution)/shard_map/all_to_all | solution.py:503
  237.1 8.8 %pack.3 = (bf16[2048,768]{1,0:T(8,128)(2,1)}, bf16[2048,768]{1,0:T(8,128)(2,1)}) custom-call(s32[16,1024]{1,0:T(8,128)S(1)} %copy.75.place_ref, bf16[1024,768]{1,0:T(8,128)(2,1)S(1)} %bitcast.187), custom_call_target="tpu_custom_call" | custom-call | flops 6442450944 | bytes 7864320 | tf_op jit(solution)/shard_map/pack/pallas_call | solution.py:332
  245.9 35.8 %collective-permute-done.6 = bf16[384,3072]{1,0:T(8,128)(2,1)} collective-permute-done((bf16[384,3072]{1,0:T(8,128)(2,1)}, bf16[384,3072]{1,0:T(8,128)(2,1)}, u32[]{:S(2)}, u32[]{:S(2)}) %collective-permute-start.6) | collective-permute-done | bytes 2359328 | tf_op jit(solution)/shard_map/ppermute | solution.py:459
  284.7 15.5 %all-to-all-start.4 = ((bf16[16,128,768]{2,1,0:T(8,128)(2,1)}), bf16[16,128,768]{2,1,0:T(8,128)(2,1)}, u32[]{:S(2)}, u32[]{:S(2)}) async-start(bf16[16,128,768]{2,1,0:T(8,128)(2,1)} %bitcast.32), calls=%async_computation.4 | async-start | bytes 6291456 | tf_op jit(solution)/shard_map/all_to_all | solution.py:503
  309.5 30.1 %feed.3 = (bf16[1024,3072]{1,0:T(8,128)(2,1)}, bf16[1024,3072]{1,0:T(8,128)(2,1)}, f32[1024,768]{1,0:T(8,128)}, f32[1024,768]{1,0:T(8,128)}) custom-call(bf16[1024,768]{1,0:T(8,128)(2,1)S(1)} %bitcast.188, bf16[1024,768]{1,0:T(8,128)(2,1)S(1)} %fusion.12.values_ref.grad_ref, bf16[3072,768]{1,0:T(8,128)(2,1)} %bitcast.212, bf16[4,768,768]{2,1,0:T(8,128)(2,1)} %bitcast.209), custom_call_target="tpu_custom_call" | custom-call | flops 19327352832 | bytes 28311552 | tf_op jit(solution)/shard_map/feed/pallas_call | solution.py:437
  397.3 50.4 %feed.4 = (bf16[2048,3072]{1,0:T(8,128)(2,1)}, bf16[2048,3072]{1,0:T(8,128)(2,1)}, bf16[2048,768]{1,0:T(8,128)(2,1)}, bf16[2048,768]{1,0:T(8,128)(2,1)}) custom-call(bf16[2048,768]{1,0:T(8,128)(2,1)} %bitcast.33.in_ref, bf16[2048,768]{1,0:T(8,128)(2,1)} %bitcast.21.grad_ref, bf16[768,3072]{1,0:T(8,128)(2,1)} %maximum_select_fusion.up_ref, ...), custom_call_target="tpu_custom_call" | custom-call | flops 38654705664 | bytes 47185920 | tf_op jit(solution)/shard_map/feed/pallas_call | solution.py:437
  447.7 7.6 all-to-all-start.6
  463.5 13.9 %fusion.58 = f32[768,3072]{1,0:T(8,128)} fusion(bf16[2048,768]{1,0:T(8,128)(2,1)} %bitcast.33.in_ref, bf16[2048,3072]{1,0:T(8,128)(2,1)S(1)} %copy-done.65), kind=kOutput, calls=%fused_computation.176 | convolution fusion | flops 9663676416 | bytes 25165824 | tf_op jit(solution)/shard_map/rd,rf->df/dot_general | solution.py:33
  477.4 50.2 %feed.5 = (bf16[2048,3072]{1,0:T(8,128)(2,1)}, bf16[2048,3072]{1,0:T(8,128)(2,1)}, bf16[2048,768]{1,0:T(8,128)(2,1)}, bf16[2048,768]{1,0:T(8,128)(2,1)}) custom-call(bf16[2048,768]{1,0:T(8,128)(2,1)} %bitcast.35.in_ref, bf16[2048,768]{1,0:T(8,128)(2,1)} %bitcast.31.grad_ref, bf16[768,3072]{1,0:T(8,128)(2,1)} %maximum_select_fusion.up_ref, ...), custom_call_target="tpu_custom_call" | custom-call | flops 38654705664 | bytes 47185920 | tf_op jit(solution)/shard_map/feed/pallas_call | solution.py:437
  535.5 16.8 %fusion.59 = f32[3072,768]{1,0:T(8,128)} fusion(bf16[2048,3072]{1,0:T(8,128)(2,1)} %get-tuple-element.109, bf16[2048,768]{1,0:T(8,128)(2,1)} %bitcast.31.grad_ref), kind=kOutput, calls=%fused_computation.177 | convolution fusion | flops 9663676416 | bytes 25165824 | tf_op jit(solution)/shard_map/rf,rd->fd/dot_general | solution.py:33
  555.6 16.1 %convolution_add_fusion = f32[3072,768]{1,0:T(8,128)S(1)} fusion(f32[3072,768]{1,0:T(8,128)} %fusion.59, bf16[2048,3072]{1,0:T(8,128)(2,1)} %get-tuple-element.108, bf16[2048,768]{1,0:T(8,128)(2,1)} %bitcast.21.grad_ref), kind=kOutput, calls=%fused_computation.14 | convolution fusion | flops 9666035712 | bytes 34603008 | tf_op jit(solution)/shard_map/rf,rd->fd/dot_general | solution.py:33
  573.5 19.6 %convolution_add_fusion.1 = f32[768,3072]{1,0:T(8,128)} fusion(f32[768,3072]{1,0:T(8,128)} %fusion.58, bf16[2048,768]{1,0:T(8,128)(2,1)} %bitcast.35.in_ref, bf16[2048,3072]{1,0:T(8,128)(2,1)} %get-tuple-element.107), kind=kOutput, calls=%fused_computation.15 | convolution fusion | flops 9666035712 | bytes 34603008 | tf_op jit(solution)/shard_map/rd,rf->df/dot_general | solution.py:33
  597.2 8.2 fusion.6
  605.5 13.2 %all-to-all-start.8 = ((bf16[16,256,768]{2,1,0:T(8,128)(2,1)}), bf16[16,256,768]{2,1,0:T(8,128)(2,1)}, u32[]{:S(2)}, u32[]{:S(2)}) async-start(bf16[16,256,768]{2,1,0:T(8,128)(2,1)} %pad_maximum_fusion), calls=%async_computation.9 | async-start | bytes 12582912 | tf_op jit(solution)/shard_map/all_to_all | solution.py:503
  620.9 10.6 %combine.2 = f32[1024,768]{1,0:T(8,128)S(1)} custom-call(s32[1024,16]{1,0:T(8,128)S(1)} %copy-done.3, bf16[2048,768]{1,0:T(8,128)(2,1)} %bitcast.217, bf16[2048,768]{1,0:T(8,128)(2,1)} %bitcast.39.refs_1_), custom_call_target="tpu_custom_call" | custom-call | flops 6442450944 | bytes 9437184 | tf_op jit(solution)/shard_map/combine/pallas_call | solution.py:374
  646.3 72.1 %attention_backward.1 = (bf16[1024,768]{1,0:T(8,128)(2,1)S(1)}, bf16[2048,768]{1,0:T(8,128)(2,1)}, bf16[2048,768]{1,0:T(8,128)(2,1)}) custom-call(s32[4]{0:T(128)S(1)} %copy-done.9, s32[4]{0:T(128)S(1)} %copy-done.7, bf16[1024,768]{1,0:T(8,128)(2,1)S(1)} %copy-done.11, bf16[2048,768]{1,0:T(8,128)(2,1)} %convolution_convert_fusion.3.k_ref, ...), custom_call_target="tpu_custom_call" | custom-call | flops 64424509440 | bytes 20447232 | tf_op jit(solution)/shard_map/attention_backward/pallas_call | solution.py:262
  748.8 12.6 %all-to-all-done.8 = bf16[16,256,768]{2,1,0:T(8,128)(2,1)} async-done(((bf16[16,256,768]{2,1,0:T(8,128)(2,1)}), bf16[16,256,768]{2,1,0:T(8,128)(2,1)}, u32[]{:S(2)}, u32[]{:S(2)}) %all-to-all-start.8) | async-done | bytes 6291488 | tf_op jit(solution)/shard_map/all_to_all | solution.py:503
  767.8 11.3 %combine.3 = f32[1024,768]{1,0:T(8,128)S(1)} custom-call(s32[1024,16]{1,0:T(8,128)S(1)} %copy-done.3, f32[1024,16]{1,0:T(8,128)S(1)} %copy.77.scale_ref, bf16[2048,768]{1,0:T(8,128)(2,1)} %bitcast.221, bf16[2048,768]{1,0:T(8,128)(2,1)} %bitcast.220), custom_call_target="tpu_custom_call" | custom-call | flops 6442450944 | bytes 9437184 | tf_op jit(solution)/shard_map/combine/pallas_call | solution.py:374
  798.3 25.5 %all-to-all-start.9 = ((bf16[16,4,288]{2,1,0:T(4,128)(2,1)}), bf16[16,4,288]{2,1,0:T(4,128)(2,1)S(1)}, u32[]{:S(2)}, u32[]{:S(2)}) async-start(bf16[16,4,288]{2,1,0:T(4,128)(2,1)} %copy.79), calls=%async_computation.10 | async-start | bytes 98304 | tf_op jit(solution)/shard_map/all_to_all | solution.py:503
  (319 shorter events, 268.2 us)
Async XLA Ops:
  7.2 134.0 %all-gather.2.cloned.1.call-start = ((), (), s32[]{:S(2)}) async-start(), calls=%async_computation.12 | async-start | bytes 15040512 | tf_op jit(solution)/shard_map/all_gather | solution.py:532
  8.3 13.8 %collective-permute-start.3 = (bf16[384,384]{1,0:T(8,128)(2,1)S(1)}, bf16[384,384]{1,0:T(8,128)(2,1)S(1)}, u32[]{:S(2)}, u32[]{:S(2)}) collective-permute-start(bf16[384,384]{1,0:T(8,128)(2,1)S(1)} %pad_maximum_fusion.4), channel_id=1, source_target_pairs={{0,1},{1,0},{2,3},{3,2},{4,5},{5,4},{6,7},{7,6},{8,9},{9,8},{10,11... | collective-permute-start | bytes 884744 | tf_op jit(solution)/shard_map/ppermute | solution.py:459
  11.3 10.2 %collective-permute-start.4 = (bf16[48,1536]{1,0:T(8,128)(2,1)}, bf16[48,1536]{1,0:T(8,128)(2,1)S(1)}, u32[]{:S(2)}, u32[]{:S(2)}) collective-permute-start(bf16[48,1536]{1,0:T(8,128)(2,1)} %bitcast.257), channel_id=1, source_target_pairs={{0,1},{1,0},{2,3},{3,2},{4,5},{5,4},{6,7},{7,6},{8,9},{9,8},{10,11... | collective-permute-start | bytes 442376 | tf_op jit(solution)/shard_map/ppermute | solution.py:459
  25.1 13.7 %all-to-all-start = ((bf16[16,4,768]{2,1,0:T(4,128)(2,1)}), bf16[16,4,768]{2,1,0:T(4,128)(2,1)S(1)}, u32[]{:S(2)}, u32[]{:S(2)}) async-start(bf16[16,4,768]{2,1,0:T(4,128)(2,1)} %broadcast_in_dim.27), calls=%async_computation | async-start | bytes 196608 | tf_op jit(solution)/shard_map/all_to_all | solution.py:503
  31.3 9.0 %collective-permute-start.1 = (bf16[384,288]{0,1:T(8,128)(2,1)S(1)}, bf16[384,288]{0,1:T(8,128)(2,1)S(1)}, u32[]{:S(2)}, u32[]{:S(2)}) collective-permute-start(bf16[384,288]{0,1:T(8,128)(2,1)S(1)} %copy-done.45), channel_id=1, source_target_pairs={{0,1},{1,0},{2,3},{3,2},{4,5},{5,4},{6,7},{7,6},{8,9},{9,8},{10,11... | collective-permute-start | bytes 663560 | tf_op jit(solution)/shard_map/ppermute | solution.py:459
  44.6 16.0 %all-to-all-start.1 = ((f32[16,8,288]{2,1,0:T(8,128)}), f32[16,8,288]{2,1,0:T(8,128)S(1)}, u32[]{:S(2)}, u32[]{:S(2)}) async-start(f32[16,8,288]{2,1,0:T(8,128)} %convolution_bitcast_fusion), calls=%async_computation.1 | async-start | bytes 393216 | tf_op jit(solution)/shard_map/all_to_all | solution.py:503
  49.3 101.6 %collective-permute-start.2 = (bf16[1024,768]{1,0:T(8,128)(2,1)S(1)}, bf16[1024,768]{1,0:T(8,128)(2,1)}, u32[]{:S(2)}, u32[]{:S(2)}) collective-permute-start(bf16[1024,768]{1,0:T(8,128)(2,1)S(1)} %copy-done.15), channel_id=1, source_target_pairs={{0,1},{1,0},{2,3},{3,2},{4,5},{5,4},{6,7},{7,6},{8,9},{9,8},{10,11... | collective-permute-start | bytes 4718600 | tf_op jit(solution)/shard_map/ppermute | solution.py:459
  145.3 64.3 %all-to-all-start.2 = ((bf16[16,128,768]{2,1,0:T(8,128)(2,1)}), bf16[16,128,768]{2,1,0:T(8,128)(2,1)}, u32[]{:S(2)}, u32[]{:S(2)}) async-start(bf16[16,128,768]{2,1,0:T(8,128)(2,1)} %bitcast.20), calls=%async_computation.2 | async-start | bytes 6291456 | tf_op jit(solution)/shard_map/all_to_all | solution.py:503
  153.6 53.8 %collective-permute-start.5 = (bf16[1536,768]{1,0:T(8,128)(2,1)S(1)}, bf16[1536,768]{1,0:T(8,128)(2,1)}, u32[]{:S(2)}, u32[]{:S(2)}) collective-permute-start(bf16[1536,768]{1,0:T(8,128)(2,1)S(1)} %bitcast.224), channel_id=1, source_target_pairs={{0,1},{1,0},{2,3},{3,2},{4,5},{5,4},{6,7},{7,6},{8,9},{9,8},{10,11... | collective-permute-start | bytes 7077896 | tf_op jit(solution)/shard_map/ppermute | solution.py:459
  209.6 75.2 %all-to-all-start.3 = ((bf16[16,128,768]{2,1,0:T(8,128)(2,1)}), bf16[16,128,768]{2,1,0:T(8,128)(2,1)}, u32[]{:S(2)}, u32[]{:S(2)}) async-start(bf16[16,128,768]{2,1,0:T(8,128)(2,1)} %bitcast.215), calls=%async_computation.3 | async-start | bytes 6291456 | tf_op jit(solution)/shard_map/all_to_all | solution.py:503
  227.8 54.0 %collective-permute-start.6 = (bf16[384,3072]{1,0:T(8,128)(2,1)}, bf16[384,3072]{1,0:T(8,128)(2,1)}, u32[]{:S(2)}, u32[]{:S(2)}) collective-permute-start(bf16[384,3072]{1,0:T(8,128)(2,1)} %bitcast.226), channel_id=1, source_target_pairs={{0,1},{1,0},{2,3},{3,2},{4,5},{5,4},{6,7},{7,6},{8,9},{9,8},{10,11... | collective-permute-start | bytes 7077896 | tf_op jit(solution)/shard_map/ppermute | solution.py:459
  284.7 89.5 %all-to-all-start.4 = ((bf16[16,128,768]{2,1,0:T(8,128)(2,1)}), bf16[16,128,768]{2,1,0:T(8,128)(2,1)}, u32[]{:S(2)}, u32[]{:S(2)}) async-start(bf16[16,128,768]{2,1,0:T(8,128)(2,1)} %bitcast.32), calls=%async_computation.4 | async-start | bytes 6291456 | tf_op jit(solution)/shard_map/all_to_all | solution.py:503
  374.2 73.5 %all-to-all-start.5 = ((bf16[16,128,768]{2,1,0:T(8,128)(2,1)}), bf16[16,128,768]{2,1,0:T(8,128)(2,1)}, u32[]{:S(2)}, u32[]{:S(2)}) async-start(bf16[16,128,768]{2,1,0:T(8,128)(2,1)} %bitcast.216), calls=%async_computation.5 | async-start | bytes 6291456 | tf_op jit(solution)/shard_map/all_to_all | solution.py:503
  447.7 79.9 %all-to-all-start.6 = ((bf16[16,128,768]{2,1,0:T(8,128)(2,1)}), bf16[16,128,768]{2,1,0:T(8,128)(2,1)S(1)}, u32[]{:S(2)}, u32[]{:S(2)}) async-start(bf16[16,128,768]{2,1,0:T(8,128)(2,1)} %bitcast.36), calls=%async_computation.6 | async-start | bytes 6291456 | tf_op jit(solution)/shard_map/all_to_all | solution.py:503
  462.0 135.2 %collective-permute-start.7 = (bf16[1,6144,384]{2,1,0:T(8,128)(2,1)}, bf16[1,6144,384]{2,1,0:T(8,128)(2,1)}, u32[]{:S(2)}, u32[]{:S(2)}) collective-permute-start(bf16[1,6144,384]{2,1,0:T(8,128)(2,1)} %fusion.8), channel_id=1, source_target_pairs={{0,1},{1,0},{2,3},{3,2},{4,5},{5,4},{6,7},{7,6},{8,9},{9,8},{10,11... | collective-permute-start | bytes 14155784 | tf_op jit(solution)/shard_map/ppermute | solution.py:459
  529.3 68.0 %all-to-all-start.7 = ((bf16[16,128,768]{2,1,0:T(8,128)(2,1)}), bf16[16,128,768]{2,1,0:T(8,128)(2,1)}, u32[]{:S(2)}, u32[]{:S(2)}) async-start(bf16[16,128,768]{2,1,0:T(8,128)(2,1)} %bitcast.38), calls=%async_computation.7 | async-start | bytes 6291456 | tf_op jit(solution)/shard_map/all_to_all | solution.py:503
  535.4 297.2 %reduce-scatter.5.cloned.1.call-start = ((), (), s32[]{:S(2)}) async-start(), calls=%async_computation.14 | async-start | bytes 5013504 | tf_op jit(solution)/shard_map/reduce_scatter | solution.py:536
  605.5 155.8 %all-to-all-start.8 = ((bf16[16,256,768]{2,1,0:T(8,128)(2,1)}), bf16[16,256,768]{2,1,0:T(8,128)(2,1)}, u32[]{:S(2)}, u32[]{:S(2)}) async-start(bf16[16,256,768]{2,1,0:T(8,128)(2,1)} %pad_maximum_fusion), calls=%async_computation.9 | async-start | bytes 12582912 | tf_op jit(solution)/shard_map/all_to_all | solution.py:503
  618.7 218.0 %reduce-scatter.3.cloned.1.call-start = ((), (), s32[]{:S(2)}) async-start(), calls=%async_computation.13 | async-start | bytes 5013504 | tf_op jit(solution)/shard_map/reduce_scatter | solution.py:536
  618.8 101.1 %collective-permute-start.8 = (bf16[384,3072]{1,0:T(8,128)(2,1)}, bf16[384,3072]{1,0:T(8,128)(2,1)}, u32[]{:S(2)}, u32[]{:S(2)}) collective-permute-start(bf16[384,3072]{1,0:T(8,128)(2,1)} %dynamic-slice_convert_fusion.1), channel_id=1, source_target_pairs={{0,1},{1,0},{2,3},{3,2},{4,5},{5,4},{6,7},{7,6},{8,9},{9,8},{10,11... | collective-permute-start | bytes 7077896 | tf_op jit(solution)/shard_map/ppermute | solution.py:459
  619.6 103.7 %collective-permute-start.9 = (bf16[1536,768]{1,0:T(8,128)(2,1)}, bf16[1536,768]{1,0:T(8,128)(2,1)}, u32[]{:S(2)}, u32[]{:S(2)}) collective-permute-start(bf16[1536,768]{1,0:T(8,128)(2,1)} %dynamic-slice_convert_fusion), channel_id=1, source_target_pairs={{0,1},{1,0},{2,3},{3,2},{4,5},{5,4},{6,7},{7,6},{8,9},{9,8},{10,11... | collective-permute-start | bytes 7077896 | tf_op jit(solution)/shard_map/ppermute | solution.py:459
  747.1 36.0 %collective-permute-start.10 = (bf16[1024,768]{1,0:T(8,128)(2,1)}, bf16[1024,768]{1,0:T(8,128)(2,1)}, u32[]{:S(2)}, u32[]{:S(2)}) collective-permute-start(bf16[1024,768]{1,0:T(8,128)(2,1)} %dynamic-slice_convert_fusion.2), channel_id=1, source_target_pairs={{0,1},{1,0},{2,3},{3,2},{4,5},{5,4},{6,7},{7,6},{8,9},{9,8},{10,11... | collective-permute-start | bytes 4718600 | tf_op jit(solution)/shard_map/ppermute | solution.py:459
  798.3 33.1 %all-to-all-start.9 = ((bf16[16,4,288]{2,1,0:T(4,128)(2,1)}), bf16[16,4,288]{2,1,0:T(4,128)(2,1)S(1)}, u32[]{:S(2)}, u32[]{:S(2)}) async-start(bf16[16,4,288]{2,1,0:T(4,128)(2,1)} %copy.79), calls=%async_computation.10 | async-start | bytes 98304 | tf_op jit(solution)/shard_map/all_to_all | solution.py:503
  837.7 6.9 collective-permute-start.12
  (72 other events, 884.1 us)
Sparse Core Ops, SparseCore 0:
  24.5 116.6 all-gather.1
  605.6 151.8 reduce-scatter.4
  762.4 73.8 reduce-scatter.2

commit v3 on v2

--- a/solution.py
+++ b/solution.py
@@ -475,6 +475,13 @@
     )
 
 
+def in_narrow_order(values, other):
+    if lax.axis_size("narrow") != 2:
+        return [other[i] for i in range(other.shape[0])]
+    first = lax.axis_index("narrow") == 0
+    return [jnp.where(first, values, other), jnp.where(first, other, values)]
+
+
 def gather_narrow(values, axis):
     return merge_narrow(values, other_narrow(values), axis)
 
@@ -563,26 +570,24 @@
     modulation_columns = gather_narrow(modulation_weight, 0)
     spread = jnp.broadcast_to(conditions[None], (experts, slots, width))
     all_conditions = gather_narrow(to_all(spread)[:, None], 1).reshape(-1, width)
-    rows_shard = gather_narrow(
-        jnp.concatenate([attention_weight.T, projection_weight.T, expand_weight.T], axis=0), 1
-    )
-    contract_shard = gather_narrow(contract_weight.T, 1)
-    column_share, hidden_size = contract_shard.shape
     half = width // narrow
+    attention_end, column_share = attention_weight.shape[1], projection_weight.shape[1]
+    expand_share = expand_weight.shape[1]
+    folds = contract_weight.shape[0] // half
+    hidden_size = narrow * contract_weight.shape[0]
     pieces = hidden_size // width
-    contract_shard = contract_shard.reshape(column_share, pieces, width).transpose(1, 0, 2)
-    contract_shard = contract_shard.reshape(pieces * column_share, width)
-    dense_shard = jnp.concatenate([rows_shard, contract_shard], axis=0)
-    dense = gather_wide(dense_shard)
-    dense = dense.reshape(experts, -1, width)
-    expand_end = rows_shard.shape[0]
-    attention_end = attention_weight.shape[1]
-    projection_end = attention_end + column_share
-    attention_t = dense[:, :attention_end].reshape(3 * width, width)
-    projection_t = dense[:, attention_end:projection_end].reshape(width, width)
-    expand_t = dense[:, projection_end:expand_end].reshape(hidden_size, width)
-    contract_t = dense[:, expand_end:].reshape(experts, pieces, column_share, width)
-    contract_t = contract_t.transpose(1, 0, 2, 3).reshape(pieces, width, width)
+    early_shard = gather_narrow(
+        jnp.concatenate([attention_weight.T, projection_weight.T], axis=0), 1
+    )
+    contract_shard = contract_weight.T.reshape(column_share, folds, half).transpose(1, 0, 2)
+    late_shard = jnp.concatenate([expand_weight.T, contract_shard.reshape(-1, half)], axis=1)
+    late_shards = other_narrow(late_shard)
+    late_shards = in_narrow_order(late_shard, late_shards)
+    late_both, early_shard = together(jnp.concatenate(late_shards, axis=1), early_shard)
+    early = gather_wide(early_shard).reshape(experts, -1, width)
+    late_both = gather_wide(late_both)
+    attention_t = early[:, :attention_end].reshape(3 * width, width)
+    projection_t = early[:, attention_end:].reshape(width, width)
     ready_patches, all_conditions, modulation_columns = together(
         patches, all_conditions, modulation_columns
     )
@@ -645,6 +650,13 @@
     packed = list(pack(places_t, None, second, capacity))
     packed[0], grad_arrived[1], other_up = together(packed[0], grad_arrived[1], other_up)
     arrived = [exchange(packed[0])]
+    halves = jnp.split(late_both, narrow, axis=1)
+    expand_t = jnp.concatenate([h[:, :half] for h in halves], axis=1)
+    columns = [h[:, half:].reshape(experts, folds, column_share, half) for h in halves]
+    columns = [c[:, k].reshape(width, half) for c in columns for k in range(folds)]
+    contract_t = jnp.stack(
+        [jnp.concatenate(columns[p * narrow : (p + 1) * narrow], axis=1) for p in range(pieces)]
+    )
     activated, grad_hidden, grad_second, shared = feed(
         second, grad_shared, expand_t, contract_t, True, F32, True
     )
@@ -654,13 +666,6 @@
         packed[1], grad_second, up, down, arrived[0]
     )
     arrived.append(exchange(last_packed))
-    fed = feed(arrived[0], grad_arrived[0], up, down, False, BF16, True)
-    grad_ready, arrived[1] = together(fed[2], arrived[1])
-    grad_returned = [exchange(grad_ready)]
-    fed_last = feed(arrived[1], grad_arrived[1], up, down, False, BF16, True)
-    grad_ready, grad_returned[0] = together(fed_last[2], grad_returned[0])
-    grad_returned.append(exchange(grad_ready))
-    expert_active, grad_expert_hidden = (fed[0], fed_last[0]), (fed[1], fed_last[1])
     spans = [slice(i * half, (i + 1) * half) for i in range(hidden_size // half)]
     contract_grads = [
         product(grad_shared, activated[:, span], "td,tf->df")
@@ -672,7 +677,6 @@
         product(grad_hidden, second[:, span], "tf,td->fd").astype(BF16).reshape(experts, -1, half)
         for span in spans[:narrow]
     ]
-    folds = len(spans) // narrow
     shared_grads = jnp.stack(
         [
             jnp.concatenate(
@@ -683,18 +687,28 @@
     )
     shared_grads = shared_grads.reshape(narrow, -1, half)
     other_shared = swap(part_of(shared_grads, 1 - mine, 1, 0)) if narrow == 2 else shared_grads
+    fed = feed(arrived[0], grad_arrived[0], up, down, False, BF16, True)
+    grad_ready, arrived[1] = together(fed[2], arrived[1])
+    grad_returned = [exchange(grad_ready)]
+    fed_last = feed(arrived[1], grad_arrived[1], up, down, False, BF16, True)
+    grad_ready, grad_returned[0], other_shared = together(
+        fed_last[2], grad_returned[0], other_shared
+    )
+    shared_sum = add_narrow(shared_grads, other_shared)[0].astype(BF16)
+    grad_returned.append(exchange(grad_ready))
+    expert_active, grad_expert_hidden = (fed[0], fed_last[0]), (fed[1], fed_last[1])
     produced = join_halves(fed[3], fed_last[3], experts)
     down_grad = sum(product(a, g, "rf,rd->fd") for a, g in zip(expert_active, grad_arrived))
     up_grad = sum(product(a, g, "rd,rf->df") for a, g in zip(arrived, grad_expert_hidden))
     send_up = part_of(up_grad, 1 - mine, half, 0) if narrow == 2 else up_grad
     send_down = part_of(down_grad, 1 - mine, hidden_size // 2, 0) if narrow == 2 else down_grad
-    *grad_returned, send_up, send_down, produced, other_shared = together(
-        *grad_returned, send_up.astype(BF16), send_down.astype(BF16), produced, other_shared
+    *grad_returned, send_up, send_down, produced, shared_sum = together(
+        *grad_returned, send_up.astype(BF16), send_down.astype(BF16), produced, shared_sum
     )
     returned = produced
     returned = exchange(returned)
 
-    shared_sum = reduce_wide(add_narrow(shared_grads, other_shared)[0].astype(BF16))
+    shared_sum = reduce_wide(shared_sum)
     other_up_grad = swap(send_up) if narrow == 2 else send_up
     other_down_grad = swap(send_down) if narrow == 2 else send_down
 
@@ -711,15 +725,37 @@
         queries, keys, values, grad_mixed, exact_heads, totals, low, high
     )
 
-    returned = together(returned, grad_queries)[0]
     other_up_grad, other_down_grad, grad_queries, grad_keys, grad_values = together(
         other_up_grad, other_down_grad, grad_queries, grad_keys, grad_values
     )
     expert_up_grad = add_narrow(up_grad, other_up_grad)[None]
     expert_down_grad = add_narrow(down_grad, other_down_grad)[None]
+    returned, expert_up_grad, expert_down_grad = together(
+        returned, expert_up_grad, expert_down_grad
+    )
     returned = split_halves(returned, experts)
     mixture = shared + combine(places, gates, returned, capacity)
     mixture = mixture.reshape(slots, IMG_SHORT, width)
+    attention_grad_t = jnp.concatenate(
+        [
+            product(grad_queries, first_entry, "te,td->ed").astype(BF16),
+            product(grad_keys, group_entry, "te,td->ed").astype(BF16),
+            product(grad_values, group_entry, "te,td->ed").astype(BF16),
+        ],
+        axis=0,
+    )
+    late_grads = jnp.concatenate(
+        [
+            attention_grad_t.reshape(experts, attention_end, width),
+            projection_grad_t.reshape(experts, column_share, width),
+        ],
+        axis=1,
+    )
+    late_grads = late_grads.reshape(-1, width)
+    late_grads, grad_queries, grad_keys, grad_values = together(
+        late_grads, grad_queries, grad_keys, grad_values
+    )
+    late_sum = reduce_wide(late_grads)
     grad_group = product(grad_keys, attention_t[width : 2 * width], "te,ed->td") + product(
         grad_values, attention_t[2 * width :], "te,ed->td"
     )
@@ -730,14 +766,6 @@
         grad_entry = add_narrow(grad_group, other_entry) + grad_own
     else:
         grad_entry = reduce_narrow(grad_group, 0) + grad_own
-    attention_grad_t = jnp.concatenate(
-        [
-            product(grad_queries, first_entry, "te,td->ed").astype(BF16),
-            product(grad_keys, group_entry, "te,td->ed").astype(BF16),
-            product(grad_values, group_entry, "te,td->ed").astype(BF16),
-        ],
-        axis=0,
-    )
     block_out = (middle + gate_b * mixture).reshape(local_rows, width).astype(BF16)
     grad_gate_b = jnp.sum(grad_top * mixture, axis=1)
     grad_entry = grad_entry.reshape(slots, IMG_SHORT, width)
@@ -758,18 +786,9 @@
         "sd,se->de",
     )
     expand_share = expand_weight.shape[1]
-    expand_share = expand_weight.shape[1]
     expand_grad = shared_sum[:expand_share].astype(F32).T
     contract_grad = shared_sum[expand_share:].astype(F32).reshape(folds, column_share, half)
     contract_grad = contract_grad.transpose(0, 2, 1).reshape(folds * half, column_share)
-    late_grads = jnp.concatenate(
-        [
-            attention_grad_t.reshape(experts, attention_end, width),
-            projection_grad_t.reshape(experts, column_share, width),
-        ],
-        axis=1,
-    )
-    late_sum = reduce_wide(late_grads.reshape(-1, width))
     late_sum, block_out, patch_grad, modulation_grad, expand_grad, contract_grad = together(
         late_sum, block_out, patch_grad, modulation_grad, expand_grad, contract_grad
     )

time: 859 us -> 847 us (0.986)
  waiting for transfers between devices: 154 us -> 119 us
  starting transfers between devices: 122 us -> 150 us
  other arithmetic: 86.3 us -> 97.2 us
  Pallas kernels: 283 us -> 274 us
    all_gather x1 -> x2, waiting for transfers between devices: 66.7 us -> 7.21 us  [gather_wide(): return lax.all_gather(values, 'wide', axis=0, tiled=True)]
    all_to_all x10, starting transfers between devices: 104 us -> 134 us  [to_all(): lax.all_to_all(blocks, 'wide', split_axis=0, concat_axis=0, tiled=True)]
    all_to_all x10, waiting for transfers between devices: 34 us -> 58 us  [to_all(): lax.all_to_all(blocks, 'wide', split_axis=0, concat_axis=0, tiled=True)]
    unnamed x158 -> x164, local copies, waits for them, and re-layouts: 20.5 us -> 22.3 us
  transfers between devices with their start and end apart: 26 -> 27, of which waited for: 13 -> 14; matrix products, arithmetic and copies ran while one was open for 30% -> 31% of each run, Pallas kernels for 33% -> 33%
where the time goes in v3:
time: 847 us; the launch traced here: 840 us
  Pallas kernels  274 us (32%)
  starting transfers between devices  150 us (18%)
  matrix products  128 us (15%)
  waiting for transfers between devices  119 us (14%)
  other arithmetic  97.2 us (11%)
  local copies, waits for them, and re-layouts  56.7 us (7%)
  between operations  15.4 us (2%)
    all_to_all x10, starting transfers between devices, to_all(): lax.all_to_all(blocks, 'wide', split_axis=0, concat_axis=0, tiled=True)  134 us
    pallas_call x3, Pallas kernels, feed(): pl.pallas_call(functools.partial(feed_kernel, transposed, tile, with_out)...  131 us
    dot_general x27, matrix products, product(): return jnp.einsum(form, left, right, preferred_element_type=F32)  126 us
    pallas_call x1, Pallas kernels, attention_backward(): pl.pallas_call(functools.partial(backward_kernel, head_dim), grid_spec=pl...  65.8 us
    all_to_all x10, waiting for transfers between devices, to_all(): lax.all_to_all(blocks, 'wide', split_axis=0, concat_axis=0, tiled=True)  58 us
    ppermute x13, waiting for transfers between devices, swap(): return lax.ppermute(values, 'narrow', [(0, 1), (1, 0)])  48.8 us
    pallas_call x1, Pallas kernels, attention_forward(): pl.pallas_call(functools.partial(forward_kernel, head_dim), grid_spec=plt...  35.6 us
    pallas_call x2, Pallas kernels, combine(): pl.pallas_call(kernel, grid=(tokens // block,), in_specs=[part] * len(ope...  22.3 us
  transfers between devices with their start and end apart: 27, of which 14 were waited for; matrix products, arithmetic and copies ran while one was open for 31% of the time, Pallas kernels for 33%

profile of v3, /device:TPU:0, one launch (start us, length us, event | category | flops | bytes accessed | tf_op | source)
XLA Modules:
  0.0 839.9 jit_solution(12403673901089135444)
XLA Ops:
  13.3 9.1 %collective-permute-done.4 = bf16[192,384]{1,0:T(8,128)(2,1)S(1)} collective-permute-done((bf16[192,384]{1,0:T(8,128)(2,1)S(1)}, bf16[192,384]{1,0:T(8,128)(2,1)S(1)}, u32[]{:S(2)}, u32[]{:S(2)}) %collective-permute-start.4) | collective-permute-done | bytes 147488 | tf_op jit(solution)/shard_map/ppermute | solution.py:459
  63.6 10.7 %pack.2 = (bf16[2048,768]{1,0:T(8,128)(2,1)}, bf16[2048,768]{1,0:T(8,128)(2,1)}) custom-call(s32[16,1024]{1,0:T(8,128)S(1)} %copy.104.place_ref, f32[16,1024]{1,0:T(8,128)S(1)} %bitcast.225, bf16[1024,768]{1,0:T(8,128)(2,1)S(1)} %fusion.12.values_ref.grad_ref), custom_call_target="tpu_custom_call" | custom-call | flops 6442450944 | bytes 7864320 | tf_op jit(solution)/shard_map/pack/pallas_call | solution.py:332
  108.2 35.6 %attention_forward.1 = (bf16[1024,768]{1,0:T(8,128)(2,1)S(1)}, f32[1024,768]{1,0:T(8,128)}, f32[3,4,1024]{2,1,0:T(4,128)S(1)}) custom-call(s32[4]{0:T(128)S(1)} %get-tuple-element.175.low_ref, s32[4]{0:T(128)S(1)} %get-tuple-element.174.high_ref, bf16[1024,768]{1,0:T(8,128)(2,1)S(1)} %convolution_convert_fusion.5.q_ref, ...), custom_call_target="tpu_custom_call" | custom-call | flops 25769803776 | bytes 12582912 | tf_op jit(solution)/shard_map/attention_forward/pallas_call | solution.py:153
  147.4 32.8 %all-to-all-done.2 = bf16[16,128,768]{2,1,0:T(8,128)(2,1)} async-done(((bf16[16,128,768]{2,1,0:T(8,128)(2,1)}), bf16[16,128,768]{2,1,0:T(8,128)(2,1)}, u32[]{:S(2)}, u32[]{:S(2)}) %all-to-all-start.2) | async-done | bytes 3145760 | tf_op jit(solution)/shard_map/all_to_all | solution.py:510
  180.2 40.8 %all-to-all-start.3 = ((bf16[16,128,768]{2,1,0:T(8,128)(2,1)}), bf16[16,128,768]{2,1,0:T(8,128)(2,1)}, u32[]{:S(2)}, u32[]{:S(2)}) async-start(bf16[16,128,768]{2,1,0:T(8,128)(2,1)} %bitcast.250), calls=%async_computation.3 | async-start | bytes 6291456 | tf_op jit(solution)/shard_map/all_to_all | solution.py:510
  236.1 8.8 %pack.3 = (bf16[2048,768]{1,0:T(8,128)(2,1)}, bf16[2048,768]{1,0:T(8,128)(2,1)}) custom-call(s32[16,1024]{1,0:T(8,128)S(1)} %copy.104.place_ref, bf16[1024,768]{1,0:T(8,128)(2,1)S(1)} %bitcast.219), custom_call_target="tpu_custom_call" | custom-call | flops 6442450944 | bytes 7864320 | tf_op jit(solution)/shard_map/pack/pallas_call | solution.py:332
  255.2 19.9 %collective-permute-done.6 = bf16[384,3072]{1,0:T(8,128)(2,1)} collective-permute-done((bf16[384,3072]{1,0:T(8,128)(2,1)}, bf16[384,3072]{1,0:T(8,128)(2,1)}, u32[]{:S(2)}, u32[]{:S(2)}) %collective-permute-start.6) | collective-permute-done | bytes 2359328 | tf_op jit(solution)/shard_map/ppermute | solution.py:459
  280.4 15.9 %all-to-all-start.4 = ((bf16[16,128,768]{2,1,0:T(8,128)(2,1)}), bf16[16,128,768]{2,1,0:T(8,128)(2,1)}, u32[]{:S(2)}, u32[]{:S(2)}) async-start(bf16[16,128,768]{2,1,0:T(8,128)(2,1)} %bitcast.42), calls=%async_computation.4 | async-start | bytes 6291456 | tf_op jit(solution)/shard_map/all_to_all | solution.py:510
  296.3 30.3 %feed.3 = (bf16[1024,3072]{1,0:T(8,128)(2,1)}, bf16[1024,3072]{1,0:T(8,128)(2,1)}, f32[1024,768]{1,0:T(8,128)}, f32[1024,768]{1,0:T(8,128)}) custom-call(bf16[1024,768]{1,0:T(8,128)(2,1)S(1)} %bitcast.220, bf16[1024,768]{1,0:T(8,128)(2,1)S(1)} %fusion.12.values_ref.grad_ref, bf16[3072,768]{1,0:T(8,128)(2,1)} %pad_maximum_fusion.1.up_ref, ...), custom_call_target="tpu_custom_call" | custom-call | flops 19327352832 | bytes 28311552 | tf_op jit(solution)/shard_map/feed/pallas_call | solution.py:437
  361.4 10.1 %all-to-all-start.5 = ((bf16[16,128,768]{2,1,0:T(8,128)(2,1)}), bf16[16,128,768]{2,1,0:T(8,128)(2,1)S(1)}, u32[]{:S(2)}, u32[]{:S(2)}) async-start(bf16[16,128,768]{2,1,0:T(8,128)(2,1)} %bitcast.44), calls=%async_computation.5 | async-start | bytes 6291456 | tf_op jit(solution)/shard_map/all_to_all | solution.py:510
  378.7 50.2 %feed.4 = (bf16[2048,3072]{1,0:T(8,128)(2,1)}, bf16[2048,3072]{1,0:T(8,128)(2,1)}, bf16[2048,768]{1,0:T(8,128)(2,1)}, bf16[2048,768]{1,0:T(8,128)(2,1)}) custom-call(bf16[2048,768]{1,0:T(8,128)(2,1)} %bitcast.43.in_ref, bf16[2048,768]{1,0:T(8,128)(2,1)} %bitcast.21.grad_ref, bf16[768,3072]{1,0:T(8,128)(2,1)} %maximum_select_fusion.up_ref, ...), custom_call_target="tpu_custom_call" | custom-call | flops 38654705664 | bytes 47185920 | tf_op jit(solution)/shard_map/feed/pallas_call | solution.py:437
  428.9 16.3 %fusion.57 = f32[768,3072]{1,0:T(8,128)} fusion(bf16[2048,768]{1,0:T(8,128)(2,1)} %bitcast.43.in_ref, bf16[2048,3072]{1,0:T(8,128)(2,1)} %get-tuple-element.119), kind=kOutput, calls=%fused_computation.186 | convolution fusion | flops 9663676416 | bytes 25165824 | tf_op jit(solution)/shard_map/rd,rf->df/dot_general | solution.py:33
  452.9 50.3 %feed.5 = (bf16[2048,3072]{1,0:T(8,128)(2,1)}, bf16[2048,3072]{1,0:T(8,128)(2,1)}, bf16[2048,768]{1,0:T(8,128)(2,1)}, bf16[2048,768]{1,0:T(8,128)(2,1)}) custom-call(bf16[2048,768]{1,0:T(8,128)(2,1)} %bitcast.252, bf16[2048,768]{1,0:T(8,128)(2,1)} %bitcast.41.grad_ref, bf16[768,3072]{1,0:T(8,128)(2,1)} %maximum_select_fusion.up_ref, ...), custom_call_target="tpu_custom_call" | custom-call | flops 38654705664 | bytes 47185920 | tf_op jit(solution)/shard_map/feed/pallas_call | solution.py:437
  508.4 16.3 %fusion.58 = f32[3072,768]{1,0:T(8,128)} fusion(bf16[2048,3072]{1,0:T(8,128)(2,1)} %get-tuple-element.122, bf16[2048,768]{1,0:T(8,128)(2,1)} %bitcast.41.grad_ref), kind=kOutput, calls=%fused_computation.187 | convolution fusion | flops 9663676416 | bytes 25165824 | tf_op jit(solution)/shard_map/rf,rd->fd/dot_general | solution.py:33
  532.5 15.9 %convolution_add_fusion = f32[3072,768]{1,0:T(8,128)S(1)} fusion(f32[3072,768]{1,0:T(8,128)} %fusion.58, bf16[2048,3072]{1,0:T(8,128)(2,1)} %get-tuple-element.121, bf16[2048,768]{1,0:T(8,128)(2,1)} %bitcast.21.grad_ref), kind=kOutput, calls=%fused_computation.14 | convolution fusion | flops 9666035712 | bytes 34603008 | tf_op jit(solution)/shard_map/rf,rd->fd/dot_general | solution.py:33
  552.5 17.6 %convolution_add_fusion.1 = f32[768,3072]{1,0:T(8,128)} fusion(f32[768,3072]{1,0:T(8,128)} %fusion.57, bf16[2048,768]{1,0:T(8,128)(2,1)S(1)} %bitcast.253, bf16[2048,3072]{1,0:T(8,128)(2,1)} %get-tuple-element.120), kind=kOutput, calls=%fused_computation.15 | convolution fusion | flops 9666035712 | bytes 34603008 | tf_op jit(solution)/shard_map/rd,rf->df/dot_general | solution.py:33
  574.3 8.3 fusion.6
  582.5 9.3 %all-to-all-done.7 = bf16[16,128,768]{2,1,0:T(8,128)(2,1)} async-done(((bf16[16,128,768]{2,1,0:T(8,128)(2,1)}), bf16[16,128,768]{2,1,0:T(8,128)(2,1)}, u32[]{:S(2)}, u32[]{:S(2)}) %all-to-all-start.7) | async-done | bytes 3145760 | tf_op jit(solution)/shard_map/all_to_all | solution.py:510
  591.9 15.6 %all-to-all-start.8 = ((bf16[16,256,768]{2,1,0:T(8,128)(2,1)}), bf16[16,256,768]{2,1,0:T(8,128)(2,1)}, u32[]{:S(2)}, u32[]{:S(2)}) async-start(bf16[16,256,768]{2,1,0:T(8,128)(2,1)} %pad_maximum_fusion), calls=%async_computation.9 | async-start | bytes 12582912 | tf_op jit(solution)/shard_map/all_to_all | solution.py:510
  609.7 10.7 %combine.2 = f32[1024,768]{1,0:T(8,128)S(1)} custom-call(s32[1024,16]{1,0:T(8,128)S(1)} %copy-done.3, bf16[2048,768]{1,0:T(8,128)(2,1)} %bitcast.251, bf16[2048,768]{1,0:T(8,128)(2,1)} %bitcast.61.refs_1_), custom_call_target="tpu_custom_call" | custom-call | flops 6442450944 | bytes 9437184 | tf_op jit(solution)/shard_map/combine/pallas_call | solution.py:374
  635.2 65.8 %attention_backward.1 = (bf16[1024,768]{1,0:T(8,128)(2,1)S(1)}, bf16[2048,768]{1,0:T(8,128)(2,1)}, bf16[2048,768]{1,0:T(8,128)(2,1)}) custom-call(s32[4]{0:T(128)S(1)} %get-tuple-element.175.low_ref, s32[4]{0:T(128)S(1)} %get-tuple-element.174.high_ref, bf16[1024,768]{1,0:T(8,128)(2,1)S(1)} %copy-done.6, bf16[2048,768]{1,0:T(8,128)(2,1)} %convolution_convert_fusion.3.k_ref, ...), custom_call_target="tpu_custom_call" | custom-call | flops 64424509440 | bytes 20447232 | tf_op jit(solution)/shard_map/attention_backward/pallas_call | solution.py:262
  702.6 9.4 %collective-permute-done.9 = bf16[1536,768]{1,0:T(8,128)(2,1)} collective-permute-done((bf16[1536,768]{1,0:T(8,128)(2,1)}, bf16[1536,768]{1,0:T(8,128)(2,1)}, u32[]{:S(2)}, u32[]{:S(2)}) %collective-permute-start.9) | collective-permute-done | bytes 2359328 | tf_op jit(solution)/shard_map/ppermute | solution.py:459
  760.9 11.6 %combine.3 = f32[1024,768]{1,0:T(8,128)S(1)} custom-call(s32[1024,16]{1,0:T(8,128)S(1)} %copy-done.3, f32[1024,16]{1,0:T(8,128)S(1)} %copy-done.4, bf16[2048,768]{1,0:T(8,128)(2,1)} %bitcast.257, bf16[2048,768]{1,0:T(8,128)(2,1)} %bitcast.256), custom_call_target="tpu_custom_call" | custom-call | flops 6442450944 | bytes 9437184 | tf_op jit(solution)/shard_map/combine/pallas_call | solution.py:374
  782.3 23.7 %all-to-all-start.9 = ((bf16[16,4,288]{2,1,0:T(4,128)(2,1)}), bf16[16,4,288]{2,1,0:T(4,128)(2,1)S(1)}, u32[]{:S(2)}, u32[]{:S(2)}) async-start(bf16[16,4,288]{2,1,0:T(4,128)(2,1)} %copy.115), calls=%async_computation.10 | async-start | bytes 98304 | tf_op jit(solution)/shard_map/all_to_all | solution.py:510
  (337 shorter events, 289.3 us)
Async XLA Ops:
  7.2 74.2 %all-gather.3.cloned.1.call-start = ((), (), s32[]{:S(2)}) async-start(), calls=%async_computation.12 | async-start | bytes 5013504 | tf_op jit(solution)/shard_map/all_gather | solution.py:539
  9.3 13.2 %collective-permute-start.3 = (bf16[192,768]{1,0:T(8,128)(2,1)S(1)}, bf16[192,768]{1,0:T(8,128)(2,1)S(1)}, u32[]{:S(2)}, u32[]{:S(2)}) collective-permute-start(bf16[192,768]{1,0:T(8,128)(2,1)S(1)} %pad_maximum_fusion.6), channel_id=1, source_target_pairs={{0,1},{1,0},{2,3},{3,2},{4,5},{5,4},{6,7},{7,6},{8,9},{9,8},{10,11... | collective-permute-start | bytes 884744 | tf_op jit(solution)/shard_map/ppermute | solution.py:459
  13.2 9.2 %collective-permute-start.4 = (bf16[192,384]{1,0:T(8,128)(2,1)S(1)}, bf16[192,384]{1,0:T(8,128)(2,1)S(1)}, u32[]{:S(2)}, u32[]{:S(2)}) collective-permute-start(bf16[192,384]{1,0:T(8,128)(2,1)S(1)} %pad_maximum_fusion.7), channel_id=1, source_target_pairs={{0,1},{1,0},{2,3},{3,2},{4,5},{5,4},{6,7},{7,6},{8,9},{9,8},{10,11... | collective-permute-start | bytes 442376 | tf_op jit(solution)/shard_map/ppermute | solution.py:459
  25.3 219.7 %all-gather.5.cloned.1.call-start = ((), (), s32[]{:S(2)}) async-start(), calls=%async_computation.13 | async-start | bytes 10027008 | tf_op jit(solution)/shard_map/all_gather | solution.py:539
  26.7 13.6 %all-to-all-start = ((bf16[16,4,768]{2,1,0:T(4,128)(2,1)}), bf16[16,4,768]{2,1,0:T(4,128)(2,1)S(1)}, u32[]{:S(2)}, u32[]{:S(2)}) async-start(bf16[16,4,768]{2,1,0:T(4,128)(2,1)} %broadcast_in_dim.27), calls=%async_computation | async-start | bytes 196608 | tf_op jit(solution)/shard_map/all_to_all | solution.py:510
  32.9 8.9 %collective-permute-start.1 = (bf16[384,288]{0,1:T(8,128)(2,1)S(1)}, bf16[384,288]{0,1:T(8,128)(2,1)S(1)}, u32[]{:S(2)}, u32[]{:S(2)}) collective-permute-start(bf16[384,288]{0,1:T(8,128)(2,1)S(1)} %copy-done.37), channel_id=1, source_target_pairs={{0,1},{1,0},{2,3},{3,2},{4,5},{5,4},{6,7},{7,6},{8,9},{9,8},{10,11... | collective-permute-start | bytes 663560 | tf_op jit(solution)/shard_map/ppermute | solution.py:459
  46.2 14.2 %all-to-all-start.1 = ((f32[16,8,288]{2,1,0:T(8,128)}), f32[16,8,288]{2,1,0:T(8,128)S(1)}, u32[]{:S(2)}, u32[]{:S(2)}) async-start(f32[16,8,288]{2,1,0:T(8,128)} %convolution_bitcast_fusion), calls=%async_computation.1 | async-start | bytes 393216 | tf_op jit(solution)/shard_map/all_to_all | solution.py:510
  53.2 37.8 %collective-permute-start.2 = (bf16[1024,768]{1,0:T(8,128)(2,1)S(1)}, bf16[1024,768]{1,0:T(8,128)(2,1)}, u32[]{:S(2)}, u32[]{:S(2)}) collective-permute-start(bf16[1024,768]{1,0:T(8,128)(2,1)S(1)} %copy-done.10), channel_id=1, source_target_pairs={{0,1},{1,0},{2,3},{3,2},{4,5},{5,4},{6,7},{7,6},{8,9},{9,8},{10,11... | collective-permute-start | bytes 4718600 | tf_op jit(solution)/shard_map/ppermute | solution.py:459
  85.6 94.6 %all-to-all-start.2 = ((bf16[16,128,768]{2,1,0:T(8,128)(2,1)}), bf16[16,128,768]{2,1,0:T(8,128)(2,1)}, u32[]{:S(2)}, u32[]{:S(2)}) async-start(bf16[16,128,768]{2,1,0:T(8,128)(2,1)} %bitcast.20), calls=%async_computation.2 | async-start | bytes 6291456 | tf_op jit(solution)/shard_map/all_to_all | solution.py:510
  93.8 53.6 %collective-permute-start.5 = (bf16[1536,768]{1,0:T(8,128)(2,1)S(1)}, bf16[1536,768]{1,0:T(8,128)(2,1)}, u32[]{:S(2)}, u32[]{:S(2)}) collective-permute-start(bf16[1536,768]{1,0:T(8,128)(2,1)S(1)} %bitcast.268), channel_id=1, source_target_pairs={{0,1},{1,0},{2,3},{3,2},{4,5},{5,4},{6,7},{7,6},{8,9},{9,8},{10,11... | collective-permute-start | bytes 7077896 | tf_op jit(solution)/shard_map/ppermute | solution.py:459
  180.2 100.2 %all-to-all-start.3 = ((bf16[16,128,768]{2,1,0:T(8,128)(2,1)}), bf16[16,128,768]{2,1,0:T(8,128)(2,1)}, u32[]{:S(2)}, u32[]{:S(2)}) async-start(bf16[16,128,768]{2,1,0:T(8,128)(2,1)} %bitcast.250), calls=%async_computation.3 | async-start | bytes 6291456 | tf_op jit(solution)/shard_map/all_to_all | solution.py:510
  221.1 54.0 %collective-permute-start.6 = (bf16[384,3072]{1,0:T(8,128)(2,1)}, bf16[384,3072]{1,0:T(8,128)(2,1)}, u32[]{:S(2)}, u32[]{:S(2)}) collective-permute-start(bf16[384,3072]{1,0:T(8,128)(2,1)} %bitcast.270), channel_id=1, source_target_pairs={{0,1},{1,0},{2,3},{3,2},{4,5},{5,4},{6,7},{7,6},{8,9},{9,8},{10,11... | collective-permute-start | bytes 7077896 | tf_op jit(solution)/shard_map/ppermute | solution.py:459
  280.4 81.0 %all-to-all-start.4 = ((bf16[16,128,768]{2,1,0:T(8,128)(2,1)}), bf16[16,128,768]{2,1,0:T(8,128)(2,1)}, u32[]{:S(2)}, u32[]{:S(2)}) async-start(bf16[16,128,768]{2,1,0:T(8,128)(2,1)} %bitcast.42), calls=%async_computation.4 | async-start | bytes 6291456 | tf_op jit(solution)/shard_map/all_to_all | solution.py:510
  361.4 83.8 %all-to-all-start.5 = ((bf16[16,128,768]{2,1,0:T(8,128)(2,1)}), bf16[16,128,768]{2,1,0:T(8,128)(2,1)S(1)}, u32[]{:S(2)}, u32[]{:S(2)}) async-start(bf16[16,128,768]{2,1,0:T(8,128)(2,1)} %bitcast.44), calls=%async_computation.5 | async-start | bytes 6291456 | tf_op jit(solution)/shard_map/all_to_all | solution.py:510
  378.1 146.6 %collective-permute-start.7 = (bf16[1,6144,384]{2,1,0:T(8,128)(2,1)}, bf16[1,6144,384]{2,1,0:T(8,128)(2,1)}, u32[]{:S(2)}, u32[]{:S(2)}) collective-permute-start(bf16[1,6144,384]{2,1,0:T(8,128)(2,1)} %fusion.8), channel_id=1, source_target_pairs={{0,1},{1,0},{2,3},{3,2},{4,5},{5,4},{6,7},{7,6},{8,9},{9,8},{10,11... | collective-permute-start | bytes 14155784 | tf_op jit(solution)/shard_map/ppermute | solution.py:459
  446.9 77.8 %all-to-all-start.6 = ((bf16[16,128,768]{2,1,0:T(8,128)(2,1)}), bf16[16,128,768]{2,1,0:T(8,128)(2,1)S(1)}, u32[]{:S(2)}, u32[]{:S(2)}) async-start(bf16[16,128,768]{2,1,0:T(8,128)(2,1)} %bitcast.46), calls=%async_computation.6 | async-start | bytes 6291456 | tf_op jit(solution)/shard_map/all_to_all | solution.py:510
  526.4 65.5 %all-to-all-start.7 = ((bf16[16,128,768]{2,1,0:T(8,128)(2,1)}), bf16[16,128,768]{2,1,0:T(8,128)(2,1)}, u32[]{:S(2)}, u32[]{:S(2)}) async-start(bf16[16,128,768]{2,1,0:T(8,128)(2,1)} %bitcast.60), calls=%async_computation.7 | async-start | bytes 6291456 | tf_op jit(solution)/shard_map/all_to_all | solution.py:510
  532.4 219.2 %reduce-scatter.5.cloned.1.call-start = ((), (), s32[]{:S(2)}) async-start(), calls=%async_computation.15 | async-start | bytes 5013504 | tf_op jit(solution)/shard_map/reduce_scatter | solution.py:543
  591.9 162.3 %all-to-all-start.8 = ((bf16[16,256,768]{2,1,0:T(8,128)(2,1)}), bf16[16,256,768]{2,1,0:T(8,128)(2,1)}, u32[]{:S(2)}, u32[]{:S(2)}) async-start(bf16[16,256,768]{2,1,0:T(8,128)(2,1)} %pad_maximum_fusion), calls=%async_computation.9 | async-start | bytes 12582912 | tf_op jit(solution)/shard_map/all_to_all | solution.py:510
  607.5 217.2 %reduce-scatter.3.cloned.1.call-start = ((), (), s32[]{:S(2)}) async-start(), calls=%async_computation.14 | async-start | bytes 5013504 | tf_op jit(solution)/shard_map/reduce_scatter | solution.py:543
  607.6 95.0 %collective-permute-start.8 = (bf16[384,3072]{1,0:T(8,128)(2,1)}, bf16[384,3072]{1,0:T(8,128)(2,1)}, u32[]{:S(2)}, u32[]{:S(2)}) collective-permute-start(bf16[384,3072]{1,0:T(8,128)(2,1)} %dynamic-slice_convert_fusion.1), channel_id=1, source_target_pairs={{0,1},{1,0},{2,3},{3,2},{4,5},{5,4},{6,7},{7,6},{8,9},{9,8},{10,11... | collective-permute-start | bytes 7077896 | tf_op jit(solution)/shard_map/ppermute | solution.py:459
  609.0 103.0 %collective-permute-start.9 = (bf16[1536,768]{1,0:T(8,128)(2,1)}, bf16[1536,768]{1,0:T(8,128)(2,1)}, u32[]{:S(2)}, u32[]{:S(2)}) collective-permute-start(bf16[1536,768]{1,0:T(8,128)(2,1)} %dynamic-slice_convert_fusion), channel_id=1, source_target_pairs={{0,1},{1,0},{2,3},{3,2},{4,5},{5,4},{6,7},{7,6},{8,9},{9,8},{10,11... | collective-permute-start | bytes 7077896 | tf_op jit(solution)/shard_map/ppermute | solution.py:459
  738.2 36.9 %collective-permute-start.10 = (bf16[1024,768]{1,0:T(8,128)(2,1)}, bf16[1024,768]{1,0:T(8,128)(2,1)}, u32[]{:S(2)}, u32[]{:S(2)}) collective-permute-start(bf16[1024,768]{1,0:T(8,128)(2,1)} %dynamic-slice_convert_fusion.2), channel_id=1, source_target_pairs={{0,1},{1,0},{2,3},{3,2},{4,5},{5,4},{6,7},{7,6},{8,9},{9,8},{10,11... | collective-permute-start | bytes 4718600 | tf_op jit(solution)/shard_map/ppermute | solution.py:459
  782.3 30.6 %all-to-all-start.9 = ((bf16[16,4,288]{2,1,0:T(4,128)(2,1)}), bf16[16,4,288]{2,1,0:T(4,128)(2,1)S(1)}, u32[]{:S(2)}, u32[]{:S(2)}) async-start(bf16[16,4,288]{2,1,0:T(4,128)(2,1)} %copy.115), calls=%async_computation.10 | async-start | bytes 98304 | tf_op jit(solution)/shard_map/all_to_all | solution.py:510
  (76 other events, 888.7 us)
Sparse Core Ops, SparseCore 0:
  25.4 56.0 all-gather.2
  84.3 136.4 all-gather.4
  592.0 154.2 reduce-scatter.4
  750.5 74.1 reduce-scatter.2

commit v4 on v3

--- a/solution.py
+++ b/solution.py
@@ -13,7 +13,7 @@
 QUAD = 4
 HALVES = 2
 FORWARD_CHUNK = 512
-BACKWARD_CHUNK = 1024
+BACKWARD_CHUNK = 2048
 FEED_ROWS = 512
 FEED_TILE = 768
 PACK_EXPERTS = 2

time: 847 us -> 847 us (level)
  Pallas kernels: 274 us -> 285 us
  waiting for transfers between devices: 119 us -> 108 us
    ppermute x13, waiting for transfers between devices: 48.8 us -> 38.4 us  [swap(): return lax.ppermute(values, 'narrow', [(0, 1), (1, 0)])]
  transfers between devices with their start and end apart: 27 -> 27, of which waited for: 14 -> 13; matrix products, arithmetic and copies ran while one was open for 31% -> 31% of each run, Pallas kernels for 33% -> 34%
where the time goes in v4:
time: 847 us; the launch traced here: 840 us
  Pallas kernels  285 us (34%)
  starting transfers between devices  150 us (18%)
  matrix products  128 us (15%)
  waiting for transfers between devices  108 us (13%)
  other arithmetic  97.2 us (11%)
  local copies, waits for them, and re-layouts  56.7 us (7%)
  between operations  15.4 us (2%)
    all_to_all x10, starting transfers between devices, to_all(): lax.all_to_all(blocks, 'wide', split_axis=0, concat_axis=0, tiled=True)  134 us
    pallas_call x3, Pallas kernels, feed(): pl.pallas_call(functools.partial(feed_kernel, transposed, tile, with_out)...  131 us
    dot_general x27, matrix products, product(): return jnp.einsum(form, left, right, preferred_element_type=F32)  126 us
    pallas_call x1, Pallas kernels, attention_backward(): pl.pallas_call(functools.partial(backward_kernel, head_dim), grid_spec=pl...  72.6 us
    all_to_all x10, waiting for transfers between devices, to_all(): lax.all_to_all(blocks, 'wide', split_axis=0, concat_axis=0, tiled=True)  58 us
    pallas_call x1, Pallas kernels, attention_forward(): pl.pallas_call(functools.partial(forward_kernel, head_dim), grid_spec=plt...  39.3 us
    ppermute x13, waiting for transfers between devices, swap(): return lax.ppermute(values, 'narrow', [(0, 1), (1, 0)])  38.4 us
    pallas_call x2, Pallas kernels, combine(): pl.pallas_call(kernel, grid=(tokens // block,), in_specs=[part] * len(ope...  22.3 us
  transfers between devices with their start and end apart: 27, of which 13 were waited for; matrix products, arithmetic and copies ran while one was open for 31% of the time, Pallas kernels for 34%

profile of v4, /device:TPU:0, one launch (start us, length us, event | category | flops | bytes accessed | tf_op | source)
XLA Modules:
  0.0 839.9 jit_solution(16736997071197148349)
XLA Ops:
  13.3 9.1 %collective-permute-done.4 = bf16[192,384]{1,0:T(8,128)(2,1)S(1)} collective-permute-done((bf16[192,384]{1,0:T(8,128)(2,1)S(1)}, bf16[192,384]{1,0:T(8,128)(2,1)S(1)}, u32[]{:S(2)}, u32[]{:S(2)}) %collective-permute-start.4) | collective-permute-done | bytes 147488 | tf_op jit(solution)/shard_map/ppermute | solution.py:459
  63.6 10.7 %pack.2 = (bf16[2048,768]{1,0:T(8,128)(2,1)}, bf16[2048,768]{1,0:T(8,128)(2,1)}) custom-call(s32[16,1024]{1,0:T(8,128)S(1)} %copy.104.place_ref, f32[16,1024]{1,0:T(8,128)S(1)} %bitcast.225, bf16[1024,768]{1,0:T(8,128)(2,1)S(1)} %fusion.12.values_ref.grad_ref), custom_call_target="tpu_custom_call" | custom-call | flops 6442450944 | bytes 7864320 | tf_op jit(solution)/shard_map/pack/pallas_call | solution.py:332
  108.2 39.3 %attention_forward.1 = (bf16[1024,768]{1,0:T(8,128)(2,1)S(1)}, f32[1024,768]{1,0:T(8,128)}, f32[3,4,1024]{2,1,0:T(4,128)S(1)}) custom-call(s32[4]{0:T(128)S(1)} %get-tuple-element.175.low_ref, s32[4]{0:T(128)S(1)} %get-tuple-element.174.high_ref, bf16[1024,768]{1,0:T(8,128)(2,1)S(1)} %convolution_convert_fusion.5.q_ref, ...), custom_call_target="tpu_custom_call" | custom-call | flops 25769803776 | bytes 12582912 | tf_op jit(solution)/shard_map/attention_forward/pallas_call | solution.py:153
  147.4 32.8 %all-to-all-done.2 = bf16[16,128,768]{2,1,0:T(8,128)(2,1)} async-done(((bf16[16,128,768]{2,1,0:T(8,128)(2,1)}), bf16[16,128,768]{2,1,0:T(8,128)(2,1)}, u32[]{:S(2)}, u32[]{:S(2)}) %all-to-all-start.2) | async-done | bytes 3145760 | tf_op jit(solution)/shard_map/all_to_all | solution.py:510
  180.2 40.8 %all-to-all-start.3 = ((bf16[16,128,768]{2,1,0:T(8,128)(2,1)}), bf16[16,128,768]{2,1,0:T(8,128)(2,1)}, u32[]{:S(2)}, u32[]{:S(2)}) async-start(bf16[16,128,768]{2,1,0:T(8,128)(2,1)} %bitcast.250), calls=%async_computation.3 | async-start | bytes 6291456 | tf_op jit(solution)/shard_map/all_to_all | solution.py:510
  236.1 8.8 %pack.3 = (bf16[2048,768]{1,0:T(8,128)(2,1)}, bf16[2048,768]{1,0:T(8,128)(2,1)}) custom-call(s32[16,1024]{1,0:T(8,128)S(1)} %copy.104.place_ref, bf16[1024,768]{1,0:T(8,128)(2,1)S(1)} %bitcast.219), custom_call_target="tpu_custom_call" | custom-call | flops 6442450944 | bytes 7864320 | tf_op jit(solution)/shard_map/pack/pallas_call | solution.py:332
  255.2 19.9 %collective-permute-done.6 = bf16[384,3072]{1,0:T(8,128)(2,1)} collective-permute-done((bf16[384,3072]{1,0:T(8,128)(2,1)}, bf16[384,3072]{1,0:T(8,128)(2,1)}, u32[]{:S(2)}, u32[]{:S(2)}) %collective-permute-start.6) | collective-permute-done | bytes 2359328 | tf_op jit(solution)/shard_map/ppermute | solution.py:459
  280.4 15.9 %all-to-all-start.4 = ((bf16[16,128,768]{2,1,0:T(8,128)(2,1)}), bf16[16,128,768]{2,1,0:T(8,128)(2,1)}, u32[]{:S(2)}, u32[]{:S(2)}) async-start(bf16[16,128,768]{2,1,0:T(8,128)(2,1)} %bitcast.42), calls=%async_computation.4 | async-start | bytes 6291456 | tf_op jit(solution)/shard_map/all_to_all | solution.py:510
  296.3 30.3 %feed.3 = (bf16[1024,3072]{1,0:T(8,128)(2,1)}, bf16[1024,3072]{1,0:T(8,128)(2,1)}, f32[1024,768]{1,0:T(8,128)}, f32[1024,768]{1,0:T(8,128)}) custom-call(bf16[1024,768]{1,0:T(8,128)(2,1)S(1)} %bitcast.220, bf16[1024,768]{1,0:T(8,128)(2,1)S(1)} %fusion.12.values_ref.grad_ref, bf16[3072,768]{1,0:T(8,128)(2,1)} %pad_maximum_fusion.1.up_ref, ...), custom_call_target="tpu_custom_call" | custom-call | flops 19327352832 | bytes 28311552 | tf_op jit(solution)/shard_map/feed/pallas_call | solution.py:437
  361.4 10.1 %all-to-all-start.5 = ((bf16[16,128,768]{2,1,0:T(8,128)(2,1)}), bf16[16,128,768]{2,1,0:T(8,128)(2,1)S(1)}, u32[]{:S(2)}, u32[]{:S(2)}) async-start(bf16[16,128,768]{2,1,0:T(8,128)(2,1)} %bitcast.44), calls=%async_computation.5 | async-start | bytes 6291456 | tf_op jit(solution)/shard_map/all_to_all | solution.py:510
  378.7 50.2 %feed.4 = (bf16[2048,3072]{1,0:T(8,128)(2,1)}, bf16[2048,3072]{1,0:T(8,128)(2,1)}, bf16[2048,768]{1,0:T(8,128)(2,1)}, bf16[2048,768]{1,0:T(8,128)(2,1)}) custom-call(bf16[2048,768]{1,0:T(8,128)(2,1)} %bitcast.43.in_ref, bf16[2048,768]{1,0:T(8,128)(2,1)} %bitcast.21.grad_ref, bf16[768,3072]{1,0:T(8,128)(2,1)} %maximum_select_fusion.up_ref, ...), custom_call_target="tpu_custom_call" | custom-call | flops 38654705664 | bytes 47185920 | tf_op jit(solution)/shard_map/feed/pallas_call | solution.py:437
  428.9 16.3 %fusion.57 = f32[768,3072]{1,0:T(8,128)} fusion(bf16[2048,768]{1,0:T(8,128)(2,1)} %bitcast.43.in_ref, bf16[2048,3072]{1,0:T(8,128)(2,1)} %get-tuple-element.119), kind=kOutput, calls=%fused_computation.186 | convolution fusion | flops 9663676416 | bytes 25165824 | tf_op jit(solution)/shard_map/rd,rf->df/dot_general | solution.py:33
  452.9 50.3 %feed.5 = (bf16[2048,3072]{1,0:T(8,128)(2,1)}, bf16[2048,3072]{1,0:T(8,128)(2,1)}, bf16[2048,768]{1,0:T(8,128)(2,1)}, bf16[2048,768]{1,0:T(8,128)(2,1)}) custom-call(bf16[2048,768]{1,0:T(8,128)(2,1)} %bitcast.252, bf16[2048,768]{1,0:T(8,128)(2,1)} %bitcast.41.grad_ref, bf16[768,3072]{1,0:T(8,128)(2,1)} %maximum_select_fusion.up_ref, ...), custom_call_target="tpu_custom_call" | custom-call | flops 38654705664 | bytes 47185920 | tf_op jit(solution)/shard_map/feed/pallas_call | solution.py:437
  508.4 16.3 %fusion.58 = f32[3072,768]{1,0:T(8,128)} fusion(bf16[2048,3072]{1,0:T(8,128)(2,1)} %get-tuple-element.122, bf16[2048,768]{1,0:T(8,128)(2,1)} %bitcast.41.grad_ref), kind=kOutput, calls=%fused_computation.187 | convolution fusion | flops 9663676416 | bytes 25165824 | tf_op jit(solution)/shard_map/rf,rd->fd/dot_general | solution.py:33
  532.5 15.9 %convolution_add_fusion = f32[3072,768]{1,0:T(8,128)S(1)} fusion(f32[3072,768]{1,0:T(8,128)} %fusion.58, bf16[2048,3072]{1,0:T(8,128)(2,1)} %get-tuple-element.121, bf16[2048,768]{1,0:T(8,128)(2,1)} %bitcast.21.grad_ref), kind=kOutput, calls=%fused_computation.14 | convolution fusion | flops 9666035712 | bytes 34603008 | tf_op jit(solution)/shard_map/rf,rd->fd/dot_general | solution.py:33
  552.5 17.6 %convolution_add_fusion.1 = f32[768,3072]{1,0:T(8,128)} fusion(f32[768,3072]{1,0:T(8,128)} %fusion.57, bf16[2048,768]{1,0:T(8,128)(2,1)S(1)} %bitcast.253, bf16[2048,3072]{1,0:T(8,128)(2,1)} %get-tuple-element.120), kind=kOutput, calls=%fused_computation.15 | convolution fusion | flops 9666035712 | bytes 34603008 | tf_op jit(solution)/shard_map/rd,rf->df/dot_general | solution.py:33
  574.3 8.3 fusion.6
  582.5 9.3 %all-to-all-done.7 = bf16[16,128,768]{2,1,0:T(8,128)(2,1)} async-done(((bf16[16,128,768]{2,1,0:T(8,128)(2,1)}), bf16[16,128,768]{2,1,0:T(8,128)(2,1)}, u32[]{:S(2)}, u32[]{:S(2)}) %all-to-all-start.7) | async-done | bytes 3145760 | tf_op jit(solution)/shard_map/all_to_all | solution.py:510
  591.9 15.6 %all-to-all-start.8 = ((bf16[16,256,768]{2,1,0:T(8,128)(2,1)}), bf16[16,256,768]{2,1,0:T(8,128)(2,1)}, u32[]{:S(2)}, u32[]{:S(2)}) async-start(bf16[16,256,768]{2,1,0:T(8,128)(2,1)} %pad_maximum_fusion), calls=%async_computation.9 | async-start | bytes 12582912 | tf_op jit(solution)/shard_map/all_to_all | solution.py:510
  609.7 10.7 %combine.2 = f32[1024,768]{1,0:T(8,128)S(1)} custom-call(s32[1024,16]{1,0:T(8,128)S(1)} %copy-done.3, bf16[2048,768]{1,0:T(8,128)(2,1)} %bitcast.251, bf16[2048,768]{1,0:T(8,128)(2,1)} %bitcast.61.refs_1_), custom_call_target="tpu_custom_call" | custom-call | flops 6442450944 | bytes 9437184 | tf_op jit(solution)/shard_map/combine/pallas_call | solution.py:374
  635.2 72.6 %attention_backward.1 = (bf16[1024,768]{1,0:T(8,128)(2,1)S(1)}, bf16[2048,768]{1,0:T(8,128)(2,1)}, bf16[2048,768]{1,0:T(8,128)(2,1)}) custom-call(s32[4]{0:T(128)S(1)} %get-tuple-element.175.low_ref, s32[4]{0:T(128)S(1)} %get-tuple-element.174.high_ref, bf16[1024,768]{1,0:T(8,128)(2,1)S(1)} %copy-done.6, bf16[2048,768]{1,0:T(8,128)(2,1)} %convolution_convert_fusion.3.k_ref, ...), custom_call_target="tpu_custom_call" | custom-call | flops 64424509440 | bytes 20447232 | tf_op jit(solution)/shard_map/attention_backward/pallas_call | solution.py:262
  722.7 7.6 fusion.21
  760.9 11.6 %combine.3 = f32[1024,768]{1,0:T(8,128)S(1)} custom-call(s32[1024,16]{1,0:T(8,128)S(1)} %copy-done.3, f32[1024,16]{1,0:T(8,128)S(1)} %copy-done.4, bf16[2048,768]{1,0:T(8,128)(2,1)} %bitcast.257, bf16[2048,768]{1,0:T(8,128)(2,1)} %bitcast.256), custom_call_target="tpu_custom_call" | custom-call | flops 6442450944 | bytes 9437184 | tf_op jit(solution)/shard_map/combine/pallas_call | solution.py:374
  782.3 23.7 %all-to-all-start.9 = ((bf16[16,4,288]{2,1,0:T(4,128)(2,1)}), bf16[16,4,288]{2,1,0:T(4,128)(2,1)S(1)}, u32[]{:S(2)}, u32[]{:S(2)}) async-start(bf16[16,4,288]{2,1,0:T(4,128)(2,1)} %copy.115), calls=%async_computation.10 | async-start | bytes 98304 | tf_op jit(solution)/shard_map/all_to_all | solution.py:510
  (337 shorter events, 280.7 us)
Async XLA Ops:
  7.2 74.2 %all-gather.3.cloned.1.call-start = ((), (), s32[]{:S(2)}) async-start(), calls=%async_computation.12 | async-start | bytes 5013504 | tf_op jit(solution)/shard_map/all_gather | solution.py:539
  9.3 13.2 %collective-permute-start.3 = (bf16[192,768]{1,0:T(8,128)(2,1)S(1)}, bf16[192,768]{1,0:T(8,128)(2,1)S(1)}, u32[]{:S(2)}, u32[]{:S(2)}) collective-permute-start(bf16[192,768]{1,0:T(8,128)(2,1)S(1)} %pad_maximum_fusion.6), channel_id=1, source_target_pairs={{0,1},{1,0},{2,3},{3,2},{4,5},{5,4},{6,7},{7,6},{8,9},{9,8},{10,11... | collective-permute-start | bytes 884744 | tf_op jit(solution)/shard_map/ppermute | solution.py:459
  13.2 9.2 %collective-permute-start.4 = (bf16[192,384]{1,0:T(8,128)(2,1)S(1)}, bf16[192,384]{1,0:T(8,128)(2,1)S(1)}, u32[]{:S(2)}, u32[]{:S(2)}) collective-permute-start(bf16[192,384]{1,0:T(8,128)(2,1)S(1)} %pad_maximum_fusion.7), channel_id=1, source_target_pairs={{0,1},{1,0},{2,3},{3,2},{4,5},{5,4},{6,7},{7,6},{8,9},{9,8},{10,11... | collective-permute-start | bytes 442376 | tf_op jit(solution)/shard_map/ppermute | solution.py:459
  25.3 219.7 %all-gather.5.cloned.1.call-start = ((), (), s32[]{:S(2)}) async-start(), calls=%async_computation.13 | async-start | bytes 10027008 | tf_op jit(solution)/shard_map/all_gather | solution.py:539
  26.7 13.6 %all-to-all-start = ((bf16[16,4,768]{2,1,0:T(4,128)(2,1)}), bf16[16,4,768]{2,1,0:T(4,128)(2,1)S(1)}, u32[]{:S(2)}, u32[]{:S(2)}) async-start(bf16[16,4,768]{2,1,0:T(4,128)(2,1)} %broadcast_in_dim.27), calls=%async_computation | async-start | bytes 196608 | tf_op jit(solution)/shard_map/all_to_all | solution.py:510
  32.9 8.9 %collective-permute-start.1 = (bf16[384,288]{0,1:T(8,128)(2,1)S(1)}, bf16[384,288]{0,1:T(8,128)(2,1)S(1)}, u32[]{:S(2)}, u32[]{:S(2)}) collective-permute-start(bf16[384,288]{0,1:T(8,128)(2,1)S(1)} %copy-done.37), channel_id=1, source_target_pairs={{0,1},{1,0},{2,3},{3,2},{4,5},{5,4},{6,7},{7,6},{8,9},{9,8},{10,11... | collective-permute-start | bytes 663560 | tf_op jit(solution)/shard_map/ppermute | solution.py:459
  46.2 14.2 %all-to-all-start.1 = ((f32[16,8,288]{2,1,0:T(8,128)}), f32[16,8,288]{2,1,0:T(8,128)S(1)}, u32[]{:S(2)}, u32[]{:S(2)}) async-start(f32[16,8,288]{2,1,0:T(8,128)} %convolution_bitcast_fusion), calls=%async_computation.1 | async-start | bytes 393216 | tf_op jit(solution)/shard_map/all_to_all | solution.py:510
  53.2 37.8 %collective-permute-start.2 = (bf16[1024,768]{1,0:T(8,128)(2,1)S(1)}, bf16[1024,768]{1,0:T(8,128)(2,1)}, u32[]{:S(2)}, u32[]{:S(2)}) collective-permute-start(bf16[1024,768]{1,0:T(8,128)(2,1)S(1)} %copy-done.10), channel_id=1, source_target_pairs={{0,1},{1,0},{2,3},{3,2},{4,5},{5,4},{6,7},{7,6},{8,9},{9,8},{10,11... | collective-permute-start | bytes 4718600 | tf_op jit(solution)/shard_map/ppermute | solution.py:459
  85.6 94.6 %all-to-all-start.2 = ((bf16[16,128,768]{2,1,0:T(8,128)(2,1)}), bf16[16,128,768]{2,1,0:T(8,128)(2,1)}, u32[]{:S(2)}, u32[]{:S(2)}) async-start(bf16[16,128,768]{2,1,0:T(8,128)(2,1)} %bitcast.20), calls=%async_computation.2 | async-start | bytes 6291456 | tf_op jit(solution)/shard_map/all_to_all | solution.py:510
  93.8 53.7 %collective-permute-start.5 = (bf16[1536,768]{1,0:T(8,128)(2,1)S(1)}, bf16[1536,768]{1,0:T(8,128)(2,1)}, u32[]{:S(2)}, u32[]{:S(2)}) collective-permute-start(bf16[1536,768]{1,0:T(8,128)(2,1)S(1)} %bitcast.268), channel_id=1, source_target_pairs={{0,1},{1,0},{2,3},{3,2},{4,5},{5,4},{6,7},{7,6},{8,9},{9,8},{10,11... | collective-permute-start | bytes 7077896 | tf_op jit(solution)/shard_map/ppermute | solution.py:459
  180.2 100.2 %all-to-all-start.3 = ((bf16[16,128,768]{2,1,0:T(8,128)(2,1)}), bf16[16,128,768]{2,1,0:T(8,128)(2,1)}, u32[]{:S(2)}, u32[]{:S(2)}) async-start(bf16[16,128,768]{2,1,0:T(8,128)(2,1)} %bitcast.250), calls=%async_computation.3 | async-start | bytes 6291456 | tf_op jit(solution)/shard_map/all_to_all | solution.py:510
  221.1 54.0 %collective-permute-start.6 = (bf16[384,3072]{1,0:T(8,128)(2,1)}, bf16[384,3072]{1,0:T(8,128)(2,1)}, u32[]{:S(2)}, u32[]{:S(2)}) collective-permute-start(bf16[384,3072]{1,0:T(8,128)(2,1)} %bitcast.270), channel_id=1, source_target_pairs={{0,1},{1,0},{2,3},{3,2},{4,5},{5,4},{6,7},{7,6},{8,9},{9,8},{10,11... | collective-permute-start | bytes 7077896 | tf_op jit(solution)/shard_map/ppermute | solution.py:459
  280.4 81.0 %all-to-all-start.4 = ((bf16[16,128,768]{2,1,0:T(8,128)(2,1)}), bf16[16,128,768]{2,1,0:T(8,128)(2,1)}, u32[]{:S(2)}, u32[]{:S(2)}) async-start(bf16[16,128,768]{2,1,0:T(8,128)(2,1)} %bitcast.42), calls=%async_computation.4 | async-start | bytes 6291456 | tf_op jit(solution)/shard_map/all_to_all | solution.py:510
  361.4 83.8 %all-to-all-start.5 = ((bf16[16,128,768]{2,1,0:T(8,128)(2,1)}), bf16[16,128,768]{2,1,0:T(8,128)(2,1)S(1)}, u32[]{:S(2)}, u32[]{:S(2)}) async-start(bf16[16,128,768]{2,1,0:T(8,128)(2,1)} %bitcast.44), calls=%async_computation.5 | async-start | bytes 6291456 | tf_op jit(solution)/shard_map/all_to_all | solution.py:510
  378.1 146.6 %collective-permute-start.7 = (bf16[1,6144,384]{2,1,0:T(8,128)(2,1)}, bf16[1,6144,384]{2,1,0:T(8,128)(2,1)}, u32[]{:S(2)}, u32[]{:S(2)}) collective-permute-start(bf16[1,6144,384]{2,1,0:T(8,128)(2,1)} %fusion.8), channel_id=1, source_target_pairs={{0,1},{1,0},{2,3},{3,2},{4,5},{5,4},{6,7},{7,6},{8,9},{9,8},{10,11... | collective-permute-start | bytes 14155784 | tf_op jit(solution)/shard_map/ppermute | solution.py:459
  446.9 77.8 %all-to-all-start.6 = ((bf16[16,128,768]{2,1,0:T(8,128)(2,1)}), bf16[16,128,768]{2,1,0:T(8,128)(2,1)S(1)}, u32[]{:S(2)}, u32[]{:S(2)}) async-start(bf16[16,128,768]{2,1,0:T(8,128)(2,1)} %bitcast.46), calls=%async_computation.6 | async-start | bytes 6291456 | tf_op jit(solution)/shard_map/all_to_all | solution.py:510
  526.4 65.5 %all-to-all-start.7 = ((bf16[16,128,768]{2,1,0:T(8,128)(2,1)}), bf16[16,128,768]{2,1,0:T(8,128)(2,1)}, u32[]{:S(2)}, u32[]{:S(2)}) async-start(bf16[16,128,768]{2,1,0:T(8,128)(2,1)} %bitcast.60), calls=%async_computation.7 | async-start | bytes 6291456 | tf_op jit(solution)/shard_map/all_to_all | solution.py:510
  532.4 219.2 %reduce-scatter.5.cloned.1.call-start = ((), (), s32[]{:S(2)}) async-start(), calls=%async_computation.15 | async-start | bytes 5013504 | tf_op jit(solution)/shard_map/reduce_scatter | solution.py:543
  591.9 162.3 %all-to-all-start.8 = ((bf16[16,256,768]{2,1,0:T(8,128)(2,1)}), bf16[16,256,768]{2,1,0:T(8,128)(2,1)}, u32[]{:S(2)}, u32[]{:S(2)}) async-start(bf16[16,256,768]{2,1,0:T(8,128)(2,1)} %pad_maximum_fusion), calls=%async_computation.9 | async-start | bytes 12582912 | tf_op jit(solution)/shard_map/all_to_all | solution.py:510
  607.5 217.2 %reduce-scatter.3.cloned.1.call-start = ((), (), s32[]{:S(2)}) async-start(), calls=%async_computation.14 | async-start | bytes 5013504 | tf_op jit(solution)/shard_map/reduce_scatter | solution.py:543
  607.6 101.8 %collective-permute-start.8 = (bf16[384,3072]{1,0:T(8,128)(2,1)}, bf16[384,3072]{1,0:T(8,128)(2,1)}, u32[]{:S(2)}, u32[]{:S(2)}) collective-permute-start(bf16[384,3072]{1,0:T(8,128)(2,1)} %dynamic-slice_convert_fusion.1), channel_id=1, source_target_pairs={{0,1},{1,0},{2,3},{3,2},{4,5},{5,4},{6,7},{7,6},{8,9},{9,8},{10,11... | collective-permute-start | bytes 7077896 | tf_op jit(solution)/shard_map/ppermute | solution.py:459
  609.0 103.0 %collective-permute-start.9 = (bf16[1536,768]{1,0:T(8,128)(2,1)}, bf16[1536,768]{1,0:T(8,128)(2,1)}, u32[]{:S(2)}, u32[]{:S(2)}) collective-permute-start(bf16[1536,768]{1,0:T(8,128)(2,1)} %dynamic-slice_convert_fusion), channel_id=1, source_target_pairs={{0,1},{1,0},{2,3},{3,2},{4,5},{5,4},{6,7},{7,6},{8,9},{9,8},{10,11... | collective-permute-start | bytes 7077896 | tf_op jit(solution)/shard_map/ppermute | solution.py:459
  738.2 36.9 %collective-permute-start.10 = (bf16[1024,768]{1,0:T(8,128)(2,1)}, bf16[1024,768]{1,0:T(8,128)(2,1)}, u32[]{:S(2)}, u32[]{:S(2)}) collective-permute-start(bf16[1024,768]{1,0:T(8,128)(2,1)} %dynamic-slice_convert_fusion.2), channel_id=1, source_target_pairs={{0,1},{1,0},{2,3},{3,2},{4,5},{5,4},{6,7},{7,6},{8,9},{9,8},{10,11... | collective-permute-start | bytes 4718600 | tf_op jit(solution)/shard_map/ppermute | solution.py:459
  782.3 30.6 %all-to-all-start.9 = ((bf16[16,4,288]{2,1,0:T(4,128)(2,1)}), bf16[16,4,288]{2,1,0:T(4,128)(2,1)S(1)}, u32[]{:S(2)}, u32[]{:S(2)}) async-start(bf16[16,4,288]{2,1,0:T(4,128)(2,1)} %copy.115), calls=%async_computation.10 | async-start | bytes 98304 | tf_op jit(solution)/shard_map/all_to_all | solution.py:510
  (76 other events, 885.1 us)
Sparse Core Ops, SparseCore 0:
  25.4 56.0 all-gather.2
  84.3 136.4 all-gather.4
  592.0 154.2 reduce-scatter.4
  750.5 74.1 reduce-scatter.2
